TPU v7x, 32 devices: a whole 2x2x4 slice. The times are simulated.
32 devices in a mesh: slab: 8 (over z, y), sector: 4 (over x, core).
Axes of the slice: x: 2, y: 2, z: 4, core: 2. Of those that a mesh axis runs over, the one named last changes fastest.
Arguments:
- source: float32 [8, 4, 8, 4096], P('slab', 'sector'), may hold values from -6 to 6
- periods: float32 [8, 8], replicated, may hold values from -4 to 4
- tiles: float32 [8, 4, 64, 4, 4096], P('slab', 'sector'), may hold values from -0.01 to 0.01
- columns: int32 [8, 4, 64, 4], P('slab', 'sector'), may hold values from 0 to 63, as said below
- coupling: float32 [8, 4, 4, 32, 4096], P('slab', 'sector'), may hold values from -0.01 to 0.01
- send_list: int32 [8, 4, 4, 32], P('slab', 'sector'), may hold values from 0 to 63, as said below
- recv_rows: int32 [8, 4, 4, 32], P('slab', 'sector'), may hold values from 0 to 63, as said below
- counts: int32 [8, 4, 4], P('slab', 'sector'), may hold values from 1 to 32, as said below
- cycle_edges: int32 [8, 4, 8, 32], P('slab', 'sector'), may hold values from 0 to 4095, as said below
- cycle_signs: int32 [8, 4, 8, 32], P('slab', 'sector'), may hold values from 0 to 1
- inverse_blocks: float32 [8, 4, 64, 4096], P('slab', 'sector'), as said below
Outputs:
- solution: float32 [8, 4, 8, 4096], P('slab', 'sector')
- residual: float32 [8, 4, 8, 4096], P('slab', 'sector')
Inputs may be any that keep to these rules, and one draw needn't show every extreme that they name: `columns`: block b's 4 column blocks are (b + o_k) mod 64 with 4 distinct offsets o_k of the device. `send_list`: the 32 blocks of one list are distinct. `recv_rows`: the 32 row blocks toward one neighbour are distinct. `counts`: some list is full. `cycle_edges`: the edges of one cycle on one device are distinct. `inverse_blocks`: each block is symmetric with diagonal entries of 0.8 or more and off-diagonal entries of magnitude 0.012 or less.
All inputs are finite; a program needn't handle non-finite values.
Results may differ from a plain program's by a relative error of at most 0.0003.
Values sent between devices are 32-bit elements; how exact they have to be, the bound alone decides.
No kernel may reach another device: no remote copies, remote signals or barrier semaphores. Data moves between devices by JAX's collectives and lax.ppermute only.
A program may use at most 128 MiB of HBM per device.

v0:
```python
import functools

import jax
import jax.numpy as jnp
from jax import lax
from jax.experimental import pallas as pl
from jax.experimental.pallas import tpu as pltpu
from jax.sharding import PartitionSpec as P

TILE = 64
LANES = 128
F32 = jnp.float32
BF16 = jnp.bfloat16
HIGH = lax.Precision.HIGHEST
AXES = ("slab", "sector")


def lane_of(shape):
    return lax.broadcasted_iota(jnp.int32, shape, len(shape) - 1)


def split(x):
    hi = x.astype(BF16)
    lo = x - hi.astype(F32)
    return hi.astype(F32), lo


def turn(x):
    return pltpu.roll(x, 64, x.ndim - 1)


def into_rows():
    row = lax.broadcasted_iota(jnp.int32, (LANES, 2 * LANES), 0)
    col = lax.broadcasted_iota(jnp.int32, (LANES, 2 * LANES), 1)
    parity = col // LANES
    group = (col % LANES) // 32
    m = col % 32
    keep = (row % 64 == 2 * m + parity) & (row // 64 == group % 2)
    return jnp.where(keep, 1.0, 0.0).astype(BF16)


def out_of_rows():
    row = lax.broadcasted_iota(jnp.int32, (LANES, 2 * LANES), 0)
    col = lax.broadcasted_iota(jnp.int32, (LANES, 2 * LANES), 1)
    keep = (col % 64) == 2 * (row % 32) + col // LANES
    return jnp.where(keep, 1.0, 0.0).astype(BF16)


def tile_split(ref, start, stride):
    v = ref[pl.ds(start, 32, stride=stride), :]
    hi = v.astype(BF16)
    lo = (v - hi.astype(F32)).astype(BF16)
    return hi, lo


def dot(a, b):
    return lax.dot_general(a, b, (((1,), (0,)), ((), ())), preferred_element_type=F32)


def dot_nt(a, b):
    return lax.dot_general(a, b, (((1,), (1,)), ((), ())), preferred_element_type=F32)


def fold(out, nf):
    t = jnp.where(lane_of((nf, LANES)) < 64, out[:nf], out[nf:])
    return t + turn(t)


def left_form(x, nf):
    low = lane_of(x.shape) < 64
    hi, lo = split(x)
    zero = jnp.zeros_like(hi)
    return jnp.concatenate(
        [jnp.where(low, hi, zero), jnp.where(low, zero, hi), jnp.where(low, lo, zero), jnp.where(low, zero, lo)],
        axis=0,
    ).astype(BF16)


def write_row_form(load, y_ref, nf, blocks, matrix):
    step = 8

    def body(i, carry):
        parts = [load(i * step + j) for j in range(step)]
        x = jnp.concatenate(parts, axis=0)
        hi, lo = split(x)
        mixed = jnp.where(lane_of(x.shape) < 64, hi, lo).astype(BF16)
        out = dot(mixed, matrix)
        for j in range(step):
            o = out[j * nf : (j + 1) * nf]
            y_ref[i * step + j] = jnp.concatenate([o[:, :LANES], o[:, LANES:]], axis=0).astype(BF16)
        return carry

    lax.fori_loop(0, blocks // step, body, 0)


def pick_two(u):
    hi, lo = split(u)
    return jnp.where(lane_of(u.shape) < 64, hi, lo).astype(BF16)


def mat_t(y, hi, lo, nf):
    w = jnp.concatenate([hi, hi, lo, lo], axis=0)
    return fold(dot(y, w), nf)


def to_natural(ref, row, nat_ref, blocks):
    for t in range(blocks // 2):
        a = ref[2 * t]
        b = ref[2 * t + 1]
        rows = nat_ref.shape[0]
        low = lane_of((rows, LANES)) < 64
        nat_ref[:, t * LANES : (t + 1) * LANES] = jnp.where(low, a[row : row + rows], b[row : row + rows])


def smooth_into(inv_ref, y_ref, out_ref, nf, blocks):
    def body(g, carry):
        for c in range(8):
            hi, lo = tile_split(inv_ref, g * 256 + c, 8)
            out_ref[g * 8 + c] = mat_t(y_ref[g * 8 + c], hi, lo, nf)
        return carry

    lax.fori_loop(0, blocks // 8, body, 0)


def write_messages(load, y_ref, coup_ref, send_ref, recv_ref, counts_ref, msgs, nf, cap):
    low = lane_of((nf, LANES)) < 64
    for d in range(4):
        def body(g, carry, d=d):
            for j in range(8):
                c = g * 8 + j
                hi, lo = tile_split(coup_ref, d * cap * 32 + g * 256 + j, 8)
                partner = mat_t(y_ref[recv_ref[d, c]], hi, lo, nf)
                weight = jnp.where(c < counts_ref[0, 0, d], 1.0, 0.0)
                msgs[d][c] = jnp.where(low, load(send_ref[d, c]) * weight, partner)
            return carry

        lax.fori_loop(0, cap // 8, body, 0)


def first_kernel(nf, blocks, cap, src_ref, per_ref, edges_ref, signs_ref, inv_ref, coup_ref, send_ref, recv_ref, counts_ref,
                 m0, m1, m2, m3, z_ref, zn_ref, r0_ref, cd_ref, y_ref, x_ref, y0_ref):
    fields = src_ref.shape[0]
    width = src_ref.shape[1]
    edges = edges_ref[...]
    orient = (2 * signs_ref[...] - 1).astype(F32)
    place = lax.broadcasted_iota(jnp.int32, (edges.shape[0], LANES), 1)
    low = lane_of((fields, LANES)) < 64

    def cycles(t, carry):
        here = place + t * LANES
        total = jnp.zeros((edges.shape[0], LANES), F32)
        for l in range(edges.shape[1]):
            total = jnp.where(edges[:, l : l + 1] == here, orient[:, l : l + 1], total)
        cd_ref[:, pl.ds(pl.multiple_of(t * LANES, LANES), LANES)] = total
        return carry

    lax.fori_loop(0, width // LANES, cycles, 0)
    r0_ref[...] = src_ref[...] + lax.dot_general(
        per_ref[...], cd_ref[...], (((0,), (0,)), ((), ())), precision=HIGH, preferred_element_type=F32)
    for t in range(width // LANES):
        r = r0_ref[:, t * LANES : (t + 1) * LANES]
        c = cd_ref[:, t * LANES : (t + 1) * LANES]
        rt = turn(r)
        ct = turn(c)
        x_ref[2 * t] = jnp.concatenate([jnp.where(low, r, rt), jnp.where(low, c, ct)], axis=0)
        x_ref[2 * t + 1] = jnp.concatenate([jnp.where(low, rt, r), jnp.where(low, ct, c)], axis=0)
    matrix = into_rows()
    write_row_form(lambda b: x_ref[b], y0_ref, nf, blocks, matrix)
    smooth_into(inv_ref, y0_ref, z_ref, nf, blocks)
    write_row_form(lambda b: z_ref[b], y_ref, nf, blocks, matrix)
    write_messages(lambda b: z_ref[b], y_ref, coup_ref, send_ref, recv_ref, counts_ref, (m0, m1, m2, m3), nf, cap)
    to_natural(z_ref, 0, zn_ref, blocks)


def local_kernel(nf, blocks, kt, cols_ref, tiles_ref, z_ref, y_ref, acc_ref, x_ref, u_ref, t_ref):
    def left(b, carry):
        x_ref[b] = left_form(z_ref[b], nf)
        return carry

    lax.fori_loop(0, blocks, left, 0, unroll=4)

    def body(i, carry):
        for s in range(2):
            b = i * 2 + s
            pieces = [tile_split(tiles_ref, b * (32 * kt) + k, kt) for k in range(kt)]
            y = y_ref[b]
            u = None
            for k in range(kt):
                hi, lo = pieces[k]
                out = dot(y, jnp.concatenate([hi, hi, lo, lo], axis=0))
                t_ref[k, b] = jnp.where(lane_of((nf, LANES)) < 64, out[:nf], out[nf:])
                col = lax.rem(b + cols_ref[0, k], blocks)
                part = dot_nt(x_ref[col], jnp.concatenate([hi, lo, hi, lo], axis=0))
                u = part if u is None else u + part
            u_ref[b] = pick_two(u[: 2 * nf] + u[2 * nf :])
        return carry

    lax.fori_loop(0, blocks // 2, body, 0)
    matrix = out_of_rows()

    def finish(i, carry):
        rows = u_ref[pl.ds(i * 8, 8)].reshape(8 * 2 * nf, LANES)
        out = dot(rows, matrix)
        for j in range(8):
            b = i * 8 + j
            o = out[j * 2 * nf : (j + 1) * 2 * nf]
            t = None
            for k in range(kt):
                v = t_ref[k, lax.rem(b + blocks - cols_ref[0, k], blocks)]
                t = v if t is None else t + v
            acc_ref[b] = z_ref[b] + o[:nf, :LANES] + o[nf:, LANES:] + t + turn(t)
        return carry

    lax.fori_loop(0, blocks // 8, finish, 0)


def absorb(acc_ref, incs, coup_ref, send_ref, recv_ref, counts_ref, nf, cap):
    matrix = out_of_rows()
    low = lane_of((nf, LANES)) < 64
    for d in range(4):
        def body(g, carry, d=d):
            rows = []
            back = []
            for j in range(8):
                c = g * 8 + j
                arr = incs[d][c]
                first = jnp.where(low, arr, 0.0)
                second = arr - first
                hi, lo = split(first)
                x = jnp.concatenate([hi, turn(hi), lo, turn(lo)], axis=0).astype(BF16)
                whi, wlo = tile_split(coup_ref, d * cap * 32 + g * 256 + j, 8)
                u = dot_nt(x, jnp.concatenate([whi, wlo, whi, wlo], axis=0))
                rows.append(pick_two(u[: 2 * nf] + u[2 * nf :]))
                weight = jnp.where(c < counts_ref[0, 0, d], 1.0, 0.0)
                back.append((second + turn(second)) * weight)
            out = dot(jnp.concatenate(rows, axis=0), matrix)
            spots = [recv_ref[d, g * 8 + j] for j in range(8)]
            old = [acc_ref[s] for s in spots]
            for j in range(8):
                o = out[j * 2 * nf : (j + 1) * 2 * nf]
                acc_ref[spots[j]] = old[j] + (o[:nf, :LANES] + o[nf:, LANES:])
            spots = [send_ref[d, g * 8 + j] for j in range(8)]
            old = [acc_ref[s] for s in spots]
            for j in range(8):
                acc_ref[spots[j]] = old[j] + back[j]
            return carry

        lax.fori_loop(0, cap // 8, body, 0)


def second_kernel(nf, blocks, cap, acc_in, i0, i1, i2, i3, inv_ref, coup_ref, send_ref, recv_ref, counts_ref,
                  m0, m1, m2, m3, qn_ref, w_ref, wn_ref, y_ref, acc_ref, y0_ref):
    acc_ref[...] = acc_in[...]
    absorb(acc_ref, (i0, i1, i2, i3), coup_ref, send_ref, recv_ref, counts_ref, 2 * nf, cap)
    to_natural(acc_ref, 0, qn_ref, blocks)
    matrix = into_rows()
    write_row_form(lambda b: acc_ref[b, 0:nf], y0_ref, nf, blocks, matrix)
    smooth_into(inv_ref, y0_ref, w_ref, nf, blocks)
    write_row_form(lambda b: w_ref[b], y_ref, nf, blocks, matrix)
    write_messages(lambda b: w_ref[b], y_ref, coup_ref, send_ref, recv_ref, counts_ref, (m0, m1, m2, m3), nf, cap)
    to_natural(w_ref, 0, wn_ref, blocks)


def column_of(values, lane, at):
    return jnp.sum(jnp.where(lane == at, values, 0.0), axis=1, keepdims=True)


def third_kernel(nf, blocks, cap, acc_in, i0, i1, i2, i3, coup_ref, send_ref, recv_ref, counts_ref,
                 zn_ref, qn_ref, wn_ref, r0_ref, cd_ref, sn_ref, pay_ref, acc_ref, g_ref):
    acc_ref[...] = acc_in[...]
    absorb(acc_ref, (i0, i1, i2, i3), coup_ref, send_ref, recv_ref, counts_ref, nf, cap)
    to_natural(acc_ref, 0, sn_ref, blocks)
    z = zn_ref[0:nf, :]
    q = qn_ref[0:nf, :]
    w = wn_ref[...]
    r = r0_ref[...]
    s = sn_ref[...]

    def inner(a, b):
        return jnp.sum(a * b, axis=1, keepdims=True)

    gamma = inner(r, z)
    base = inner(z, q)
    safe = jnp.where(base > 0.0, base, 1.0)
    centre = jnp.where(base > 0.0, jnp.clip(gamma / safe, 0.0, 4.0), 0.0)
    zc = z - centre * w
    kz = q - centre * s
    values = [
        gamma,
        base,
        centre,
        inner(r - centre * q, zc),
        inner(q, zc),
        inner(q, w),
        inner(zc, kz),
        inner(zc, s),
        inner(w, s),
    ]
    left_hi, left_lo = split(jnp.concatenate([z, w, zn_ref[nf:, :]], axis=0))
    right_hi, right_lo = split(jnp.concatenate([cd_ref[...], qn_ref[nf:, :]], axis=0))
    left = jnp.concatenate([left_hi, left_lo], axis=0).astype(BF16)
    products = dot_nt(left, right_hi.astype(BF16)) + dot_nt(left, right_lo.astype(BF16))
    g_ref[...] = jnp.zeros_like(g_ref)
    g_ref[:, 0:16] = products[:24] + products[24:]
    lane = lane_of((nf, LANES))
    pay = g_ref[0:8, :] + pltpu.roll(g_ref[8:16, :], 32, 1) + pltpu.roll(g_ref[16:24, :], 64, 1)
    for at, value in enumerate(values):
        pay = jnp.where(lane == 16 + at, value, pay)
    pay_ref[...] = pay


def last_kernel(nf, rho, all_ref, zn_ref, wn_ref, qn_ref, r0_ref, cd_ref, sn_ref, x_ref, res_ref):
    lane = lane_of((nf, LANES))
    total = all_ref[0]
    for d in range(1, all_ref.shape[0]):
        total = total + all_ref[d]

    def mat(x):
        return lax.dot_general(x[0], x[1], (((1,), (0,)), ((), ())), precision=HIGH, preferred_element_type=F32)

    t0 = total[:, 0:8]
    z_h = total[:, 8:16]
    cw = total[:, 32:40]
    w_h = total[:, 40:48]
    b = total[:, 64:72]
    d_h = total[:, 72:80]
    gamma0 = column_of(total, lane, 16)
    base = column_of(total, lane, 17) + rho * jnp.sum(t0 * t0, axis=1, keepdims=True)
    alpha0 = gamma0 / base

    def about(d, carry):
        g1, kz = carry
        part = all_ref[d]
        off = alpha0 - column_of(part, lane, 18)
        g1 = g1 + column_of(part, lane, 19) - 2.0 * off * column_of(part, lane, 20) + off * off * column_of(part, lane, 21)
        kz = kz + column_of(part, lane, 22) - 2.0 * off * column_of(part, lane, 23) + off * off * column_of(part, lane, 24)
        return g1, kz

    zero = jnp.zeros((nf, 1), F32)
    gamma1, delta = lax.fori_loop(0, all_ref.shape[0], about, (zero, zero))
    t0b = mat((t0, b))
    t0d = mat((t0, d_h))
    step = alpha0 * rho
    gamma1 = gamma1 - 2.0 * step * jnp.sum(t0 * (t0 - alpha0 * cw), axis=1, keepdims=True)
    gamma1 = gamma1 + step * step * jnp.sum(t0 * t0b, axis=1, keepdims=True)
    delta = delta - 2.0 * step * jnp.sum(t0 * (z_h - alpha0 * w_h), axis=1, keepdims=True)
    delta = delta + step * step * jnp.sum(t0 * t0d, axis=1, keepdims=True)
    tw = cw + rho * t0b
    cz = t0 - alpha0 * tw
    delta = delta + rho * jnp.sum(cz * cz, axis=1, keepdims=True)
    beta = gamma1 / gamma0
    alpha1 = gamma1 / (delta - beta * (gamma1 / alpha0))
    both = alpha0 * alpha1
    lead = alpha0 + alpha1 * (1.0 + beta)
    x_ref[...] = lead * zn_ref[0:nf, :] - both * wn_ref[...] + mat((-(both * rho) * t0, zn_ref[nf:, :]))
    res_ref[...] = (
        r0_ref[...] - lead * qn_ref[0:nf, :] + both * sn_ref[...]
        + mat((rho * (both * tw - lead * t0), cd_ref[...]))
        + mat((both * rho * t0, qn_ref[nf:, :]))
    )


SMEM = pl.BlockSpec(memory_space=pltpu.SMEM)
VMEM = pl.BlockSpec(memory_space=pltpu.VMEM)
PARAMS = pltpu.CompilerParams(vmem_limit_bytes=56 * 1024 * 1024)


def like(*shape, dtype=F32):
    return jax.ShapeDtypeStruct(shape, dtype)


def call(kernel, ins, outs, scratch, name, flops=0):
    return pl.pallas_call(
        kernel, in_specs=ins, out_shape=outs, out_specs=jax.tree.map(lambda _: VMEM, outs), scratch_shapes=scratch,
        compiler_params=PARAMS, name=name,
        cost_estimate=pl.CostEstimate(flops=flops, transcendentals=0, bytes_accessed=8 << 20) if flops else None)


def exchange(msgs):
    slabs = lax.axis_size("slab")
    sectors = lax.axis_size("sector")
    up = [(i, i + 1) for i in range(slabs - 1)]
    down = [(i + 1, i) for i in range(slabs - 1)]
    right = [(i, (i + 1) % sectors) for i in range(sectors)]
    left = [((i + 1) % sectors, i) for i in range(sectors)]
    return (
        lax.ppermute(msgs[1], "slab", up),
        lax.ppermute(msgs[0], "slab", down),
        lax.ppermute(msgs[3], "sector", right),
        lax.ppermute(msgs[2], "sector", left),
    )


def rows_of(x, group):
    n = x.shape[0]
    return x.reshape(n // group, group, 32, LANES).transpose(0, 2, 1, 3).reshape(n * 32, LANES)


def on_device(source, periods, tiles, columns, coupling, send_list, recv_rows, counts, cycle_edges, cycle_signs, inverse_blocks):
    src = source[0, 0]
    nf, width = src.shape
    blocks = width // TILE
    kt = tiles.shape[3]
    cap = coupling.shape[3]
    cycles = periods.shape[0]
    both = nf + cycles
    devices = lax.axis_size("slab") * lax.axis_size("sector")
    rho = 1.0 / (cycle_edges.shape[3] * devices)
    tiles2 = rows_of(tiles[0, 0].reshape(blocks * kt, TILE * TILE), kt)
    coup2 = rows_of(coupling[0, 0].reshape(4 * cap, TILE * TILE), 8)
    inv2 = rows_of(inverse_blocks[0, 0], 8)
    send, recv, cols = send_list[0, 0], recv_rows[0, 0], columns[0, 0]

    msg = like(cap, both, LANES)
    *msgs, z, zn, r0, cd, y = call(
        functools.partial(first_kernel, both, blocks, cap),
        [VMEM] * 6 + [SMEM] * 3,
        [msg] * 4 + [like(blocks, both, LANES), like(both, width), like(nf, width), like(cycles, width),
                     like(blocks, 2 * both, LANES, dtype=BF16)],
        [pltpu.VMEM((blocks, both, LANES), F32), pltpu.VMEM((blocks, 2 * both, LANES), BF16)],
        "first",
    )(src, periods, cycle_edges[0, 0], cycle_signs[0, 0], inv2, coup2, send, recv, counts)

    def local(vector, y, n):
        return call(
            functools.partial(local_kernel, n, blocks, kt),
            [SMEM] + [VMEM] * 3,
            like(blocks, n, LANES),
            [pltpu.VMEM((blocks, 4 * n, LANES), BF16), pltpu.VMEM((blocks, 2 * n, LANES), BF16),
             pltpu.VMEM((kt, blocks, n, LANES), F32)],
            "local", flops=2 * 10**9,
        )(cols, tiles2, vector, y)

    incoming = exchange(msgs)
    acc = local(z, y, both)
    msg = like(cap, nf, LANES)
    *msgs, qn, w, wn, y = call(
        functools.partial(second_kernel, nf, blocks, cap),
        [VMEM] * 7 + [SMEM] * 3,
        [msg] * 4 + [like(both, width), like(blocks, nf, LANES), like(nf, width), like(blocks, 2 * nf, LANES, dtype=BF16)],
        [pltpu.VMEM((blocks, both, LANES), F32), pltpu.VMEM((blocks, 2 * nf, LANES), BF16)],
        "second",
    )(acc, *incoming, inv2, coup2, send, recv, counts)
    incoming = exchange(msgs)
    acc = local(w, y, nf)
    sn, pay = call(
        functools.partial(third_kernel, nf, blocks, cap),
        [VMEM] * 6 + [SMEM] * 3 + [VMEM] * 5,
        [like(nf, width), like(nf, LANES)],
        [pltpu.VMEM((blocks, nf, LANES), F32), pltpu.VMEM((24, LANES), F32)],
        "third",
    )(acc, *incoming, coup2, send, recv, counts, zn, qn, wn, r0, cd)
    everyone = lax.all_to_all(jnp.broadcast_to(pay[None], (devices,) + pay.shape), AXES, 0, 0)
    out, res = call(
        functools.partial(last_kernel, nf, rho),
        [VMEM] * 7,
        [like(nf, width), like(nf, width)],
        [],
        "last",
    )(everyone, zn, wn, qn, r0, cd, sn)
    return out[None, None], res[None, None]


def solution(mesh):
    two = P("slab", "sector")
    return jax.shard_map(
        on_device,
        mesh=mesh,
        in_specs=(two, P(), two, two, two, two, two, two, two, two, two),
        out_specs=(two, two),
        check_vma=False,
    )
```

profile of v0, /device:TPU:0, one launch (start us, length us, event | category | flops | bytes accessed | tf_op | source)
XLA Modules:
  0.0 121.4 jit_solution(18401779354569163144)
XLA Ops:
  0.6 17.9 %first.1 = (f32[32,16,128]{2,1,0:T(8,128)}, f32[32,16,128]{2,1,0:T(8,128)}, f32[32,16,128]{2,1,0:T(8,128)}, f32[32,16,128]{2,1,0:T(8,128)}, f32[64,16,128]{2,1,0...) custom-call(f32[8,4096]{1,0:T(8,128)} %bitcast.28, ...), custom_call_target="tpu_custom_call" | custom-call | tf_op jit(solution)/shard_map/first/pallas_call | solution.py:415
  18.6 4.9 %collective-permute-start = (f32[32,16,128]{2,1,0:T(8,128)}, f32[32,16,128]{2,1,0:T(8,128)S(1)}, u32[]{:S(2)}, u32[]{:S(2)}) collective-permute-start(f32[32,16,128]{2,1,0:T(8,128)} %get-tuple-element.25), channel_id=1, source_target_pairs={{0,4},{4,8},{8,12},{12,16},{16,20},{20,24},{24,28},{1,5},{5,9},{9,... | collective-permute-start | bytes 786440 | tf_op jit(solution)/shard_map/ppermute | solution.py:387
  23.4 1.3 %collective-permute-start.1 = (f32[32,16,128]{2,1,0:T(8,128)}, f32[32,16,128]{2,1,0:T(8,128)S(1)}, u32[]{:S(2)}, u32[]{:S(2)}) collective-permute-start(f32[32,16,128]{2,1,0:T(8,128)} %get-tuple-element.26), channel_id=1, source_target_pairs={{4,0},{8,4},{12,8},{16,12},{20,16},{24,20},{28,24},{5,1},{9,5},{13... | collective-permute-start | bytes 786440 | tf_op jit(solution)/shard_map/ppermute | solution.py:388
  24.8 0.1 collective-permute-start.2
  24.8 1.7 %collective-permute-start.3 = (f32[32,16,128]{2,1,0:T(8,128)}, f32[32,16,128]{2,1,0:T(8,128)S(1)}, u32[]{:S(2)}, u32[]{:S(2)}) collective-permute-start(f32[32,16,128]{2,1,0:T(8,128)} %get-tuple-element.28), channel_id=1, source_target_pairs={{1,0},{2,1},{3,2},{0,3},{5,4},{6,5},{7,6},{4,7},{9,8},{10,9},{11,1... | collective-permute-start | bytes 786440 | tf_op jit(solution)/shard_map/ppermute | solution.py:390
  26.5 1.4 %copy.13 = s32[1,1,64,4]{3,2,1,0:T(8,128)} copy(s32[1,1,64,4]{2,3,1,0:T(4,128)} %param.14) | data formatting | bytes 2048 | tf_op args[3]
  27.9 16.3 %local.2.acc_in = f32[64,16,128]{2,1,0:T(8,128)} custom-call(s32[64,4]{1,0:T(8,128)} %bitcast.29, f32[8192,128]{1,0:T(8,128)} %bitcast.39, f32[64,16,128]{2,1,0:T(8,128)} %get-tuple-element.23.z_ref, bf16[64,32,128]{2,1,0:T(8,128)(2,1)} %get-tuple-element.24.y_ref), custom_call_target="tpu_custom_call" | custom-call | flops 2000000000 | bytes 8388608 | tf_op jit(solution)/shard_map/local/pallas_call | solution.py:425
  44.2 0.0 collective-permute-done.i0
  44.2 0.0 collective-permute-done.2.i2
  44.3 0.7 copy-done
  44.9 0.1 copy-done.1
  45.0 0.1 copy-done.2
  45.1 0.7 copy-done.3
  45.8 19.7 %second.1 = (f32[32,8,128]{2,1,0:T(8,128)}, f32[32,8,128]{2,1,0:T(8,128)}, f32[32,8,128]{2,1,0:T(8,128)}, f32[32,8,128]{2,1,0:T(8,128)}, f32[16,4096]{1,0:T(8,12...) custom-call(f32[64,16,128]{2,1,0:T(8,128)} %local.2.acc_in, f32[32,16,128]{2,1,0:T(8,128)} %copy-done, ...), custom_call_target="tpu_custom_call" | custom-call | tf_op jit(solution)/shard_map/second/pallas_call | solution.py:437
  65.5 4.5 %collective-permute-start.4 = (f32[32,8,128]{2,1,0:T(8,128)}, f32[32,8,128]{2,1,0:T(8,128)S(1)}, u32[]{:S(2)}, u32[]{:S(2)}) collective-permute-start(f32[32,8,128]{2,1,0:T(8,128)} %get-tuple-element.31), channel_id=1, source_target_pairs={{0,4},{4,8},{8,12},{12,16},{16,20},{20,24},{24,28},{1,5},{5,9},{9,... | collective-permute-start | bytes 393224 | tf_op jit(solution)/shard_map/ppermute | solution.py:387
  70.0 1.3 %collective-permute-start.5 = (f32[32,8,128]{2,1,0:T(8,128)}, f32[32,8,128]{2,1,0:T(8,128)S(1)}, u32[]{:S(2)}, u32[]{:S(2)}) collective-permute-start(f32[32,8,128]{2,1,0:T(8,128)} %get-tuple-element.32), channel_id=1, source_target_pairs={{4,0},{8,4},{12,8},{16,12},{20,16},{24,20},{28,24},{5,1},{9,5},{13... | collective-permute-start | bytes 393224 | tf_op jit(solution)/shard_map/ppermute | solution.py:388
  71.3 0.1 collective-permute-start.6
  71.4 1.7 %collective-permute-start.7 = (f32[32,8,128]{2,1,0:T(8,128)}, f32[32,8,128]{2,1,0:T(8,128)S(1)}, u32[]{:S(2)}, u32[]{:S(2)}) collective-permute-start(f32[32,8,128]{2,1,0:T(8,128)} %get-tuple-element.34), channel_id=1, source_target_pairs={{1,0},{2,1},{3,2},{0,3},{5,4},{6,5},{7,6},{4,7},{9,8},{10,9},{11,1... | collective-permute-start | bytes 393224 | tf_op jit(solution)/shard_map/ppermute | solution.py:390
  73.1 15.0 %local.3.acc_in = f32[64,8,128]{2,1,0:T(8,128)} custom-call(s32[64,4]{1,0:T(8,128)} %bitcast.30, f32[8192,128]{1,0:T(8,128)} %bitcast.40, f32[64,8,128]{2,1,0:T(8,128)} %get-tuple-element.29.z_ref, bf16[64,16,128]{2,1,0:T(8,128)(2,1)} %get-tuple-element.30.y_ref), custom_call_target="tpu_custom_call" | custom-call | flops 2000000000 | bytes 8388608 | tf_op jit(solution)/shard_map/local/pallas_call | solution.py:425
  88.1 0.0 collective-permute-done.4.i0
  88.1 0.0 collective-permute-done.5.i1
  88.1 0.0 copy-start.5
  88.1 0.0 collective-permute-done.6.i2
  88.1 0.0 collective-permute-done.7.i3
  88.2 0.6 copy-done.4
  88.8 0.0 copy-done.5
  88.8 0.0 copy-done.6
  88.8 0.0 copy-done.7
  88.9 10.0 %third.1 = (f32[8,4096]{1,0:T(8,128)}, f32[8,128]{1,0:T(8,128)}) custom-call(f32[64,8,128]{2,1,0:T(8,128)} %local.3.acc_in, f32[32,8,128]{2,1,0:T(8,128)} %copy-done.4, f32[32,8,128]{2,1,0:T(8,128)} %copy-done.5, f32[32,8,128]{2,1,0:T(8,128)} %copy-done.6, f32[32,8,128]{2,1,0:T(8,128)} %copy-done.7, f32[4096,128]{1,0:T(8,128)} %bitcast.25, ...), custom_call_target="tpu_custom_call" | custom-call | tf_op jit(solution)/shard_map/third/pallas_call | solution.py:446
  98.9 0.7 broadcast_in_dim.12
  99.5 16.0 %all_to_all.5.all_ref = f32[32,8,128]{2,1,0:T(8,128)} all-to-all(f32[32,8,128]{2,1,0:T(8,128)S(1)} %broadcast_in_dim.12), channel_id=1, replica_groups=mesh['slab'=8,'sector'=4] {'slab','sector'}, dimensions={0} | all-to-all | bytes 262144 | tf_op jit(solution)/shard_map/all_to_all | solution.py:453
  115.5 5.9 %last.1 = (f32[8,4096]{1,0:T(8,128)}, f32[8,4096]{1,0:T(8,128)}) custom-call(f32[32,8,128]{2,1,0:T(8,128)} %all_to_all.5.all_ref, f32[16,4096]{1,0:T(8,128)} %get-tuple-element.35.zn_ref, f32[8,4096]{1,0:T(8,128)} %get-tuple-element.37.wn_ref, f32[16,4096]{1,0:T(8,128)} %get-tuple-element.36.qn_ref, f32[8,4096]{1,0:T(8,128)} %get-tuple-element.38.r0_ref, ...), custom_call_target="tpu_custom_call" | custom-call | tf_op jit(solution)/shard_map/last/pallas_call | solution.py:454
  (9 shorter events, 0.0 us)
Async XLA Ops:
  18.6 25.7 %collective-permute-start = (f32[32,16,128]{2,1,0:T(8,128)}, f32[32,16,128]{2,1,0:T(8,128)S(1)}, u32[]{:S(2)}, u32[]{:S(2)}) collective-permute-start(f32[32,16,128]{2,1,0:T(8,128)} %get-tuple-element.25), channel_id=1, source_target_pairs={{0,4},{4,8},{8,12},{12,16},{16,20},{20,24},{24,28},{1,5},{5,9},{9,... | collective-permute-start | bytes 786440 | tf_op jit(solution)/shard_map/ppermute | solution.py:387
  23.4 20.8 %collective-permute-start.1 = (f32[32,16,128]{2,1,0:T(8,128)}, f32[32,16,128]{2,1,0:T(8,128)S(1)}, u32[]{:S(2)}, u32[]{:S(2)}) collective-permute-start(f32[32,16,128]{2,1,0:T(8,128)} %get-tuple-element.26), channel_id=1, source_target_pairs={{4,0},{8,4},{12,8},{16,12},{20,16},{24,20},{28,24},{5,1},{9,5},{13... | collective-permute-start | bytes 786440 | tf_op jit(solution)/shard_map/ppermute | solution.py:388
  24.8 19.5 %collective-permute-start.2 = (f32[32,16,128]{2,1,0:T(8,128)}, f32[32,16,128]{2,1,0:T(8,128)S(1)}, u32[]{:S(2)}, u32[]{:S(2)}) collective-permute-start(f32[32,16,128]{2,1,0:T(8,128)} %get-tuple-element.27), channel_id=1, source_target_pairs={{0,1},{1,2},{2,3},{3,0},{4,5},{5,6},{6,7},{7,4},{8,9},{9,10},{10,1... | collective-permute-start | bytes 786440 | tf_op jit(solution)/shard_map/ppermute | solution.py:389
  24.8 19.5 %collective-permute-start.3 = (f32[32,16,128]{2,1,0:T(8,128)}, f32[32,16,128]{2,1,0:T(8,128)S(1)}, u32[]{:S(2)}, u32[]{:S(2)}) collective-permute-start(f32[32,16,128]{2,1,0:T(8,128)} %get-tuple-element.28), channel_id=1, source_target_pairs={{1,0},{2,1},{3,2},{0,3},{5,4},{6,5},{7,6},{4,7},{9,8},{10,9},{11,1... | collective-permute-start | bytes 786440 | tf_op jit(solution)/shard_map/ppermute | solution.py:390
  44.2 0.7 copy-start
  44.2 0.8 copy-start.1
  44.3 0.9 copy-start.2
  45.1 0.7 copy-start.3
  65.5 22.6 %collective-permute-start.4 = (f32[32,8,128]{2,1,0:T(8,128)}, f32[32,8,128]{2,1,0:T(8,128)S(1)}, u32[]{:S(2)}, u32[]{:S(2)}) collective-permute-start(f32[32,8,128]{2,1,0:T(8,128)} %get-tuple-element.31), channel_id=1, source_target_pairs={{0,4},{4,8},{8,12},{12,16},{16,20},{20,24},{24,28},{1,5},{5,9},{9,... | collective-permute-start | bytes 393224 | tf_op jit(solution)/shard_map/ppermute | solution.py:387
  70.0 18.1 %collective-permute-start.5 = (f32[32,8,128]{2,1,0:T(8,128)}, f32[32,8,128]{2,1,0:T(8,128)S(1)}, u32[]{:S(2)}, u32[]{:S(2)}) collective-permute-start(f32[32,8,128]{2,1,0:T(8,128)} %get-tuple-element.32), channel_id=1, source_target_pairs={{4,0},{8,4},{12,8},{16,12},{20,16},{24,20},{28,24},{5,1},{9,5},{13... | collective-permute-start | bytes 393224 | tf_op jit(solution)/shard_map/ppermute | solution.py:388
  71.3 16.8 %collective-permute-start.6 = (f32[32,8,128]{2,1,0:T(8,128)}, f32[32,8,128]{2,1,0:T(8,128)S(1)}, u32[]{:S(2)}, u32[]{:S(2)}) collective-permute-start(f32[32,8,128]{2,1,0:T(8,128)} %get-tuple-element.33), channel_id=1, source_target_pairs={{0,1},{1,2},{2,3},{3,0},{4,5},{5,6},{6,7},{7,4},{8,9},{9,10},{10,1... | collective-permute-start | bytes 393224 | tf_op jit(solution)/shard_map/ppermute | solution.py:389
  71.4 16.7 %collective-permute-start.7 = (f32[32,8,128]{2,1,0:T(8,128)}, f32[32,8,128]{2,1,0:T(8,128)S(1)}, u32[]{:S(2)}, u32[]{:S(2)}) collective-permute-start(f32[32,8,128]{2,1,0:T(8,128)} %get-tuple-element.34), channel_id=1, source_target_pairs={{1,0},{2,1},{3,2},{0,3},{5,4},{6,5},{7,6},{4,7},{9,8},{10,9},{11,1... | collective-permute-start | bytes 393224 | tf_op jit(solution)/shard_map/ppermute | solution.py:390
  88.1 0.7 copy-start.4
  88.1 0.7 copy-start.5
  88.1 0.7 copy-start.6
  88.2 0.7 copy-start.7
where the time goes:
time: 122 us; the launch traced here: 121 us
  Pallas kernels  84.7 us (69%)
  blocking collectives  16 us (13%)
  starting transfers between devices  15.6 us (13%)
  local copies, waits for them, and re-layouts  4.31 us (4%)
    pallas_call x2, Pallas kernels, local(): call(functools.partial(local_kernel, n, blocks, kt), [SMEM] + [VMEM] * 3,...  31.3 us
    pallas_call x1, Pallas kernels, on_device(): call(functools.partial(second_kernel, nf, blocks, cap), [VMEM] * 7 + [SME...  19.7 us
    pallas_call x1, Pallas kernels, on_device(): call(functools.partial(first_kernel, both, blocks, cap), [VMEM] * 6 + [SM...  17.9 us
    all_to_all x1, blocking collectives, on_device(): lax.all_to_all(jnp.broadcast_to(pay[None], (devices,) + pay.shape), AXES,...  16 us
    pallas_call x1, Pallas kernels, on_device(): call(functools.partial(third_kernel, nf, blocks, cap), [VMEM] * 6 + [SMEM...  9.98 us
    ppermute x2, starting transfers between devices, exchange(): lax.ppermute(msgs[1], 'slab', up)  9.41 us
    pallas_call x1, Pallas kernels, on_device(): call(functools.partial(last_kernel, nf, rho), [VMEM] * 7, [like(nf, width...  5.86 us
    unnamed x17, local copies, waits for them, and re-layouts  3.63 us
  transfers between devices with their start and end apart: 8, of which 0 were waited for; matrix products, arithmetic and copies ran while one was open for 1% of the time, Pallas kernels for 26%

commit v1 on v0

v1 whole, which is shorter than its diff:
```python
import functools

import jax
import jax.numpy as jnp
from jax import lax
from jax.experimental import pallas as pl
from jax.experimental.pallas import tpu as pltpu
from jax.sharding import PartitionSpec as P

TILE = 64
LANES = 128
F32 = jnp.float32
BF16 = jnp.bfloat16
AXES = ("slab", "sector")
ROWS_STEP = 32
SMOOTH_STEP = 32
SEND_STEP = 32
ABSORB_STEP = 32
LOCAL_STEP = 8


def lane_of(shape):
    return lax.broadcasted_iota(jnp.int32, shape, len(shape) - 1)


def split(x):
    hi = x.astype(BF16)
    lo = x - hi.astype(F32)
    return hi.astype(F32), lo


def turn(x):
    return pltpu.roll(x, 64, x.ndim - 1)


def into_rows():
    row = lax.broadcasted_iota(jnp.int32, (LANES, LANES), 0)
    col = lane_of((LANES, LANES))
    return jnp.where(row == 2 * (col % 32) + (col // 32) % 2, 1.0, 0.0).astype(BF16)


def out_of_rows():
    row = lax.broadcasted_iota(jnp.int32, (LANES, LANES), 0)
    col = lane_of((LANES, LANES))
    return jnp.where(col % 64 == 2 * (row % 32) + (row // 32) % 2, 1.0, 0.0).astype(BF16)


def stacked(x):
    hi, lo = split(x)
    return jnp.concatenate([hi, lo], axis=0).astype(BF16)


def single(ref, start, stride):
    v = ref[pl.ds(start, 32, stride=stride), :]
    t = turn(v)
    low = lane_of(v.shape) < 64
    return stacked(jnp.concatenate([jnp.where(low, v, t), jnp.where(low, t, v)], axis=0))


def pair(ref, start, stride):
    a = ref[pl.ds(start, 32, stride=stride), :]
    b = ref[pl.ds(start + 1, 32, stride=stride), :]
    low = lane_of(a.shape) < 64
    return stacked(jnp.concatenate([jnp.where(low, a, turn(b)), jnp.where(low, turn(a), b)], axis=0))


def dot(a, b):
    return lax.dot_general(a, b, (((1,), (0,)), ((), ())), preferred_element_type=F32)


def dot_nt(a, b):
    return lax.dot_general(a, b, (((1,), (1,)), ((), ())), preferred_element_type=F32)


def halves(out, nf):
    return out[:nf] + out[nf:]


def write_row_form(load, y_ref, nf, blocks, matrix):
    def body(i, carry):
        x = jnp.concatenate([stacked(load(i * ROWS_STEP + j)) for j in range(ROWS_STEP)], axis=0)
        out = dot(x, matrix).astype(BF16)
        for j in range(ROWS_STEP):
            y_ref[i * ROWS_STEP + j] = out[j * 2 * nf : (j + 1) * 2 * nf]
        return carry

    lax.fori_loop(0, blocks // ROWS_STEP, body, 0)


def to_natural(ref, nat_ref, blocks):
    rows = nat_ref.shape[0]
    low = lane_of((rows, LANES)) < 64
    for t in range(blocks // 2):
        a = ref[2 * t]
        b = ref[2 * t + 1]
        nat_ref[:, t * LANES : (t + 1) * LANES] = jnp.where(low, a[:rows], b[:rows])


def smooth_into(inv_ref, y_ref, out_ref, nf, blocks):
    def body(g, carry):
        for c in range(SMOOTH_STEP):
            w = single(inv_ref, g * (32 * SMOOTH_STEP) + (c // 8) * 256 + c % 8, 8)
            out_ref[g * SMOOTH_STEP + c] = halves(dot(y_ref[g * SMOOTH_STEP + c], w), nf)
        return carry

    lax.fori_loop(0, blocks // SMOOTH_STEP, body, 0)


def write_messages(load, y_ref, coup, send_ref, recv_ref, counts_ref, msgs, nf, cap):
    low = lane_of((nf, LANES)) < 64
    for d in range(4):
        coup_ref = coup(d)

        def body(g, carry, d=d, coup_ref=coup_ref):
            for j in range(SEND_STEP):
                c = g * SEND_STEP + j
                w = single(coup_ref, d * cap * 32 + g * (32 * SEND_STEP) + (j // 8) * 256 + j % 8, 8)
                partner = halves(dot(y_ref[recv_ref[d, c]], w), nf)
                weight = jnp.where(c < counts_ref[0, 0, d], 1.0, 0.0)
                msgs[d][c] = jnp.where(low, load(send_ref[d, c]) * weight, partner)
            return carry

        lax.fori_loop(0, cap // SEND_STEP, body, 0)


class Copies:
    def __init__(self, sems, pairs):
        self.copies = [pltpu.make_async_copy(a, b, sems.at[i]) for i, (a, b) in enumerate(pairs)]
        for copy in self.copies:
            copy.start()

    def wait(self, i):
        self.copies[i].wait()


def quarters(hbm, vmem):
    rows = vmem.shape[0] // 4
    return [(hbm.at[pl.ds(d * rows, rows)], vmem.at[pl.ds(d * rows, rows)]) for d in range(4)]


def weighted_rows(coef, rows, at):
    out = None
    for g in range(coef.shape[1]):
        term = coef[:, g : g + 1] * rows[g : g + 1, at]
        out = term if out is None else out + term
    return out


def first_kernel(nf, blocks, cap, src_ref, per_ref, edges_ref, signs_ref, inv_hbm, coup_hbm, send_ref, recv_ref, counts_ref,
                 m0, m1, m2, m3, z_ref, zn_ref, r0_ref, cd_ref, y_ref, x_ref, y0_ref, inv_ref, coup_ref, sems):
    copies = Copies(sems, [(inv_hbm, inv_ref)] + quarters(coup_hbm, coup_ref))
    fields = src_ref.shape[0]
    width = src_ref.shape[1]
    count = edges_ref.shape[0]
    edges = edges_ref[...]
    orient = (2 * signs_ref[...] - 1).astype(F32)
    low = lane_of((fields, LANES)) < 64
    step = 8 * LANES
    place = lane_of((count, step))
    totals = per_ref[...].T

    def cycles(t, carry):
        at = pl.ds(pl.multiple_of(t * step, step), step)
        here = place + t * step
        total = jnp.zeros((count, step), F32)
        for l in range(edges.shape[1]):
            total = jnp.where(edges[:, l : l + 1] == here, orient[:, l : l + 1], total)
        cd_ref[:, at] = total
        r0_ref[:, at] = src_ref[:, at] + weighted_rows(totals, cd_ref, at)
        return carry

    lax.fori_loop(0, width // step, cycles, 0)
    for t in range(width // LANES):
        r = r0_ref[:, t * LANES : (t + 1) * LANES]
        c = cd_ref[:, t * LANES : (t + 1) * LANES]
        rt = turn(r)
        ct = turn(c)
        x_ref[2 * t] = jnp.concatenate([jnp.where(low, r, rt), jnp.where(low, c, ct)], axis=0)
        x_ref[2 * t + 1] = jnp.concatenate([jnp.where(low, rt, r), jnp.where(low, ct, c)], axis=0)
    matrix = into_rows()
    write_row_form(lambda b: x_ref[b], y0_ref, nf, blocks, matrix)
    copies.wait(0)
    smooth_into(inv_ref, y0_ref, z_ref, nf, blocks)
    write_row_form(lambda b: z_ref[b], y_ref, nf, blocks, matrix)

    def coup(d):
        copies.wait(1 + d)
        return coup_ref

    write_messages(lambda b: z_ref[b], y_ref, coup, send_ref, recv_ref, counts_ref, (m0, m1, m2, m3), nf, cap)
    to_natural(z_ref, zn_ref, blocks)


def local_kernel(nf, blocks, kt, cols_ref, tiles_hbm, z_ref, y_ref, acc_ref, x_ref, u_ref, t_ref, tiles_ref, sems):
    rows = LOCAL_STEP * kt * 32

    def copy(i):
        at = pl.ds(pl.multiple_of(i * rows, rows), rows)
        return pltpu.make_async_copy(tiles_hbm.at[at], tiles_ref.at[at], sems.at[i])

    for i in range(blocks // LOCAL_STEP):
        copy(i).start()

    def left(b, carry):
        x_ref[b] = stacked(z_ref[b])
        return carry

    lax.fori_loop(0, blocks, left, 0, unroll=8)
    wide = lane_of((2 * nf, LANES)) < 64

    def body(i, carry):
        copy(i).wait()
        for s in range(LOCAL_STEP):
            b = i * LOCAL_STEP + s
            w = jnp.concatenate([pair(tiles_ref, b * (32 * kt) + k, kt) for k in range(0, kt, 2)], axis=1)
            t_ref[b] = halves(dot(y_ref[b], w), nf)
            x = [x_ref[lax.rem(b + cols_ref[k, 0], blocks)] for k in range(kt)]
            x = jnp.concatenate([jnp.where(wide, x[k], x[k + 1]) for k in range(0, kt, 2)], axis=1)
            u_ref[b] = stacked(halves(dot_nt(x, w), nf))
        return carry

    lax.fori_loop(0, blocks // LOCAL_STEP, body, 0)
    matrix = out_of_rows()
    low = lane_of((nf, LANES)) < 64

    def finish(i, carry):
        out = dot(u_ref[pl.ds(i * 8, 8)].reshape(8 * 2 * nf, LANES), matrix)
        for j in range(8):
            b = i * 8 + j
            t = None
            for k in range(0, kt, 2):
                at = slice(k // 2 * LANES, (k // 2 + 1) * LANES)
                v = jnp.where(low, t_ref[lax.rem(b + blocks - cols_ref[k, 0], blocks), :, at],
                              t_ref[lax.rem(b + blocks - cols_ref[k + 1, 0], blocks), :, at])
                t = v if t is None else t + v
            acc_ref[b] = z_ref[b] + halves(out[j * 2 * nf : (j + 1) * 2 * nf], nf) + t + turn(t)
        return carry

    lax.fori_loop(0, blocks // 8, finish, 0)


def absorb(acc_ref, incs, coup, send_ref, recv_ref, counts_ref, nf, cap):
    matrix = out_of_rows()
    low = lane_of((nf, LANES)) < 64
    for d in range(4):
        coup_ref = coup(d)

        def body(g, carry, d=d, coup_ref=coup_ref):
            rows = []
            back = []
            for j in range(ABSORB_STEP):
                c = g * ABSORB_STEP + j
                arr = incs[d][c]
                hi, lo = split(arr)
                x = jnp.where(low, hi, turn(lo)).astype(BF16)
                w = single(coup_ref, d * cap * 32 + g * (32 * ABSORB_STEP) + (j // 8) * 256 + j % 8, 8)
                rows.append(stacked(dot_nt(x, w)))
                weight = jnp.where(c < counts_ref[0, 0, d], 1.0, 0.0)
                back.append(jnp.where(low, turn(arr), arr) * weight)
            out = dot(jnp.concatenate(rows, axis=0), matrix)
            spots = [recv_ref[d, g * ABSORB_STEP + j] for j in range(ABSORB_STEP)]
            old = [acc_ref[s] for s in spots]
            for j in range(ABSORB_STEP):
                acc_ref[spots[j]] = old[j] + halves(out[j * 2 * nf : (j + 1) * 2 * nf], nf)
            spots = [send_ref[d, g * ABSORB_STEP + j] for j in range(ABSORB_STEP)]
            old = [acc_ref[s] for s in spots]
            for j in range(ABSORB_STEP):
                acc_ref[spots[j]] = old[j] + back[j]
            return carry

        lax.fori_loop(0, cap // ABSORB_STEP, body, 0)


def gathered(copies, coup_ref):
    def coup(d):
        copies.wait(2 * d)
        copies.wait(2 * d + 1)
        return coup_ref

    return coup


def arrivals(incs, inc_ref, coup_hbm, coup_ref):
    pairs = []
    for d, part in enumerate(quarters(coup_hbm, coup_ref)):
        pairs += [(incs[d], inc_ref.at[d]), part]
    return pairs


def second_kernel(nf, blocks, cap, acc_in, i0, i1, i2, i3, inv_hbm, coup_hbm, send_ref, recv_ref, counts_ref,
                  m0, m1, m2, m3, qn_ref, w_ref, wn_ref, y_ref, acc_ref, y0_ref, inv_ref, coup_ref, inc_ref, sems):
    copies = Copies(sems, arrivals((i0, i1, i2, i3), inc_ref, coup_hbm, coup_ref) + [(inv_hbm, inv_ref)])
    acc_ref[...] = acc_in[...]
    incs = [inc_ref.at[d] for d in range(4)]
    absorb(acc_ref, incs, gathered(copies, coup_ref), send_ref, recv_ref, counts_ref, 2 * nf, cap)
    to_natural(acc_ref, qn_ref, blocks)
    matrix = into_rows()
    write_row_form(lambda b: acc_ref[b, 0:nf], y0_ref, nf, blocks, matrix)
    copies.wait(8)
    smooth_into(inv_ref, y0_ref, w_ref, nf, blocks)
    write_row_form(lambda b: w_ref[b], y_ref, nf, blocks, matrix)
    write_messages(lambda b: w_ref[b], y_ref, lambda d: coup_ref, send_ref, recv_ref, counts_ref, (m0, m1, m2, m3), nf, cap)
    to_natural(w_ref, wn_ref, blocks)


def column_of(values, lane, at):
    return jnp.sum(jnp.where(lane == at, values, 0.0), axis=1, keepdims=True)


def third_kernel(nf, blocks, cap, acc_in, i0, i1, i2, i3, coup_hbm, send_ref, recv_ref, counts_ref,
                 zn_ref, qn_ref, wn_ref, r0_ref, cd_ref, sn_ref, pay_ref, acc_ref, g_ref, coup_ref, inc_ref, sems):
    copies = Copies(sems, arrivals((i0, i1, i2, i3), inc_ref, coup_hbm, coup_ref))
    acc_ref[...] = acc_in[...]
    incs = [inc_ref.at[d] for d in range(4)]
    absorb(acc_ref, incs, gathered(copies, coup_ref), send_ref, recv_ref, counts_ref, nf, cap)
    to_natural(acc_ref, sn_ref, blocks)
    z = zn_ref[0:nf, :]
    q = qn_ref[0:nf, :]
    w = wn_ref[...]
    r = r0_ref[...]
    s = sn_ref[...]

    def inner(a, b):
        return jnp.sum(a * b, axis=1, keepdims=True)

    gamma = inner(r, z)
    base = inner(z, q)
    safe = jnp.where(base > 0.0, base, 1.0)
    centre = jnp.where(base > 0.0, jnp.clip(gamma / safe, 0.0, 4.0), 0.0)
    zc = z - centre * w
    kz = q - centre * s
    values = {
        16: gamma,
        17: base,
        24: inner(r - centre * q, zc),
        25: inner(q, zc),
        26: inner(q, w),
        27: inner(zc, kz),
        28: inner(zc, s),
        29: inner(w, s),
    }
    left_hi, left_lo = split(jnp.concatenate([z, w, zn_ref[nf:, :]], axis=0))
    right_hi, right_lo = split(jnp.concatenate([cd_ref[...], qn_ref[nf:, :]], axis=0))
    left = jnp.concatenate([left_hi, left_lo], axis=0).astype(BF16)
    products = dot_nt(left, right_hi.astype(BF16)) + dot_nt(left, right_lo.astype(BF16))
    g_ref[...] = jnp.zeros_like(g_ref)
    g_ref[:, 0:16] = products[:24] + products[24:]
    lane = lane_of((nf, LANES))
    pay = g_ref[0:8, :] + pltpu.roll(g_ref[8:16, :], 32, 1) + pltpu.roll(g_ref[16:24, :], 64, 1)
    for at, value in values.items():
        pay = jnp.where(lane == at, value, pay)
    pay = jnp.where((lane >= 56) & (lane < 62), centre, pay)
    pay_ref[...] = jnp.broadcast_to(pay[None], pay_ref.shape)


def last_kernel(nf, rho, all_ref, zn_ref, wn_ref, qn_ref, r0_ref, cd_ref, sn_ref, x_ref, res_ref):
    lane = lane_of((nf, LANES))
    total = lax.fori_loop(0, all_ref.shape[0], lambda d, t: t + all_ref[d], jnp.zeros((nf, LANES), F32), unroll=16)

    def mat(a, b):
        out = None
        for g in range(a.shape[1]):
            term = a[:, g : g + 1] * b[g : g + 1, :]
            out = term if out is None else out + term
        return out

    t0 = total[:, 0:8]
    z_h = total[:, 8:16]
    cw = total[:, 32:40]
    w_h = total[:, 40:48]
    b = total[:, 64:72]
    d_h = total[:, 72:80]
    gamma0 = column_of(total, lane, 16)
    base = column_of(total, lane, 17) + rho * jnp.sum(t0 * t0, axis=1, keepdims=True)
    alpha0 = gamma0 / base
    wide = jnp.broadcast_to(alpha0, (nf, LANES))
    constant = (lane == 24) | (lane == 27)
    linear = (lane == 25) | (lane == 28)

    def about(d, carry):
        part = all_ref[d]
        off = wide - pltpu.roll(part, LANES - 32, 1)
        return carry + part * jnp.where(constant, 1.0, jnp.where(linear, -2.0 * off, off * off))

    sums = lax.fori_loop(0, all_ref.shape[0], about, jnp.zeros((nf, LANES), F32), unroll=16)
    gamma1 = jnp.sum(jnp.where((lane >= 24) & (lane < 27), sums, 0.0), axis=1, keepdims=True)
    delta = jnp.sum(jnp.where((lane >= 27) & (lane < 30), sums, 0.0), axis=1, keepdims=True)
    t0b = mat(t0, b)
    t0d = mat(t0, d_h)
    tw = cw + rho * t0b
    cz = t0 - alpha0 * tw
    step = alpha0 * rho
    gamma1 = gamma1 + step * jnp.sum(t0 * (step * t0b - 2.0 * (t0 - alpha0 * cw)), axis=1, keepdims=True)
    delta = delta + jnp.sum(step * t0 * (step * t0d - 2.0 * (z_h - alpha0 * w_h)) + rho * cz * cz, axis=1, keepdims=True)
    beta = gamma1 / gamma0
    alpha1 = gamma1 / (delta - beta * (gamma1 / alpha0))
    both = alpha0 * alpha1
    lead = alpha0 + alpha1 * (1.0 + beta)
    on_d = -(both * rho) * t0
    on_c = rho * (both * tw - lead * t0)
    chunk = 8 * LANES

    def body(i, carry):
        at = pl.ds(pl.multiple_of(i * chunk, chunk), chunk)
        x_ref[:, at] = lead * zn_ref[0:nf, at] - both * wn_ref[:, at] + weighted_rows(on_d, zn_ref.at[nf:], at)
        res_ref[:, at] = (
            r0_ref[:, at] - lead * qn_ref[0:nf, at] + both * sn_ref[:, at]
            + (weighted_rows(on_c, cd_ref, at) - weighted_rows(on_d, qn_ref.at[nf:], at))
        )
        return carry

    lax.fori_loop(0, x_ref.shape[1] // chunk, body, 0)


SMEM = pl.BlockSpec(memory_space=pltpu.SMEM)
VMEM = pl.BlockSpec(memory_space=pltpu.VMEM)
ANY = pl.BlockSpec(memory_space=pl.ANY)
PARAMS = pltpu.CompilerParams(vmem_limit_bytes=56 * 1024 * 1024)


def like(*shape, dtype=F32):
    return jax.ShapeDtypeStruct(shape, dtype)


def call(kernel, ins, outs, scratch, name, flops=0):
    return pl.pallas_call(
        kernel, in_specs=ins, out_shape=outs, out_specs=jax.tree.map(lambda _: VMEM, outs), scratch_shapes=scratch,
        compiler_params=PARAMS, name=name,
        cost_estimate=pl.CostEstimate(flops=flops, transcendentals=0, bytes_accessed=8 << 20) if flops else None)


def exchange(msgs):
    slabs = lax.axis_size("slab")
    sectors = lax.axis_size("sector")
    up = [(i, i + 1) for i in range(slabs - 1)]
    down = [(i + 1, i) for i in range(slabs - 1)]
    right = [(i, (i + 1) % sectors) for i in range(sectors)]
    left = [((i + 1) % sectors, i) for i in range(sectors)]
    return (
        lax.ppermute(msgs[1], "slab", up),
        lax.ppermute(msgs[0], "slab", down),
        lax.ppermute(msgs[3], "sector", right),
        lax.ppermute(msgs[2], "sector", left),
    )


def rows_of(x, group):
    n = x.shape[0]
    return x.reshape(n // group, group, 32, LANES).transpose(0, 2, 1, 3).reshape(n * 32, LANES)


def on_device(source, periods, tiles, columns, coupling, send_list, recv_rows, counts, cycle_edges, cycle_signs, inverse_blocks):
    src = source[0, 0]
    nf, width = src.shape
    blocks = width // TILE
    kt = tiles.shape[3]
    cap = coupling.shape[3]
    cycles = periods.shape[0]
    both = nf + cycles
    devices = lax.axis_size("slab") * lax.axis_size("sector")
    rho = 1.0 / (cycle_edges.shape[3] * devices)
    tiles2 = rows_of(tiles[0, 0].reshape(blocks * kt, TILE * TILE), kt)
    coup2 = rows_of(coupling[0, 0].reshape(4 * cap, TILE * TILE), 8)
    inv2 = rows_of(inverse_blocks[0, 0], 8)
    send, recv, cols = send_list[0, 0], recv_rows[0, 0], columns[0, 0].T
    coup_buf = pltpu.VMEM(coup2.shape, F32)
    inv_buf = pltpu.VMEM(inv2.shape, F32)

    msg = like(cap, both, LANES)
    *msgs, z, zn, r0, cd, y = call(
        functools.partial(first_kernel, both, blocks, cap),
        [VMEM] * 4 + [ANY] * 2 + [SMEM] * 3,
        [msg] * 4 + [like(blocks, both, LANES), like(both, width), like(nf, width), like(cycles, width),
                     like(blocks, 2 * both, LANES, dtype=BF16)],
        [pltpu.VMEM((blocks, both, LANES), F32), pltpu.VMEM((blocks, 2 * both, LANES), BF16), inv_buf, coup_buf,
         pltpu.SemaphoreType.DMA((5,))],
        "first",
    )(src, periods, cycle_edges[0, 0], cycle_signs[0, 0], inv2, coup2, send, recv, counts)

    def local(vector, y, n):
        return call(
            functools.partial(local_kernel, n, blocks, kt),
            [SMEM, ANY, VMEM, VMEM],
            like(blocks, n, LANES),
            [pltpu.VMEM((blocks, 2 * n, LANES), BF16), pltpu.VMEM((blocks, 2 * n, LANES), BF16),
             pltpu.VMEM((blocks, n, kt // 2 * LANES), F32), pltpu.VMEM(tiles2.shape, F32),
             pltpu.SemaphoreType.DMA((blocks // LOCAL_STEP,))],
            "local", flops=2 * 10**9,
        )(cols, tiles2, vector, y)

    incoming = exchange(msgs)
    acc = local(z, y, both)
    msg = like(cap, nf, LANES)
    *msgs, qn, w, wn, y = call(
        functools.partial(second_kernel, nf, blocks, cap),
        [VMEM] + [ANY] * 6 + [SMEM] * 3,
        [msg] * 4 + [like(both, width), like(blocks, nf, LANES), like(nf, width), like(blocks, 2 * nf, LANES, dtype=BF16)],
        [pltpu.VMEM((blocks, both, LANES), F32), pltpu.VMEM((blocks, 2 * nf, LANES), BF16), inv_buf, coup_buf,
         pltpu.VMEM((4, cap, both, LANES), F32), pltpu.SemaphoreType.DMA((9,))],
        "second",
    )(acc, *incoming, inv2, coup2, send, recv, counts)
    incoming = exchange(msgs)
    acc = local(w, y, nf)
    sn, pay = call(
        functools.partial(third_kernel, nf, blocks, cap),
        [VMEM] + [ANY] * 5 + [SMEM] * 3 + [VMEM] * 5,
        [like(nf, width), like(devices, nf, LANES)],
        [pltpu.VMEM((blocks, nf, LANES), F32), pltpu.VMEM((24, LANES), F32), coup_buf,
         pltpu.VMEM((4, cap, nf, LANES), F32), pltpu.SemaphoreType.DMA((8,))],
        "third",
    )(acc, *incoming, coup2, send, recv, counts, zn, qn, wn, r0, cd)
    everyone = lax.all_to_all(pay, AXES, 0, 0)
    out, res = call(
        functools.partial(last_kernel, nf, rho),
        [VMEM] * 7,
        [like(nf, width), like(nf, width)],
        [],
        "last",
    )(everyone, zn, wn, qn, r0, cd, sn)
    return out[None, None], res[None, None]


def solution(mesh):
    two = P("slab", "sector")
    return jax.shard_map(
        on_device,
        mesh=mesh,
        in_specs=(two, P(), two, two, two, two, two, two, two, two, two),
        out_specs=(two, two),
        check_vma=False,
    )
```

time: 122 us -> 78.4 us (0.64)
  Pallas kernels: 84.7 us -> 43.1 us
  local copies, waits for them, and re-layouts: 4.31 us -> 2.28 us
    pallas_call x5, Pallas kernels: 78.9 us -> 39.9 us  [the longest x2 15.7 us: local(): call(functools.partial(local_kernel, n, blocks, kt), [SMEM, ANY, VMEM, VM...]
    pallas_call x1, Pallas kernels: 5.86 us -> 3.16 us  [on_device(): call(functools.partial(last_kernel, nf, rho), [VMEM] * 7, [like(nf, width...]
    unnamed x17 -> x16, local copies, waits for them, and re-layouts: 3.63 us -> 2.28 us
  transfers between devices with their start and end apart: 8 -> 8, of which waited for: 0 -> 1; matrix products, arithmetic and copies ran while one was open for 1% -> 0% of each run, Pallas kernels for 26% -> 20%
where the time goes in v1:
time: 78.4 us; the launch traced here: 78 us
  Pallas kernels  43.1 us (55%)
  blocking collectives  16.1 us (21%)
  starting transfers between devices  15.5 us (20%)
  local copies, waits for them, and re-layouts  2.28 us (3%)
  between operations  0.81 us (1%)
    all_to_all x1, blocking collectives, on_device(): everyone = lax.all_to_all(pay, AXES, 0, 0)  16.1 us
    pallas_call x2, Pallas kernels, local(): call(functools.partial(local_kernel, n, blocks, kt), [SMEM, ANY, VMEM, VM...  15.7 us
    pallas_call x1, Pallas kernels, on_device(): call(functools.partial(second_kernel, nf, blocks, cap), [VMEM] + [ANY] *...  9.98 us
    ppermute x2, starting transfers between devices, exchange(): lax.ppermute(msgs[1], 'slab', up)  9.32 us
    pallas_call x1, Pallas kernels, on_device(): call(functools.partial(third_kernel, nf, blocks, cap), [VMEM] + [ANY] * 5...  7.18 us
    pallas_call x1, Pallas kernels, on_device(): call(functools.partial(first_kernel, both, blocks, cap), [VMEM] * 4 + [AN...  7.12 us
    ppermute x2, starting transfers between devices, exchange(): lax.ppermute(msgs[2], 'sector', left)  3.47 us
    pallas_call x1, Pallas kernels, on_device(): call(functools.partial(last_kernel, nf, rho), [VMEM] * 7, [like(nf, width...  3.16 us
  transfers between devices with their start and end apart: 8, of which 1 were waited for; matrix products, arithmetic and copies ran while one was open for 0% of the time, Pallas kernels for 20%

profile of v1, /device:TPU:0, one launch (start us, length us, event | category | flops | bytes accessed | tf_op | source)
XLA Modules:
  0.0 78.0 jit_solution(16255947732352349254)
XLA Ops:
  0.6 7.1 %first.1 = (f32[32,16,128]{2,1,0:T(8,128)}, f32[32,16,128]{2,1,0:T(8,128)}, f32[32,16,128]{2,1,0:T(8,128)}, f32[32,16,128]{2,1,0:T(8,128)}, f32[64,16,128]{2,1,0...) custom-call(f32[8,4096]{1,0:T(8,128)} %bitcast.30, ...), custom_call_target="tpu_custom_call" | custom-call | tf_op jit(solution)/shard_map/first/pallas_call | solution.py:470
  7.8 4.9 %collective-permute-start = (f32[32,16,128]{2,1,0:T(8,128)}, f32[32,16,128]{2,1,0:T(8,128)S(1)}, u32[]{:S(2)}, u32[]{:S(2)}) collective-permute-start(f32[32,16,128]{2,1,0:T(8,128)} %get-tuple-element.25), channel_id=1, source_target_pairs={{0,4},{4,8},{8,12},{12,16},{16,20},{20,24},{24,28},{1,5},{5,9},{9,... | collective-permute-start | bytes 786440 | tf_op jit(solution)/shard_map/ppermute | solution.py:440
  12.7 1.3 %collective-permute-start.1 = (f32[32,16,128]{2,1,0:T(8,128)}, f32[32,16,128]{2,1,0:T(8,128)S(1)}, u32[]{:S(2)}, u32[]{:S(2)}) collective-permute-start(f32[32,16,128]{2,1,0:T(8,128)} %get-tuple-element.26), channel_id=1, source_target_pairs={{4,0},{8,4},{12,8},{16,12},{20,16},{24,20},{28,24},{5,1},{9,5},{13... | collective-permute-start | bytes 786440 | tf_op jit(solution)/shard_map/ppermute | solution.py:441
  14.0 0.1 collective-permute-start.2
  14.0 1.7 %collective-permute-start.3 = (f32[32,16,128]{2,1,0:T(8,128)}, f32[32,16,128]{2,1,0:T(8,128)S(1)}, u32[]{:S(2)}, u32[]{:S(2)}) collective-permute-start(f32[32,16,128]{2,1,0:T(8,128)} %get-tuple-element.28), channel_id=1, source_target_pairs={{1,0},{2,1},{3,2},{0,3},{5,4},{6,5},{7,6},{4,7},{9,8},{10,9},{11,1... | collective-permute-start | bytes 786440 | tf_op jit(solution)/shard_map/ppermute | solution.py:443
  15.8 8.2 %local.2.acc_in = f32[64,16,128]{2,1,0:T(8,128)} custom-call(s32[4,64]{1,0:T(4,128)} %bitcast.43, f32[8192,128]{1,0:T(8,128)} %bitcast.39, f32[64,16,128]{2,1,0:T(8,128)} %get-tuple-element.23.z_ref, bf16[64,32,128]{2,1,0:T(8,128)(2,1)} %get-tuple-element.24.y_ref), custom_call_target="tpu_custom_call" | custom-call | flops 2000000000 | bytes 8388608 | tf_op jit(solution)/shard_map/local/pallas_call | solution.py:481
  23.9 0.2 collective-permute-done.i0
  24.1 0.0 collective-permute-done.1.i1
  24.1 0.0 collective-permute-done.2.i2
  24.1 0.0 collective-permute-done.3.i3
  24.1 0.7 copy-done
  24.8 0.1 copy-done.1
  24.9 0.1 copy-done.2
  25.0 0.7 copy-done.3
  25.7 10.0 %second.1 = (f32[32,8,128]{2,1,0:T(8,128)}, f32[32,8,128]{2,1,0:T(8,128)}, f32[32,8,128]{2,1,0:T(8,128)}, f32[32,8,128]{2,1,0:T(8,128)}, f32[16,4096]{1,0:T(8,12...) custom-call(f32[64,16,128]{2,1,0:T(8,128)} %local.2.acc_in, f32[32,16,128]{2,1,0:T(8,128)} %copy-done, ...), custom_call_target="tpu_custom_call" | custom-call | tf_op jit(solution)/shard_map/second/pallas_call | solution.py:494
  35.7 4.4 %collective-permute-start.4 = (f32[32,8,128]{2,1,0:T(8,128)}, f32[32,8,128]{2,1,0:T(8,128)S(1)}, u32[]{:S(2)}, u32[]{:S(2)}) collective-permute-start(f32[32,8,128]{2,1,0:T(8,128)} %get-tuple-element.31), channel_id=1, source_target_pairs={{0,4},{4,8},{8,12},{12,16},{16,20},{20,24},{24,28},{1,5},{5,9},{9,... | collective-permute-start | bytes 393224 | tf_op jit(solution)/shard_map/ppermute | solution.py:440
  40.1 1.3 %collective-permute-start.5 = (f32[32,8,128]{2,1,0:T(8,128)}, f32[32,8,128]{2,1,0:T(8,128)S(1)}, u32[]{:S(2)}, u32[]{:S(2)}) collective-permute-start(f32[32,8,128]{2,1,0:T(8,128)} %get-tuple-element.32), channel_id=1, source_target_pairs={{4,0},{8,4},{12,8},{16,12},{20,16},{24,20},{28,24},{5,1},{9,5},{13... | collective-permute-start | bytes 393224 | tf_op jit(solution)/shard_map/ppermute | solution.py:441
  41.4 0.1 collective-permute-start.6
  41.5 1.7 %collective-permute-start.7 = (f32[32,8,128]{2,1,0:T(8,128)}, f32[32,8,128]{2,1,0:T(8,128)S(1)}, u32[]{:S(2)}, u32[]{:S(2)}) collective-permute-start(f32[32,8,128]{2,1,0:T(8,128)} %get-tuple-element.34), channel_id=1, source_target_pairs={{1,0},{2,1},{3,2},{0,3},{5,4},{6,5},{7,6},{4,7},{9,8},{10,9},{11,1... | collective-permute-start | bytes 393224 | tf_op jit(solution)/shard_map/ppermute | solution.py:443
  43.2 7.5 %local.3.acc_in = f32[64,8,128]{2,1,0:T(8,128)} custom-call(s32[4,64]{1,0:T(4,128)} %bitcast.44, f32[8192,128]{1,0:T(8,128)} %bitcast.40, f32[64,8,128]{2,1,0:T(8,128)} %get-tuple-element.29.z_ref, bf16[64,16,128]{2,1,0:T(8,128)(2,1)} %get-tuple-element.30.y_ref), custom_call_target="tpu_custom_call" | custom-call | flops 2000000000 | bytes 8388608 | tf_op jit(solution)/shard_map/local/pallas_call | solution.py:481
  50.7 0.0 collective-permute-done.4.i0
  50.7 0.0 copy-start.4
  50.7 0.0 collective-permute-done.5.i1
  50.8 0.0 copy-start.5
  50.8 0.0 collective-permute-done.6.i2
  50.8 0.6 copy-done.4
  51.4 0.0 copy-done.5
  51.4 0.0 copy-done.6
  51.5 0.0 copy-done.7
  51.5 7.2 %third.1 = (f32[8,4096]{1,0:T(8,128)}, f32[32,8,128]{2,1,0:T(8,128)}) custom-call(f32[64,8,128]{2,1,0:T(8,128)} %local.3.acc_in, f32[32,8,128]{2,1,0:T(8,128)} %copy-done.4, f32[32,8,128]{2,1,0:T(8,128)} %copy-done.5, f32[32,8,128]{2,1,0:T(8,128)} %copy-done.6, f32[32,8,128]{2,1,0:T(8,128)} %copy-done.7, f32[4096,128]{1,0:T(8,128)} %bitcast.27, ...), custom_call_target="tpu_custom_call" | custom-call | tf_op jit(solution)/shard_map/third/pallas_call | solution.py:504
  58.7 16.1 %all_to_all.5.all_ref = f32[32,8,128]{2,1,0:T(8,128)} all-to-all(f32[32,8,128]{2,1,0:T(8,128)} %get-tuple-element.40), channel_id=1, replica_groups=mesh['slab'=8,'sector'=4] {'slab','sector'}, dimensions={0} | all-to-all | bytes 262144 | tf_op jit(solution)/shard_map/all_to_all | solution.py:512
  74.8 3.2 %last.1 = (f32[8,4096]{1,0:T(8,128)}, f32[8,4096]{1,0:T(8,128)}) custom-call(f32[32,8,128]{2,1,0:T(8,128)} %all_to_all.5.all_ref, f32[16,4096]{1,0:T(8,128)} %get-tuple-element.35.zn_ref, f32[8,4096]{1,0:T(8,128)} %get-tuple-element.37.wn_ref, f32[16,4096]{1,0:T(8,128)} %get-tuple-element.36.qn_ref, f32[8,4096]{1,0:T(8,128)} %get-tuple-element.38.r0_ref, ...), custom_call_target="tpu_custom_call" | custom-call | tf_op jit(solution)/shard_map/last/pallas_call | solution.py:513
  (7 shorter events, 0.0 us)
Async XLA Ops:
  7.8 16.3 %collective-permute-start = (f32[32,16,128]{2,1,0:T(8,128)}, f32[32,16,128]{2,1,0:T(8,128)S(1)}, u32[]{:S(2)}, u32[]{:S(2)}) collective-permute-start(f32[32,16,128]{2,1,0:T(8,128)} %get-tuple-element.25), channel_id=1, source_target_pairs={{0,4},{4,8},{8,12},{12,16},{16,20},{20,24},{24,28},{1,5},{5,9},{9,... | collective-permute-start | bytes 786440 | tf_op jit(solution)/shard_map/ppermute | solution.py:440
  12.7 11.5 %collective-permute-start.1 = (f32[32,16,128]{2,1,0:T(8,128)}, f32[32,16,128]{2,1,0:T(8,128)S(1)}, u32[]{:S(2)}, u32[]{:S(2)}) collective-permute-start(f32[32,16,128]{2,1,0:T(8,128)} %get-tuple-element.26), channel_id=1, source_target_pairs={{4,0},{8,4},{12,8},{16,12},{20,16},{24,20},{28,24},{5,1},{9,5},{13... | collective-permute-start | bytes 786440 | tf_op jit(solution)/shard_map/ppermute | solution.py:441
  14.0 10.2 %collective-permute-start.2 = (f32[32,16,128]{2,1,0:T(8,128)}, f32[32,16,128]{2,1,0:T(8,128)S(1)}, u32[]{:S(2)}, u32[]{:S(2)}) collective-permute-start(f32[32,16,128]{2,1,0:T(8,128)} %get-tuple-element.27), channel_id=1, source_target_pairs={{0,1},{1,2},{2,3},{3,0},{4,5},{5,6},{6,7},{7,4},{8,9},{9,10},{10,1... | collective-permute-start | bytes 786440 | tf_op jit(solution)/shard_map/ppermute | solution.py:442
  14.0 10.1 %collective-permute-start.3 = (f32[32,16,128]{2,1,0:T(8,128)}, f32[32,16,128]{2,1,0:T(8,128)S(1)}, u32[]{:S(2)}, u32[]{:S(2)}) collective-permute-start(f32[32,16,128]{2,1,0:T(8,128)} %get-tuple-element.28), channel_id=1, source_target_pairs={{1,0},{2,1},{3,2},{0,3},{5,4},{6,5},{7,6},{4,7},{9,8},{10,9},{11,1... | collective-permute-start | bytes 786440 | tf_op jit(solution)/shard_map/ppermute | solution.py:443
  24.1 0.7 copy-start
  24.1 0.8 %copy-start.1 = (f32[32,16,128]{2,1,0:T(8,128)}, f32[32,16,128]{2,1,0:T(8,128)S(1)}, u32[]{:S(2)}) copy-start(f32[32,16,128]{2,1,0:T(8,128)S(1)} %collective-permute-done.1.i1) | copy-start | bytes 786436
  24.1 0.9 %copy-start.2 = (f32[32,16,128]{2,1,0:T(8,128)}, f32[32,16,128]{2,1,0:T(8,128)S(1)}, u32[]{:S(2)}) copy-start(f32[32,16,128]{2,1,0:T(8,128)S(1)} %collective-permute-done.2.i2) | copy-start | bytes 786436
  25.0 0.7 copy-start.3
  35.7 15.0 %collective-permute-start.4 = (f32[32,8,128]{2,1,0:T(8,128)}, f32[32,8,128]{2,1,0:T(8,128)S(1)}, u32[]{:S(2)}, u32[]{:S(2)}) collective-permute-start(f32[32,8,128]{2,1,0:T(8,128)} %get-tuple-element.31), channel_id=1, source_target_pairs={{0,4},{4,8},{8,12},{12,16},{16,20},{20,24},{24,28},{1,5},{5,9},{9,... | collective-permute-start | bytes 393224 | tf_op jit(solution)/shard_map/ppermute | solution.py:440
  40.1 10.6 %collective-permute-start.5 = (f32[32,8,128]{2,1,0:T(8,128)}, f32[32,8,128]{2,1,0:T(8,128)S(1)}, u32[]{:S(2)}, u32[]{:S(2)}) collective-permute-start(f32[32,8,128]{2,1,0:T(8,128)} %get-tuple-element.32), channel_id=1, source_target_pairs={{4,0},{8,4},{12,8},{16,12},{20,16},{24,20},{28,24},{5,1},{9,5},{13... | collective-permute-start | bytes 393224 | tf_op jit(solution)/shard_map/ppermute | solution.py:441
  41.4 9.3 %collective-permute-start.6 = (f32[32,8,128]{2,1,0:T(8,128)}, f32[32,8,128]{2,1,0:T(8,128)S(1)}, u32[]{:S(2)}, u32[]{:S(2)}) collective-permute-start(f32[32,8,128]{2,1,0:T(8,128)} %get-tuple-element.33), channel_id=1, source_target_pairs={{0,1},{1,2},{2,3},{3,0},{4,5},{5,6},{6,7},{7,4},{8,9},{9,10},{10,1... | collective-permute-start | bytes 393224 | tf_op jit(solution)/shard_map/ppermute | solution.py:442
  41.5 9.3 %collective-permute-start.7 = (f32[32,8,128]{2,1,0:T(8,128)}, f32[32,8,128]{2,1,0:T(8,128)S(1)}, u32[]{:S(2)}, u32[]{:S(2)}) collective-permute-start(f32[32,8,128]{2,1,0:T(8,128)} %get-tuple-element.34), channel_id=1, source_target_pairs={{1,0},{2,1},{3,2},{0,3},{5,4},{6,5},{7,6},{4,7},{9,8},{10,9},{11,1... | collective-permute-start | bytes 393224 | tf_op jit(solution)/shard_map/ppermute | solution.py:443
  50.7 0.7 copy-start.4
  50.8 0.7 copy-start.5
  50.8 0.7 copy-start.6
  50.8 0.7 copy-start.7

commit v2 on v1

--- a/solution.py
+++ b/solution.py
@@ -16,7 +16,7 @@
 SMOOTH_STEP = 32
 SEND_STEP = 32
 ABSORB_STEP = 32
-LOCAL_STEP = 8
+LOCAL_STEP = 16
 
 
 def lane_of(shape):
@@ -96,25 +96,38 @@
         nat_ref[:, t * LANES : (t + 1) * LANES] = jnp.where(low, a[:rows], b[:rows])
 
 
-def smooth_into(inv_ref, y_ref, out_ref, nf, blocks):
+def made(ref, keep_ref):
+    def tile(first, j):
+        w = single(ref, first * 32 + (j // 8) * 256 + j % 8, 8)
+        keep_ref[first + j] = w
+        return w
+
+    return tile
+
+
+def kept(keep_ref):
+    return lambda first, j: keep_ref[first + j]
+
+
+def smooth_into(tile, y_ref, out_ref, nf, blocks):
     def body(g, carry):
         for c in range(SMOOTH_STEP):
-            w = single(inv_ref, g * (32 * SMOOTH_STEP) + (c // 8) * 256 + c % 8, 8)
+            w = tile(g * SMOOTH_STEP, c)
             out_ref[g * SMOOTH_STEP + c] = halves(dot(y_ref[g * SMOOTH_STEP + c], w), nf)
         return carry
 
     lax.fori_loop(0, blocks // SMOOTH_STEP, body, 0)
 
 
-def write_messages(load, y_ref, coup, send_ref, recv_ref, counts_ref, msgs, nf, cap):
+def write_messages(load, y_ref, ready, tile, send_ref, recv_ref, counts_ref, msgs, nf, cap):
     low = lane_of((nf, LANES)) < 64
     for d in range(4):
-        coup_ref = coup(d)
-
-        def body(g, carry, d=d, coup_ref=coup_ref):
+        ready(d)
+
+        def body(g, carry, d=d):
             for j in range(SEND_STEP):
                 c = g * SEND_STEP + j
-                w = single(coup_ref, d * cap * 32 + g * (32 * SEND_STEP) + (j // 8) * 256 + j % 8, 8)
+                w = tile(d * cap + g * SEND_STEP, j)
                 partner = halves(dot(y_ref[recv_ref[d, c]], w), nf)
                 weight = jnp.where(c < counts_ref[0, 0, d], 1.0, 0.0)
                 msgs[d][c] = jnp.where(low, load(send_ref[d, c]) * weight, partner)
@@ -147,7 +160,8 @@
 
 
 def first_kernel(nf, blocks, cap, src_ref, per_ref, edges_ref, signs_ref, inv_hbm, coup_hbm, send_ref, recv_ref, counts_ref,
-                 m0, m1, m2, m3, z_ref, zn_ref, r0_ref, cd_ref, y_ref, x_ref, y0_ref, inv_ref, coup_ref, sems):
+                 m0, m1, m2, m3, z_ref, zn_ref, r0_ref, cd_ref, y_ref, winv_ref, wcoup_ref,
+                 x_ref, y0_ref, inv_ref, coup_ref, sems):
     copies = Copies(sems, [(inv_hbm, inv_ref)] + quarters(coup_hbm, coup_ref))
     fields = src_ref.shape[0]
     width = src_ref.shape[1]
@@ -180,26 +194,29 @@
     matrix = into_rows()
     write_row_form(lambda b: x_ref[b], y0_ref, nf, blocks, matrix)
     copies.wait(0)
-    smooth_into(inv_ref, y0_ref, z_ref, nf, blocks)
+    smooth_into(made(inv_ref, winv_ref), y0_ref, z_ref, nf, blocks)
     write_row_form(lambda b: z_ref[b], y_ref, nf, blocks, matrix)
 
-    def coup(d):
-        copies.wait(1 + d)
-        return coup_ref
-
-    write_messages(lambda b: z_ref[b], y_ref, coup, send_ref, recv_ref, counts_ref, (m0, m1, m2, m3), nf, cap)
+    write_messages(lambda b: z_ref[b], y_ref, lambda d: copies.wait(1 + d), made(coup_ref, wcoup_ref),
+                   send_ref, recv_ref, counts_ref, (m0, m1, m2, m3), nf, cap)
     to_natural(z_ref, zn_ref, blocks)
 
 
-def local_kernel(nf, blocks, kt, cols_ref, tiles_hbm, z_ref, y_ref, acc_ref, x_ref, u_ref, t_ref, tiles_ref, sems):
+def local_kernel(nf, blocks, kt, fresh, cols_ref, tiles_hbm, z_ref, y_ref, acc_ref, *rest):
+    if fresh:
+        w_ref, x_ref, u_ref, t_ref, tiles_ref, sems = rest
+    else:
+        x_ref, u_ref, t_ref = rest
+        w_ref = tiles_hbm
     rows = LOCAL_STEP * kt * 32
 
     def copy(i):
         at = pl.ds(pl.multiple_of(i * rows, rows), rows)
         return pltpu.make_async_copy(tiles_hbm.at[at], tiles_ref.at[at], sems.at[i])
 
-    for i in range(blocks // LOCAL_STEP):
-        copy(i).start()
+    if fresh:
+        for i in range(blocks // LOCAL_STEP):
+            copy(i).start()
 
     def left(b, carry):
         x_ref[b] = stacked(z_ref[b])
@@ -209,10 +226,15 @@
     wide = lane_of((2 * nf, LANES)) < 64
 
     def body(i, carry):
-        copy(i).wait()
+        if fresh:
+            copy(i).wait()
         for s in range(LOCAL_STEP):
             b = i * LOCAL_STEP + s
-            w = jnp.concatenate([pair(tiles_ref, b * (32 * kt) + k, kt) for k in range(0, kt, 2)], axis=1)
+            if fresh:
+                w = jnp.concatenate([pair(tiles_ref, b * (32 * kt) + k, kt) for k in range(0, kt, 2)], axis=1)
+                w_ref[b] = w
+            else:
+                w = w_ref[b]
             t_ref[b] = halves(dot(y_ref[b], w), nf)
             x = [x_ref[lax.rem(b + cols_ref[k, 0], blocks)] for k in range(kt)]
             x = jnp.concatenate([jnp.where(wide, x[k], x[k + 1]) for k in range(0, kt, 2)], axis=1)
@@ -224,9 +246,9 @@
     low = lane_of((nf, LANES)) < 64
 
     def finish(i, carry):
-        out = dot(u_ref[pl.ds(i * 8, 8)].reshape(8 * 2 * nf, LANES), matrix)
-        for j in range(8):
-            b = i * 8 + j
+        out = dot(u_ref[pl.ds(i * 16, 16)].reshape(16 * 2 * nf, LANES), matrix)
+        for j in range(16):
+            b = i * 16 + j
             t = None
             for k in range(0, kt, 2):
                 at = slice(k // 2 * LANES, (k // 2 + 1) * LANES)
@@ -236,24 +258,33 @@
             acc_ref[b] = z_ref[b] + halves(out[j * 2 * nf : (j + 1) * 2 * nf], nf) + t + turn(t)
         return carry
 
-    lax.fori_loop(0, blocks // 8, finish, 0)
-
-
-def absorb(acc_ref, incs, coup, send_ref, recv_ref, counts_ref, nf, cap):
+    lax.fori_loop(0, blocks // 16, finish, 0)
+
+
+def present(d):
+    if d > 1:
+        return None
+    end = 0 if d == 0 else lax.axis_size("slab") - 1
+    return jnp.where(lax.axis_index("slab") == end, 0.0, 1.0)
+
+
+def absorb(acc_ref, incs, tile, send_ref, recv_ref, counts_ref, nf, cap):
     matrix = out_of_rows()
     low = lane_of((nf, LANES)) < 64
     for d in range(4):
-        coup_ref = coup(d)
-
-        def body(g, carry, d=d, coup_ref=coup_ref):
+        there = present(d)
+
+        def body(g, carry, d=d, there=there):
             rows = []
             back = []
             for j in range(ABSORB_STEP):
                 c = g * ABSORB_STEP + j
                 arr = incs[d][c]
+                if there is not None:
+                    arr = arr * there
                 hi, lo = split(arr)
                 x = jnp.where(low, hi, turn(lo)).astype(BF16)
-                w = single(coup_ref, d * cap * 32 + g * (32 * ABSORB_STEP) + (j // 8) * 256 + j % 8, 8)
+                w = tile(d * cap + g * ABSORB_STEP, j)
                 rows.append(stacked(dot_nt(x, w)))
                 weight = jnp.where(c < counts_ref[0, 0, d], 1.0, 0.0)
                 back.append(jnp.where(low, turn(arr), arr) * weight)
@@ -271,35 +302,17 @@
         lax.fori_loop(0, cap // ABSORB_STEP, body, 0)
 
 
-def gathered(copies, coup_ref):
-    def coup(d):
-        copies.wait(2 * d)
-        copies.wait(2 * d + 1)
-        return coup_ref
-
-    return coup
-
-
-def arrivals(incs, inc_ref, coup_hbm, coup_ref):
-    pairs = []
-    for d, part in enumerate(quarters(coup_hbm, coup_ref)):
-        pairs += [(incs[d], inc_ref.at[d]), part]
-    return pairs
-
-
-def second_kernel(nf, blocks, cap, acc_in, i0, i1, i2, i3, inv_hbm, coup_hbm, send_ref, recv_ref, counts_ref,
-                  m0, m1, m2, m3, qn_ref, w_ref, wn_ref, y_ref, acc_ref, y0_ref, inv_ref, coup_ref, inc_ref, sems):
-    copies = Copies(sems, arrivals((i0, i1, i2, i3), inc_ref, coup_hbm, coup_ref) + [(inv_hbm, inv_ref)])
+def second_kernel(nf, blocks, cap, acc_in, i0, i1, i2, i3, winv_ref, wcoup_ref, send_ref, recv_ref, counts_ref,
+                  m0, m1, m2, m3, qn_ref, w_ref, wn_ref, y_ref, acc_ref, y0_ref):
     acc_ref[...] = acc_in[...]
-    incs = [inc_ref.at[d] for d in range(4)]
-    absorb(acc_ref, incs, gathered(copies, coup_ref), send_ref, recv_ref, counts_ref, 2 * nf, cap)
+    coup = kept(wcoup_ref)
+    absorb(acc_ref, (i0, i1, i2, i3), coup, send_ref, recv_ref, counts_ref, 2 * nf, cap)
     to_natural(acc_ref, qn_ref, blocks)
     matrix = into_rows()
     write_row_form(lambda b: acc_ref[b, 0:nf], y0_ref, nf, blocks, matrix)
-    copies.wait(8)
-    smooth_into(inv_ref, y0_ref, w_ref, nf, blocks)
+    smooth_into(kept(winv_ref), y0_ref, w_ref, nf, blocks)
     write_row_form(lambda b: w_ref[b], y_ref, nf, blocks, matrix)
-    write_messages(lambda b: w_ref[b], y_ref, lambda d: coup_ref, send_ref, recv_ref, counts_ref, (m0, m1, m2, m3), nf, cap)
+    write_messages(lambda b: w_ref[b], y_ref, lambda d: None, coup, send_ref, recv_ref, counts_ref, (m0, m1, m2, m3), nf, cap)
     to_natural(w_ref, wn_ref, blocks)
 
 
@@ -307,12 +320,10 @@
     return jnp.sum(jnp.where(lane == at, values, 0.0), axis=1, keepdims=True)
 
 
-def third_kernel(nf, blocks, cap, acc_in, i0, i1, i2, i3, coup_hbm, send_ref, recv_ref, counts_ref,
-                 zn_ref, qn_ref, wn_ref, r0_ref, cd_ref, sn_ref, pay_ref, acc_ref, g_ref, coup_ref, inc_ref, sems):
-    copies = Copies(sems, arrivals((i0, i1, i2, i3), inc_ref, coup_hbm, coup_ref))
+def third_kernel(nf, blocks, cap, acc_in, i0, i1, i2, i3, wcoup_ref, send_ref, recv_ref, counts_ref,
+                 zn_ref, qn_ref, wn_ref, r0_ref, cd_ref, sn_ref, pay_ref, acc_ref, g_ref):
     acc_ref[...] = acc_in[...]
-    incs = [inc_ref.at[d] for d in range(4)]
-    absorb(acc_ref, incs, gathered(copies, coup_ref), send_ref, recv_ref, counts_ref, nf, cap)
+    absorb(acc_ref, (i0, i1, i2, i3), kept(wcoup_ref), send_ref, recv_ref, counts_ref, nf, cap)
     to_natural(acc_ref, sn_ref, blocks)
     z = zn_ref[0:nf, :]
     q = qn_ref[0:nf, :]
@@ -414,12 +425,16 @@
 
 SMEM = pl.BlockSpec(memory_space=pltpu.SMEM)
 VMEM = pl.BlockSpec(memory_space=pltpu.VMEM)
-ANY = pl.BlockSpec(memory_space=pl.ANY)
-PARAMS = pltpu.CompilerParams(vmem_limit_bytes=56 * 1024 * 1024)
+ANY = pl.BlockSpec(memory_space=pltpu.HBM)
+PARAMS = pltpu.CompilerParams(vmem_limit_bytes=20 * 1024 * 1024)
 
 
 def like(*shape, dtype=F32):
-    return jax.ShapeDtypeStruct(shape, dtype)
+    return pltpu.VMEM(shape, dtype)
+
+
+def in_hbm(x):
+    return pltpu.with_memory_space_constraint(x, pltpu.HBM)
 
 
 def call(kernel, ins, outs, scratch, name, flops=0):
@@ -432,8 +447,8 @@
 def exchange(msgs):
     slabs = lax.axis_size("slab")
     sectors = lax.axis_size("sector")
-    up = [(i, i + 1) for i in range(slabs - 1)]
-    down = [(i + 1, i) for i in range(slabs - 1)]
+    up = [(i, (i + 1) % slabs) for i in range(slabs)]
+    down = [((i + 1) % slabs, i) for i in range(slabs)]
     right = [(i, (i + 1) % sectors) for i in range(sectors)]
     left = [((i + 1) % sectors, i) for i in range(sectors)]
     return (
@@ -459,61 +474,61 @@
     both = nf + cycles
     devices = lax.axis_size("slab") * lax.axis_size("sector")
     rho = 1.0 / (cycle_edges.shape[3] * devices)
-    tiles2 = rows_of(tiles[0, 0].reshape(blocks * kt, TILE * TILE), kt)
-    coup2 = rows_of(coupling[0, 0].reshape(4 * cap, TILE * TILE), 8)
-    inv2 = rows_of(inverse_blocks[0, 0], 8)
-    send, recv, cols = send_list[0, 0], recv_rows[0, 0], columns[0, 0].T
-    coup_buf = pltpu.VMEM(coup2.shape, F32)
-    inv_buf = pltpu.VMEM(inv2.shape, F32)
-
+    tiles2 = in_hbm(rows_of(tiles[0, 0].reshape(blocks * kt, TILE * TILE), kt))
+    coup2 = in_hbm(rows_of(coupling[0, 0].reshape(4 * cap, TILE * TILE), 8))
+    inv2 = in_hbm(rows_of(inverse_blocks[0, 0], 8))
+    send, recv, cols = in_hbm(send_list[0, 0]), in_hbm(recv_rows[0, 0]), in_hbm(columns[0, 0].T)
+    counts, periods, src = in_hbm(counts), in_hbm(periods), in_hbm(src)
+    edges, signs = in_hbm(cycle_edges[0, 0]), in_hbm(cycle_signs[0, 0])
     msg = like(cap, both, LANES)
-    *msgs, z, zn, r0, cd, y = call(
+    *msgs, z, zn, r0, cd, y, winv, wcoup = call(
         functools.partial(first_kernel, both, blocks, cap),
         [VMEM] * 4 + [ANY] * 2 + [SMEM] * 3,
         [msg] * 4 + [like(blocks, both, LANES), like(both, width), like(nf, width), like(cycles, width),
-                     like(blocks, 2 * both, LANES, dtype=BF16)],
-        [pltpu.VMEM((blocks, both, LANES), F32), pltpu.VMEM((blocks, 2 * both, LANES), BF16), inv_buf, coup_buf,
-         pltpu.SemaphoreType.DMA((5,))],
+                     like(blocks, 2 * both, LANES, dtype=BF16), like(blocks, LANES, LANES, dtype=BF16),
+                     like(4 * cap, LANES, LANES, dtype=BF16)],
+        [pltpu.VMEM((blocks, both, LANES), F32), pltpu.VMEM((blocks, 2 * both, LANES), BF16), pltpu.VMEM(inv2.shape, F32),
+         pltpu.VMEM(coup2.shape, F32), pltpu.SemaphoreType.DMA((5,))],
         "first",
-    )(src, periods, cycle_edges[0, 0], cycle_signs[0, 0], inv2, coup2, send, recv, counts)
-
-    def local(vector, y, n):
+    )(src, periods, edges, signs, inv2, coup2, send, recv, counts)
+
+    def local(vector, y, n, forms):
+        fresh = forms is None
+        out = [like(blocks, n, LANES)]
+        scratch = [pltpu.VMEM((blocks, 2 * n, LANES), BF16), pltpu.VMEM((blocks, 2 * n, LANES), BF16),
+                   pltpu.VMEM((blocks, n, kt // 2 * LANES), F32)]
+        if fresh:
+            out.append(like(blocks, LANES, kt // 2 * LANES, dtype=BF16))
+            scratch += [pltpu.VMEM(tiles2.shape, F32), pltpu.SemaphoreType.DMA((blocks // LOCAL_STEP,))]
         return call(
-            functools.partial(local_kernel, n, blocks, kt),
-            [SMEM, ANY, VMEM, VMEM],
-            like(blocks, n, LANES),
-            [pltpu.VMEM((blocks, 2 * n, LANES), BF16), pltpu.VMEM((blocks, 2 * n, LANES), BF16),
-             pltpu.VMEM((blocks, n, kt // 2 * LANES), F32), pltpu.VMEM(tiles2.shape, F32),
-             pltpu.SemaphoreType.DMA((blocks // LOCAL_STEP,))],
-            "local", flops=2 * 10**9,
-        )(cols, tiles2, vector, y)
+            functools.partial(local_kernel, n, blocks, kt, fresh),
+            [SMEM, ANY if fresh else VMEM, VMEM, VMEM], out, scratch, "local", flops=2 * 10**9,
+        )(cols, tiles2 if fresh else forms, vector, y)
 
     incoming = exchange(msgs)
-    acc = local(z, y, both)
+    acc, forms = local(z, y, both, None)
     msg = like(cap, nf, LANES)
     *msgs, qn, w, wn, y = call(
         functools.partial(second_kernel, nf, blocks, cap),
-        [VMEM] + [ANY] * 6 + [SMEM] * 3,
+        [VMEM] * 7 + [SMEM] * 3,
         [msg] * 4 + [like(both, width), like(blocks, nf, LANES), like(nf, width), like(blocks, 2 * nf, LANES, dtype=BF16)],
-        [pltpu.VMEM((blocks, both, LANES), F32), pltpu.VMEM((blocks, 2 * nf, LANES), BF16), inv_buf, coup_buf,
-         pltpu.VMEM((4, cap, both, LANES), F32), pltpu.SemaphoreType.DMA((9,))],
+        [pltpu.VMEM((blocks, both, LANES), F32), pltpu.VMEM((blocks, 2 * nf, LANES), BF16)],
         "second",
-    )(acc, *incoming, inv2, coup2, send, recv, counts)
+    )(acc, *incoming, winv, wcoup, send, recv, counts)
     incoming = exchange(msgs)
-    acc = local(w, y, nf)
+    (acc,) = local(w, y, nf, forms)
     sn, pay = call(
         functools.partial(third_kernel, nf, blocks, cap),
-        [VMEM] + [ANY] * 5 + [SMEM] * 3 + [VMEM] * 5,
+        [VMEM] * 6 + [SMEM] * 3 + [VMEM] * 5,
         [like(nf, width), like(devices, nf, LANES)],
-        [pltpu.VMEM((blocks, nf, LANES), F32), pltpu.VMEM((24, LANES), F32), coup_buf,
-         pltpu.VMEM((4, cap, nf, LANES), F32), pltpu.SemaphoreType.DMA((8,))],
+        [pltpu.VMEM((blocks, nf, LANES), F32), pltpu.VMEM((24, LANES), F32)],
         "third",
-    )(acc, *incoming, coup2, send, recv, counts, zn, qn, wn, r0, cd)
+    )(acc, *incoming, wcoup, send, recv, counts, zn, qn, wn, r0, cd)
     everyone = lax.all_to_all(pay, AXES, 0, 0)
     out, res = call(
         functools.partial(last_kernel, nf, rho),
         [VMEM] * 7,
-        [like(nf, width), like(nf, width)],
+        [jax.ShapeDtypeStruct((nf, width), F32)] * 2,
         [],
         "last",
     )(everyone, zn, wn, qn, r0, cd, sn)

time: 78.4 us -> 57 us (0.73)
  Pallas kernels: 43.1 us -> 27.7 us
  blocking collectives: 16.1 us -> 11.3 us
  waiting for transfers between devices: 0.18 us -> 2.67 us
  local copies, waits for them, and re-layouts: 2.28 us -> 0 us
  starting transfers between devices: 15.5 us -> 14.4 us
    pallas_call x5, Pallas kernels: 36 us -> 21.9 us  [the longest x2 9.78 us: local(): call(functools.partial(local_kernel, n, blocks, kt, fresh), [SMEM, ANY if...]
    ppermute x2, starting transfers between devices: 9.32 us -> 3.37 us  [exchange(): lax.ppermute(msgs[1], 'slab', up)]
    ppermute x2, starting transfers between devices: 2.58 us -> 7.52 us  [exchange(): lax.ppermute(msgs[0], 'slab', down)]
    all_to_all x1, blocking collectives: 16.1 us -> 11.3 us  [on_device(): everyone = lax.all_to_all(pay, AXES, 0, 0)]
    unnamed x16 -> x0, local copies, waits for them, and re-layouts: 2.28 us -> none
    ppermute x2, waiting for transfers between devices: 0.01 us -> 2.2 us  [exchange(): lax.ppermute(msgs[0], 'slab', down)]
    pallas_call x1, Pallas kernels: 7.12 us -> 5.82 us  [on_device(): call(functools.partial(first_kernel, both, blocks, cap), [VMEM] * 4 + [AN...]
  transfers between devices with their start and end apart: 8 -> 8, of which waited for: 1 -> 2; matrix products, arithmetic and copies ran while one was open for 0% -> 0% of each run, Pallas kernels for 20% -> 17%
where the time goes in v2:
time: 57 us; the launch traced here: 56.8 us
  Pallas kernels  27.7 us (49%)
  starting transfers between devices  14.4 us (25%)
  blocking collectives  11.3 us (20%)
  waiting for transfers between devices  2.67 us (5%)
  between operations  0.68 us (1%)
    all_to_all x1, blocking collectives, on_device(): everyone = lax.all_to_all(pay, AXES, 0, 0)  11.3 us
    pallas_call x2, Pallas kernels, local(): call(functools.partial(local_kernel, n, blocks, kt, fresh), [SMEM, ANY if...  9.78 us
    ppermute x2, starting transfers between devices, exchange(): lax.ppermute(msgs[0], 'slab', down)  7.52 us
    pallas_call x1, Pallas kernels, on_device(): call(functools.partial(second_kernel, nf, blocks, cap), [VMEM] * 7 + [SME...  6.39 us
    pallas_call x1, Pallas kernels, on_device(): call(functools.partial(first_kernel, both, blocks, cap), [VMEM] * 4 + [AN...  5.82 us
    pallas_call x1, Pallas kernels, on_device(): call(functools.partial(third_kernel, nf, blocks, cap), [VMEM] * 6 + [SMEM...  3.79 us
    ppermute x2, starting transfers between devices, exchange(): lax.ppermute(msgs[2], 'sector', left)  3.49 us
    ppermute x2, starting transfers between devices, exchange(): lax.ppermute(msgs[1], 'slab', up)  3.37 us
  transfers between devices with their start and end apart: 8, of which 2 were waited for; matrix products, arithmetic and copies ran while one was open for 0% of the time, Pallas kernels for 17%

profile of v2, /device:TPU:0, one launch (start us, length us, event | category | flops | bytes accessed | tf_op | source)
XLA Modules:
  0.0 56.8 jit_solution(13397824038192854061)
XLA Ops:
  0.6 5.8 %first.1 = (f32[32,16,128]{2,1,0:T(8,128)S(1)}, f32[32,16,128]{2,1,0:T(8,128)S(1)}, f32[32,16,128]{2,1,0:T(8,128)S(1)}, f32[32,16,128]{2,1,0:T(8,128)S(1)}, f32[...) custom-call(f32[8,4096]{1,0:T(8,128)} %bitcast.27, ...), custom_call_target="tpu_custom_call" | custom-call | tf_op jit(solution)/shard_map/first/pallas_call | solution.py:484
  6.5 3.0 %collective-permute-start = (f32[32,16,128]{2,1,0:T(8,128)S(1)}, f32[32,16,128]{2,1,0:T(8,128)S(1)}, u32[]{:S(2)}, u32[]{:S(2)}) collective-permute-start(f32[32,16,128]{2,1,0:T(8,128)S(1)} %get-tuple-element.31), channel_id=1, source_target_pairs={{0,4},{4,8},{8,12},{12,16},{16,20},{20,24},{24,28},{28,0},{1,5},{5... | collective-permute-start | bytes 786440 | tf_op jit(solution)/shard_map/ppermute | solution.py:455
  9.5 3.1 %collective-permute-start.1 = (f32[32,16,128]{2,1,0:T(8,128)S(1)}, f32[32,16,128]{2,1,0:T(8,128)S(1)}, u32[]{:S(2)}, u32[]{:S(2)}) collective-permute-start(f32[32,16,128]{2,1,0:T(8,128)S(1)} %get-tuple-element.32), channel_id=1, source_target_pairs={{4,0},{8,4},{12,8},{16,12},{20,16},{24,20},{28,24},{0,28},{5,1},{9... | collective-permute-start | bytes 786440 | tf_op jit(solution)/shard_map/ppermute | solution.py:456
  12.6 0.0 collective-permute-start.2
  12.6 1.7 %collective-permute-start.3 = (f32[32,16,128]{2,1,0:T(8,128)S(1)}, f32[32,16,128]{2,1,0:T(8,128)S(1)}, u32[]{:S(2)}, u32[]{:S(2)}) collective-permute-start(f32[32,16,128]{2,1,0:T(8,128)S(1)} %get-tuple-element.34), channel_id=1, source_target_pairs={{1,0},{2,1},{3,2},{0,3},{5,4},{6,5},{7,6},{4,7},{9,8},{10,9},{11,1... | collective-permute-start | bytes 786440 | tf_op jit(solution)/shard_map/ppermute | solution.py:458
  14.3 5.9 %local.2 = (f32[64,16,128]{2,1,0:T(8,128)S(1)}, bf16[64,128,256]{2,1,0:T(8,128)(2,1)S(1)}) custom-call(s32[4,64]{1,0:T(4,128)} %bitcast.39, f32[8192,128]{1,0:T(8,128)} %bitcast.36, f32[64,16,128]{2,1,0:T(8,128)S(1)} %get-tuple-element.27.z_ref, bf16[64,32,128]{2,1,0:T(8,128)(2,1)S(1)} %get-tuple-element.28.y_ref), custom_call_target="tpu_custom_call" | custom-call | flops 2000000000 | bytes 8388608 | tf_op jit(solution)/shard_map/local/pallas_call | solution.py:503
  20.2 0.5 collective-permute-done.i0
  20.7 2.2 %collective-permute-done.1.i1 = f32[32,16,128]{2,1,0:T(8,128)S(1)} collective-permute-done((f32[32,16,128]{2,1,0:T(8,128)S(1)}, f32[32,16,128]{2,1,0:T(8,128)S(1)}, u32[]{:S(2)}, u32[]{:S(2)}) %collective-permute-start.1) | collective-permute-done | bytes 262176 | tf_op jit(solution)/shard_map/ppermute | solution.py:456
  22.9 0.0 collective-permute-done.2.i2
  22.9 0.0 collective-permute-done.3.i3
  22.9 6.4 %second.1 = (f32[32,8,128]{2,1,0:T(8,128)S(1)}, f32[32,8,128]{2,1,0:T(8,128)S(1)}, f32[32,8,128]{2,1,0:T(8,128)S(1)}, f32[32,8,128]{2,1,0:T(8,128)S(1)}, f32[16,...) custom-call(f32[64,16,128]{2,1,0:T(8,128)S(1)} %get-tuple-element.30.acc_, ...), custom_call_target="tpu_custom_call" | custom-call | tf_op jit(solution)/shard_map/second/pallas_call | solution.py:511
  29.3 0.3 collective-permute-start.4
  29.6 4.4 %collective-permute-start.5 = (f32[32,8,128]{2,1,0:T(8,128)S(1)}, f32[32,8,128]{2,1,0:T(8,128)S(1)}, u32[]{:S(2)}, u32[]{:S(2)}) collective-permute-start(f32[32,8,128]{2,1,0:T(8,128)S(1)} %get-tuple-element.40), channel_id=1, source_target_pairs={{4,0},{8,4},{12,8},{16,12},{20,16},{24,20},{28,24},{0,28},{5,1},{9... | collective-permute-start | bytes 393224 | tf_op jit(solution)/shard_map/ppermute | solution.py:456
  34.0 0.0 collective-permute-start.6
  34.0 1.7 %collective-permute-start.7 = (f32[32,8,128]{2,1,0:T(8,128)S(1)}, f32[32,8,128]{2,1,0:T(8,128)S(1)}, u32[]{:S(2)}, u32[]{:S(2)}) collective-permute-start(f32[32,8,128]{2,1,0:T(8,128)S(1)} %get-tuple-element.42), channel_id=1, source_target_pairs={{1,0},{2,1},{3,2},{0,3},{5,4},{6,5},{7,6},{4,7},{9,8},{10,9},{11,1... | collective-permute-start | bytes 393224 | tf_op jit(solution)/shard_map/ppermute | solution.py:458
  35.8 3.9 %local.3.acc_in = f32[64,8,128]{2,1,0:T(8,128)S(1)} custom-call(s32[4,64]{1,0:T(4,128)} %bitcast.40, bf16[64,128,256]{2,1,0:T(8,128)(2,1)S(1)} %get-tuple-element.29.tiles_hbm, f32[64,8,128]{2,1,0:T(8,128)S(1)} %get-tuple-element.37.z_ref, bf16[64,16,128]{2,1,0:T(8,128)(2,1)S(1)} %get-tuple-element.38.y_ref), custom_call_target="tpu_custom_call" | custom-call | flops 2000000000 | bytes 8388608 | tf_op jit(solution)/shard_map/local/pallas_call | solution.py:503
  39.7 0.0 collective-permute-done.4.i0
  39.7 0.0 collective-permute-done.5.i1
  39.7 0.0 collective-permute-done.6.i2
  39.7 0.0 collective-permute-done.7.i3
  39.7 3.8 %third.1 = (f32[8,4096]{1,0:T(8,128)S(1)}, f32[32,8,128]{2,1,0:T(8,128)S(1)}) custom-call(f32[64,8,128]{2,1,0:T(8,128)S(1)} %local.3.acc_in, f32[32,8,128]{2,1,0:T(8,128)S(1)} %collective-permute-done.4.i0, f32[32,8,128]{2,1,0:T(8,128)S(1)} %collective-permute-done.5.i1, f32[32,8,128]{2,1,0:T(8,128)S(1)} %collective-permute-done.6.i2, ...), custom_call_target="tpu_custom_call" | custom-call | tf_op jit(solution)/shard_map/third/pallas_call | solution.py:520
  43.5 11.3 %all_to_all.5.all_ref = f32[32,8,128]{2,1,0:T(8,128)S(1)} all-to-all(f32[32,8,128]{2,1,0:T(8,128)S(1)} %get-tuple-element.48), channel_id=1, replica_groups=mesh['slab'=8,'sector'=4] {'slab','sector'}, dimensions={0} | all-to-all | bytes 262144 | tf_op jit(solution)/shard_map/all_to_all | solution.py:527
  54.8 1.9 %last.1 = (f32[8,4096]{1,0:T(8,128)}, f32[8,4096]{1,0:T(8,128)}) custom-call(f32[32,8,128]{2,1,0:T(8,128)S(1)} %all_to_all.5.all_ref, f32[16,4096]{1,0:T(8,128)S(1)} %get-tuple-element.43.zn_ref, f32[8,4096]{1,0:T(8,128)S(1)} %get-tuple-element.45.wn_ref, f32[16,4096]{1,0:T(8,128)S(1)} %get-tuple-element.44.qn_ref, f32[8,4096]{1,0:T(8,128)S(1)} %get-tuple-element.46.r0_ref, ...), custom_call_target="tpu_custom_call" | custom-call | tf_op jit(solution)/shard_map/last/pallas_call | solution.py:528
Async XLA Ops:
  6.5 14.2 %collective-permute-start = (f32[32,16,128]{2,1,0:T(8,128)S(1)}, f32[32,16,128]{2,1,0:T(8,128)S(1)}, u32[]{:S(2)}, u32[]{:S(2)}) collective-permute-start(f32[32,16,128]{2,1,0:T(8,128)S(1)} %get-tuple-element.31), channel_id=1, source_target_pairs={{0,4},{4,8},{8,12},{12,16},{16,20},{20,24},{24,28},{28,0},{1,5},{5... | collective-permute-start | bytes 786440 | tf_op jit(solution)/shard_map/ppermute | solution.py:455
  9.5 13.4 %collective-permute-start.1 = (f32[32,16,128]{2,1,0:T(8,128)S(1)}, f32[32,16,128]{2,1,0:T(8,128)S(1)}, u32[]{:S(2)}, u32[]{:S(2)}) collective-permute-start(f32[32,16,128]{2,1,0:T(8,128)S(1)} %get-tuple-element.32), channel_id=1, source_target_pairs={{4,0},{8,4},{12,8},{16,12},{20,16},{24,20},{28,24},{0,28},{5,1},{9... | collective-permute-start | bytes 786440 | tf_op jit(solution)/shard_map/ppermute | solution.py:456
  12.6 10.3 %collective-permute-start.2 = (f32[32,16,128]{2,1,0:T(8,128)S(1)}, f32[32,16,128]{2,1,0:T(8,128)S(1)}, u32[]{:S(2)}, u32[]{:S(2)}) collective-permute-start(f32[32,16,128]{2,1,0:T(8,128)S(1)} %get-tuple-element.33), channel_id=1, source_target_pairs={{0,1},{1,2},{2,3},{3,0},{4,5},{5,6},{6,7},{7,4},{8,9},{9,10},{10,1... | collective-permute-start | bytes 786440 | tf_op jit(solution)/shard_map/ppermute | solution.py:457
  12.6 10.3 %collective-permute-start.3 = (f32[32,16,128]{2,1,0:T(8,128)S(1)}, f32[32,16,128]{2,1,0:T(8,128)S(1)}, u32[]{:S(2)}, u32[]{:S(2)}) collective-permute-start(f32[32,16,128]{2,1,0:T(8,128)S(1)} %get-tuple-element.34), channel_id=1, source_target_pairs={{1,0},{2,1},{3,2},{0,3},{5,4},{6,5},{7,6},{4,7},{9,8},{10,9},{11,1... | collective-permute-start | bytes 786440 | tf_op jit(solution)/shard_map/ppermute | solution.py:458
  29.3 10.4 %collective-permute-start.4 = (f32[32,8,128]{2,1,0:T(8,128)S(1)}, f32[32,8,128]{2,1,0:T(8,128)S(1)}, u32[]{:S(2)}, u32[]{:S(2)}) collective-permute-start(f32[32,8,128]{2,1,0:T(8,128)S(1)} %get-tuple-element.39), channel_id=1, source_target_pairs={{0,4},{4,8},{8,12},{12,16},{16,20},{20,24},{24,28},{28,0},{1,5},{5... | collective-permute-start | bytes 393224 | tf_op jit(solution)/shard_map/ppermute | solution.py:455
  29.6 10.1 %collective-permute-start.5 = (f32[32,8,128]{2,1,0:T(8,128)S(1)}, f32[32,8,128]{2,1,0:T(8,128)S(1)}, u32[]{:S(2)}, u32[]{:S(2)}) collective-permute-start(f32[32,8,128]{2,1,0:T(8,128)S(1)} %get-tuple-element.40), channel_id=1, source_target_pairs={{4,0},{8,4},{12,8},{16,12},{20,16},{24,20},{28,24},{0,28},{5,1},{9... | collective-permute-start | bytes 393224 | tf_op jit(solution)/shard_map/ppermute | solution.py:456
  34.0 5.7 %collective-permute-start.6 = (f32[32,8,128]{2,1,0:T(8,128)S(1)}, f32[32,8,128]{2,1,0:T(8,128)S(1)}, u32[]{:S(2)}, u32[]{:S(2)}) collective-permute-start(f32[32,8,128]{2,1,0:T(8,128)S(1)} %get-tuple-element.41), channel_id=1, source_target_pairs={{0,1},{1,2},{2,3},{3,0},{4,5},{5,6},{6,7},{7,4},{8,9},{9,10},{10,1... | collective-permute-start | bytes 393224 | tf_op jit(solution)/shard_map/ppermute | solution.py:457
  34.0 5.7 %collective-permute-start.7 = (f32[32,8,128]{2,1,0:T(8,128)S(1)}, f32[32,8,128]{2,1,0:T(8,128)S(1)}, u32[]{:S(2)}, u32[]{:S(2)}) collective-permute-start(f32[32,8,128]{2,1,0:T(8,128)S(1)} %get-tuple-element.42), channel_id=1, source_target_pairs={{1,0},{2,1},{3,2},{0,3},{5,4},{6,5},{7,6},{4,7},{9,8},{10,9},{11,1... | collective-permute-start | bytes 393224 | tf_op jit(solution)/shard_map/ppermute | solution.py:458

commit v3 on v2

--- a/solution.py
+++ b/solution.py
@@ -72,16 +72,39 @@
     return lax.dot_general(a, b, (((1,), (1,)), ((), ())), preferred_element_type=F32)
 
 
+def rows_and_lanes(parts):
+    return jnp.concatenate([jnp.concatenate(row, axis=1) for row in parts], axis=0)
+
+
+def turned_products(ys, ws, nf):
+    none = jnp.zeros_like(ys[0])
+    left = rows_and_lanes([[ys[0], none], [ys[1], none], [none, ys[2]], [none, ys[3]]])
+    out = dot(left, rows_and_lanes([ws[:2], ws[2:]]))
+    n = 2 * nf
+    return [halves(out[i * n : (i + 1) * n, i % 2 * LANES : (i % 2 + 1) * LANES], nf) for i in range(4)]
+
+
+def straight_products(xs, ws, nf):
+    none = jnp.zeros_like(xs[0])
+    left = rows_and_lanes([[xs[0], none], [none, xs[1]], [xs[2], none], [none, xs[3]]]).astype(BF16)
+    out = dot_nt(left, rows_and_lanes([ws[:2], ws[2:]]))
+    return [out[i * nf : (i + 1) * nf, i // 2 * LANES : (i // 2 + 1) * LANES] for i in range(4)]
+
+
 def halves(out, nf):
     return out[:nf] + out[nf:]
 
 
-def write_row_form(load, y_ref, nf, blocks, matrix):
+def write_row_form(load, y_ref, nf, blocks, matrix, narrow_ref=None):
     def body(i, carry):
         x = jnp.concatenate([stacked(load(i * ROWS_STEP + j)) for j in range(ROWS_STEP)], axis=0)
-        out = dot(x, matrix).astype(BF16)
+        out = dot(x, matrix)
         for j in range(ROWS_STEP):
-            y_ref[i * ROWS_STEP + j] = out[j * 2 * nf : (j + 1) * 2 * nf]
+            o = out[j * 2 * nf : (j + 1) * 2 * nf]
+            y_ref[i * ROWS_STEP + j] = o.astype(BF16)
+            if narrow_ref is not None:
+                half = nf // 2
+                narrow_ref[i * ROWS_STEP + j] = jnp.concatenate([o[:half], o[nf : nf + half]], axis=0).astype(BF16)
         return carry
 
     lax.fori_loop(0, blocks // ROWS_STEP, body, 0)
@@ -111,9 +134,11 @@
 
 def smooth_into(tile, y_ref, out_ref, nf, blocks):
     def body(g, carry):
-        for c in range(SMOOTH_STEP):
-            w = tile(g * SMOOTH_STEP, c)
-            out_ref[g * SMOOTH_STEP + c] = halves(dot(y_ref[g * SMOOTH_STEP + c], w), nf)
+        for c in range(0, SMOOTH_STEP, 4):
+            ws = [tile(g * SMOOTH_STEP, c + i) for i in range(4)]
+            at = g * SMOOTH_STEP + c
+            for i, value in enumerate(turned_products([y_ref[at + i] for i in range(4)], ws, nf)):
+                out_ref[at + i] = value
         return carry
 
     lax.fori_loop(0, blocks // SMOOTH_STEP, body, 0)
@@ -121,16 +146,22 @@
 
 def write_messages(load, y_ref, ready, tile, send_ref, recv_ref, counts_ref, msgs, nf, cap):
     low = lane_of((nf, LANES)) < 64
-    for d in range(4):
-        ready(d)
-
-        def body(g, carry, d=d):
-            for j in range(SEND_STEP):
+    for way in range(4):
+        ready(way)
+        d = sends(way)
+
+        def body(g, carry, d=d, way=way):
+            for j in range(0, SEND_STEP, 4):
                 c = g * SEND_STEP + j
-                w = tile(d * cap + g * SEND_STEP, j)
-                partner = halves(dot(y_ref[recv_ref[d, c]], w), nf)
-                weight = jnp.where(c < counts_ref[0, 0, d], 1.0, 0.0)
-                msgs[d][c] = jnp.where(low, load(send_ref[d, c]) * weight, partner)
+                ws = [tile(d * cap + g * SEND_STEP, j + i) for i in range(4)]
+                ys = [y_ref[recv_ref[d, c + i]] for i in range(4)]
+                for i, partner in enumerate(turned_products(ys, ws, nf)):
+                    weight = jnp.where(c + i < counts_ref[0, 0, d], 1.0, 0.0)
+                    value = jnp.where(low, load(send_ref[d, c + i]) * weight, partner)
+                    at = 0
+                    for msg in msgs[way]:
+                        msg[c + i] = value[at : at + msg.shape[1]]
+                        at += msg.shape[1]
             return carry
 
         lax.fori_loop(0, cap // SEND_STEP, body, 0)
@@ -160,8 +191,8 @@
 
 
 def first_kernel(nf, blocks, cap, src_ref, per_ref, edges_ref, signs_ref, inv_hbm, coup_hbm, send_ref, recv_ref, counts_ref,
-                 m0, m1, m2, m3, z_ref, zn_ref, r0_ref, cd_ref, y_ref, winv_ref, wcoup_ref,
-                 x_ref, y0_ref, inv_ref, coup_ref, sems):
+                 m0, m1, m2, m3, d0, d1, z_ref, zn_ref, r0_ref, cd_ref, narrow_ref, winv_ref, wcoup_ref,
+                 x_ref, y0_ref, y_ref, inv_ref, coup_ref, sems):
     copies = Copies(sems, [(inv_hbm, inv_ref)] + quarters(coup_hbm, coup_ref))
     fields = src_ref.shape[0]
     width = src_ref.shape[1]
@@ -195,10 +226,15 @@
     write_row_form(lambda b: x_ref[b], y0_ref, nf, blocks, matrix)
     copies.wait(0)
     smooth_into(made(inv_ref, winv_ref), y0_ref, z_ref, nf, blocks)
-    write_row_form(lambda b: z_ref[b], y_ref, nf, blocks, matrix)
-
-    write_messages(lambda b: z_ref[b], y_ref, lambda d: copies.wait(1 + d), made(coup_ref, wcoup_ref),
-                   send_ref, recv_ref, counts_ref, (m0, m1, m2, m3), nf, cap)
+    write_row_form(lambda b: z_ref[b], y_ref, nf, blocks, matrix, narrow_ref)
+
+
+    def ready(way):
+        for part in ((0, 1), (), (3,), (2,))[way]:
+            copies.wait(1 + part)
+
+    write_messages(lambda b: z_ref[b], y_ref, ready, made(coup_ref, wcoup_ref),
+                   send_ref, recv_ref, counts_ref, ((m0, d0), (m1, d1), (m2,), (m3,)), nf, cap)
     to_natural(z_ref, zn_ref, blocks)
 
 
@@ -219,7 +255,7 @@
             copy(i).start()
 
     def left(b, carry):
-        x_ref[b] = stacked(z_ref[b])
+        x_ref[b] = stacked(z_ref[b, 0:nf])
         return carry
 
     lax.fori_loop(0, blocks, left, 0, unroll=8)
@@ -228,17 +264,26 @@
     def body(i, carry):
         if fresh:
             copy(i).wait()
-        for s in range(LOCAL_STEP):
+        for s in range(0, LOCAL_STEP, 2):
+            xs, ws = [], []
             b = i * LOCAL_STEP + s
-            if fresh:
-                w = jnp.concatenate([pair(tiles_ref, b * (32 * kt) + k, kt) for k in range(0, kt, 2)], axis=1)
-                w_ref[b] = w
-            else:
-                w = w_ref[b]
-            t_ref[b] = halves(dot(y_ref[b], w), nf)
-            x = [x_ref[lax.rem(b + cols_ref[k, 0], blocks)] for k in range(kt)]
-            x = jnp.concatenate([jnp.where(wide, x[k], x[k + 1]) for k in range(0, kt, 2)], axis=1)
-            u_ref[b] = stacked(halves(dot_nt(x, w), nf))
+            for at in (b, b + 1):
+                if fresh:
+                    w = jnp.concatenate([pair(tiles_ref, at * (32 * kt) + k, kt) for k in range(0, kt, 2)], axis=1)
+                    w_ref[at] = w
+                    ws.append(w)
+                else:
+                    ws.append(w_ref[at])
+                x = [x_ref[lax.rem(at + cols_ref[k, 0], blocks)] for k in range(kt)]
+                xs.append(jnp.concatenate([jnp.where(wide, x[k], x[k + 1]) for k in range(0, kt, 2)], axis=1))
+            w = jnp.concatenate(ws, axis=0)
+            none = jnp.zeros_like(y_ref[b])
+            out = dot(rows_and_lanes([[y_ref[b], none], [none, y_ref[b + 1]]]), w)
+            t_ref[b] = halves(out[: 2 * nf], nf)
+            t_ref[b + 1] = halves(out[2 * nf :], nf)
+            out = dot_nt(jnp.concatenate(xs, axis=0), w)
+            u_ref[b] = stacked(halves(out[: 2 * nf, :LANES], nf))
+            u_ref[b + 1] = stacked(halves(out[2 * nf :, LANES:], nf))
         return carry
 
     lax.fori_loop(0, blocks // LOCAL_STEP, body, 0)
@@ -246,48 +291,63 @@
     low = lane_of((nf, LANES)) < 64
 
     def finish(i, carry):
-        out = dot(u_ref[pl.ds(i * 16, 16)].reshape(16 * 2 * nf, LANES), matrix)
-        for j in range(16):
-            b = i * 16 + j
+        out = dot(u_ref[pl.ds(i * 32, 32)].reshape(32 * 2 * nf, LANES), matrix)
+        for j in range(32):
+            b = i * 32 + j
             t = None
             for k in range(0, kt, 2):
                 at = slice(k // 2 * LANES, (k // 2 + 1) * LANES)
                 v = jnp.where(low, t_ref[lax.rem(b + blocks - cols_ref[k, 0], blocks), :, at],
                               t_ref[lax.rem(b + blocks - cols_ref[k + 1, 0], blocks), :, at])
                 t = v if t is None else t + v
-            acc_ref[b] = z_ref[b] + halves(out[j * 2 * nf : (j + 1) * 2 * nf], nf) + t + turn(t)
+            acc_ref[b] = z_ref[b, 0:nf] + halves(out[j * 2 * nf : (j + 1) * 2 * nf], nf) + t + turn(t)
         return carry
 
-    lax.fori_loop(0, blocks // 16, finish, 0)
-
-
-def present(d):
-    if d > 1:
+    lax.fori_loop(0, blocks // 32, finish, 0)
+
+
+def odd_sector():
+    return lax.rem(lax.axis_index("sector"), 2)
+
+
+def sends(way):
+    return 1 - odd_sector() if way == 0 else odd_sector() if way == 1 else 5 - way
+
+
+def receives(way):
+    return odd_sector() if way == 0 else 1 - odd_sector() if way == 1 else way
+
+
+def present(way, d):
+    if way > 1:
         return None
-    end = 0 if d == 0 else lax.axis_size("slab") - 1
+    end = d * (lax.axis_size("slab") - 1)
     return jnp.where(lax.axis_index("slab") == end, 0.0, 1.0)
 
 
 def absorb(acc_ref, incs, tile, send_ref, recv_ref, counts_ref, nf, cap):
     matrix = out_of_rows()
     low = lane_of((nf, LANES)) < 64
-    for d in range(4):
-        there = present(d)
-
-        def body(g, carry, d=d, there=there):
+    for way in range(4):
+        d = receives(way)
+        there = present(way, d)
+
+        def body(g, carry, d=d, way=way, there=there):
             rows = []
             back = []
-            for j in range(ABSORB_STEP):
-                c = g * ABSORB_STEP + j
-                arr = incs[d][c]
-                if there is not None:
-                    arr = arr * there
-                hi, lo = split(arr)
-                x = jnp.where(low, hi, turn(lo)).astype(BF16)
-                w = tile(d * cap + g * ABSORB_STEP, j)
-                rows.append(stacked(dot_nt(x, w)))
-                weight = jnp.where(c < counts_ref[0, 0, d], 1.0, 0.0)
-                back.append(jnp.where(low, turn(arr), arr) * weight)
+            for j in range(0, ABSORB_STEP, 4):
+                xs = []
+                for i in range(4):
+                    c = g * ABSORB_STEP + j + i
+                    arr = jnp.concatenate([inc[c, at : at + nf // len(incs[way])] for inc, at in incs[way]], axis=0)
+                    if there is not None:
+                        arr = arr * there
+                    hi, lo = split(arr)
+                    xs.append(jnp.where(low, hi, turn(lo)))
+                    weight = jnp.where(c < counts_ref[0, 0, d], 1.0, 0.0)
+                    back.append(jnp.where(low, turn(arr), arr) * weight)
+                ws = [tile(d * cap + g * ABSORB_STEP, j + i) for i in range(4)]
+                rows += [stacked(u) for u in straight_products(xs, ws, nf)]
             out = dot(jnp.concatenate(rows, axis=0), matrix)
             spots = [recv_ref[d, g * ABSORB_STEP + j] for j in range(ABSORB_STEP)]
             old = [acc_ref[s] for s in spots]
@@ -302,17 +362,20 @@
         lax.fori_loop(0, cap // ABSORB_STEP, body, 0)
 
 
-def second_kernel(nf, blocks, cap, acc_in, i0, i1, i2, i3, winv_ref, wcoup_ref, send_ref, recv_ref, counts_ref,
-                  m0, m1, m2, m3, qn_ref, w_ref, wn_ref, y_ref, acc_ref, y0_ref):
+def second_kernel(nf, blocks, cap, acc_in, i0, i1, i2, i3, z_ref, winv_ref, wcoup_ref, send_ref, recv_ref, counts_ref,
+                  m0, m1, m2, m3, qn_ref, wd_ref, wn_ref, y_ref, acc_ref, y0_ref, w_ref, narrow_ref):
     acc_ref[...] = acc_in[...]
     coup = kept(wcoup_ref)
-    absorb(acc_ref, (i0, i1, i2, i3), coup, send_ref, recv_ref, counts_ref, 2 * nf, cap)
+    absorb(acc_ref, [[(inc, 0)] for inc in (i0, i1, i2, i3)], coup, send_ref, recv_ref, counts_ref, nf, cap)
+    matrix = into_rows()
+    write_row_form(lambda b: acc_ref[b], y0_ref, nf, blocks, matrix)
+    smooth_into(kept(winv_ref), y0_ref, w_ref, nf, blocks)
+    for b in range(blocks):
+        wd_ref[b] = jnp.concatenate([w_ref[b], z_ref[b, nf:]], axis=0)
+    write_row_form(lambda b: wd_ref[b], y_ref, wd_ref.shape[1], blocks, matrix, narrow_ref)
+    write_messages(lambda b: w_ref[b], narrow_ref, lambda d: None, coup, send_ref, recv_ref, counts_ref,
+                   ((m0,), (m1,), (m2,), (m3,)), nf, cap)
     to_natural(acc_ref, qn_ref, blocks)
-    matrix = into_rows()
-    write_row_form(lambda b: acc_ref[b, 0:nf], y0_ref, nf, blocks, matrix)
-    smooth_into(kept(winv_ref), y0_ref, w_ref, nf, blocks)
-    write_row_form(lambda b: w_ref[b], y_ref, nf, blocks, matrix)
-    write_messages(lambda b: w_ref[b], y_ref, lambda d: None, coup, send_ref, recv_ref, counts_ref, (m0, m1, m2, m3), nf, cap)
     to_natural(w_ref, wn_ref, blocks)
 
 
@@ -320,16 +383,22 @@
     return jnp.sum(jnp.where(lane == at, values, 0.0), axis=1, keepdims=True)
 
 
-def third_kernel(nf, blocks, cap, acc_in, i0, i1, i2, i3, wcoup_ref, send_ref, recv_ref, counts_ref,
+def packed(x):
+    return jnp.where(lane_of((4, LANES)) < 64, x[0:4], turn(x[4:8]))
+
+
+def third_kernel(nf, blocks, cap, acc_in, i0, i1, i2, i3, d0, d1, e2, e3, wcoup_ref, send_ref, recv_ref, counts_ref,
                  zn_ref, qn_ref, wn_ref, r0_ref, cd_ref, sn_ref, pay_ref, acc_ref, g_ref):
     acc_ref[...] = acc_in[...]
-    absorb(acc_ref, (i0, i1, i2, i3), kept(wcoup_ref), send_ref, recv_ref, counts_ref, nf, cap)
+    incs = [[(i0, 0), (d0, 0)], [(i1, 0), (d1, 0)], [(i2, 0), (e2, nf)], [(i3, 0), (e3, nf)]]
+    absorb(acc_ref, incs, kept(wcoup_ref), send_ref, recv_ref, counts_ref,
+           acc_ref.shape[1], cap)
     to_natural(acc_ref, sn_ref, blocks)
     z = zn_ref[0:nf, :]
-    q = qn_ref[0:nf, :]
+    q = qn_ref[...]
     w = wn_ref[...]
     r = r0_ref[...]
-    s = sn_ref[...]
+    s = sn_ref[0:nf, :]
 
     def inner(a, b):
         return jnp.sum(a * b, axis=1, keepdims=True)
@@ -343,30 +412,31 @@
     values = {
         16: gamma,
         17: base,
-        24: inner(r - centre * q, zc),
-        25: inner(q, zc),
-        26: inner(q, w),
-        27: inner(zc, kz),
-        28: inner(zc, s),
-        29: inner(w, s),
+        18: inner(r - centre * q, zc),
+        19: inner(q, zc),
+        20: inner(q, w),
+        21: inner(zc, kz),
+        22: inner(zc, s),
+        23: inner(w, s),
     }
     left_hi, left_lo = split(jnp.concatenate([z, w, zn_ref[nf:, :]], axis=0))
-    right_hi, right_lo = split(jnp.concatenate([cd_ref[...], qn_ref[nf:, :]], axis=0))
+    right_hi, right_lo = split(jnp.concatenate([cd_ref[...], sn_ref[nf:, :]], axis=0))
     left = jnp.concatenate([left_hi, left_lo], axis=0).astype(BF16)
     products = dot_nt(left, right_hi.astype(BF16)) + dot_nt(left, right_lo.astype(BF16))
     g_ref[...] = jnp.zeros_like(g_ref)
     g_ref[:, 0:16] = products[:24] + products[24:]
     lane = lane_of((nf, LANES))
-    pay = g_ref[0:8, :] + pltpu.roll(g_ref[8:16, :], 32, 1) + pltpu.roll(g_ref[16:24, :], 64, 1)
+    pay = g_ref[0:8, :] + pltpu.roll(g_ref[8:16, :], 32, 1) + pltpu.roll(g_ref[16:24, :], 48, 1)
     for at, value in values.items():
         pay = jnp.where(lane == at, value, pay)
-    pay = jnp.where((lane >= 56) & (lane < 62), centre, pay)
-    pay_ref[...] = jnp.broadcast_to(pay[None], pay_ref.shape)
+    pay = jnp.where((lane >= 24) & (lane < 30), centre, pay)
+    pay_ref[...] = jnp.broadcast_to(packed(pay)[None], pay_ref.shape)
 
 
 def last_kernel(nf, rho, all_ref, zn_ref, wn_ref, qn_ref, r0_ref, cd_ref, sn_ref, x_ref, res_ref):
     lane = lane_of((nf, LANES))
-    total = lax.fori_loop(0, all_ref.shape[0], lambda d, t: t + all_ref[d], jnp.zeros((nf, LANES), F32), unroll=16)
+    total = lax.fori_loop(0, all_ref.shape[0], lambda d, t: t + all_ref[d], jnp.zeros((nf // 2, LANES), F32), unroll=16)
+    total = jnp.concatenate([total, turn(total)], axis=0)
 
     def mat(a, b):
         out = None
@@ -379,23 +449,25 @@
     z_h = total[:, 8:16]
     cw = total[:, 32:40]
     w_h = total[:, 40:48]
-    b = total[:, 64:72]
-    d_h = total[:, 72:80]
+    b = total[:, 48:56]
+    d_h = total[:, 56:64]
     gamma0 = column_of(total, lane, 16)
     base = column_of(total, lane, 17) + rho * jnp.sum(t0 * t0, axis=1, keepdims=True)
     alpha0 = gamma0 / base
-    wide = jnp.broadcast_to(alpha0, (nf, LANES))
-    constant = (lane == 24) | (lane == 27)
-    linear = (lane == 25) | (lane == 28)
+    wide = packed(jnp.broadcast_to(alpha0, (nf, LANES)))
+    spot = lane_of((nf // 2, LANES)) % 64
+    constant = (spot == 18) | (spot == 21)
+    linear = (spot == 19) | (spot == 22)
 
     def about(d, carry):
         part = all_ref[d]
-        off = wide - pltpu.roll(part, LANES - 32, 1)
+        off = wide - pltpu.roll(part, LANES - 6, 1)
         return carry + part * jnp.where(constant, 1.0, jnp.where(linear, -2.0 * off, off * off))
 
-    sums = lax.fori_loop(0, all_ref.shape[0], about, jnp.zeros((nf, LANES), F32), unroll=16)
-    gamma1 = jnp.sum(jnp.where((lane >= 24) & (lane < 27), sums, 0.0), axis=1, keepdims=True)
-    delta = jnp.sum(jnp.where((lane >= 27) & (lane < 30), sums, 0.0), axis=1, keepdims=True)
+    sums = lax.fori_loop(0, all_ref.shape[0], about, jnp.zeros((nf // 2, LANES), F32), unroll=16)
+    sums = jnp.concatenate([sums, turn(sums)], axis=0)
+    gamma1 = jnp.sum(jnp.where((lane >= 18) & (lane < 21), sums, 0.0), axis=1, keepdims=True)
+    delta = jnp.sum(jnp.where((lane >= 21) & (lane < 24), sums, 0.0), axis=1, keepdims=True)
     t0b = mat(t0, b)
     t0d = mat(t0, d_h)
     tw = cw + rho * t0b
@@ -415,8 +487,8 @@
         at = pl.ds(pl.multiple_of(i * chunk, chunk), chunk)
         x_ref[:, at] = lead * zn_ref[0:nf, at] - both * wn_ref[:, at] + weighted_rows(on_d, zn_ref.at[nf:], at)
         res_ref[:, at] = (
-            r0_ref[:, at] - lead * qn_ref[0:nf, at] + both * sn_ref[:, at]
-            + (weighted_rows(on_c, cd_ref, at) - weighted_rows(on_d, qn_ref.at[nf:], at))
+            r0_ref[:, at] - lead * qn_ref[:, at] + both * sn_ref[0:nf, at]
+            + (weighted_rows(on_c, cd_ref, at) - weighted_rows(on_d, sn_ref.at[nf:], at))
         )
         return carry
 
@@ -444,19 +516,30 @@
         cost_estimate=pl.CostEstimate(flops=flops, transcendentals=0, bytes_accessed=8 << 20) if flops else None)
 
 
+def along_slabs(one, two):
+    slabs, sectors = lax.axis_size("slab"), lax.axis_size("sector")
+
+    def steps(way):
+        pairs = []
+        for s in range(slabs):
+            for e in range(sectors):
+                to = s + 1 if (e + way) % 2 == 0 else s - 1
+                target = (to, e) if 0 <= to < slabs else (s, e ^ 1)
+                pairs.append((s * sectors + e, target[0] * sectors + target[1]))
+        return pairs
+
+    return lax.ppermute(one, AXES, steps(0)), lax.ppermute(two, AXES, steps(1))
+
+
+def along_sectors(one, two):
+    count = lax.axis_size("sector")
+    up = [(i, (i + 1) % count) for i in range(count)]
+    down = [((i + 1) % count, i) for i in range(count)]
+    return lax.ppermute(one, "sector", up), lax.ppermute(two, "sector", down)
+
+
 def exchange(msgs):
-    slabs = lax.axis_size("slab")
-    sectors = lax.axis_size("sector")
-    up = [(i, (i + 1) % slabs) for i in range(slabs)]
-    down = [((i + 1) % slabs, i) for i in range(slabs)]
-    right = [(i, (i + 1) % sectors) for i in range(sectors)]
-    left = [((i + 1) % sectors, i) for i in range(sectors)]
-    return (
-        lax.ppermute(msgs[1], "slab", up),
-        lax.ppermute(msgs[0], "slab", down),
-        lax.ppermute(msgs[3], "sector", right),
-        lax.ppermute(msgs[2], "sector", left),
-    )
+    return along_slabs(msgs[0], msgs[1]) + along_sectors(msgs[2], msgs[3])
 
 
 def rows_of(x, group):
@@ -480,15 +563,16 @@
     send, recv, cols = in_hbm(send_list[0, 0]), in_hbm(recv_rows[0, 0]), in_hbm(columns[0, 0].T)
     counts, periods, src = in_hbm(counts), in_hbm(periods), in_hbm(src)
     edges, signs = in_hbm(cycle_edges[0, 0]), in_hbm(cycle_signs[0, 0])
-    msg = like(cap, both, LANES)
+    msg = like(cap, nf, LANES)
     *msgs, z, zn, r0, cd, y, winv, wcoup = call(
         functools.partial(first_kernel, both, blocks, cap),
         [VMEM] * 4 + [ANY] * 2 + [SMEM] * 3,
-        [msg] * 4 + [like(blocks, both, LANES), like(both, width), like(nf, width), like(cycles, width),
-                     like(blocks, 2 * both, LANES, dtype=BF16), like(blocks, LANES, LANES, dtype=BF16),
+        [msg] * 2 + [like(cap, both, LANES)] * 2 + [msg] * 2 + [like(blocks, both, LANES), like(both, width), like(nf, width), like(cycles, width),
+                     like(blocks, 2 * nf, LANES, dtype=BF16), like(blocks, LANES, LANES, dtype=BF16),
                      like(4 * cap, LANES, LANES, dtype=BF16)],
-        [pltpu.VMEM((blocks, both, LANES), F32), pltpu.VMEM((blocks, 2 * both, LANES), BF16), pltpu.VMEM(inv2.shape, F32),
-         pltpu.VMEM(coup2.shape, F32), pltpu.SemaphoreType.DMA((5,))],
+        [pltpu.VMEM((blocks, both, LANES), F32), pltpu.VMEM((blocks, 2 * both, LANES), BF16),
+         pltpu.VMEM((blocks, 2 * both, LANES), BF16), pltpu.VMEM(inv2.shape, F32), pltpu.VMEM(coup2.shape, F32),
+         pltpu.SemaphoreType.DMA((5,))],
         "first",
     )(src, periods, edges, signs, inv2, coup2, send, recv, counts)
 
@@ -505,25 +589,28 @@
             [SMEM, ANY if fresh else VMEM, VMEM, VMEM], out, scratch, "local", flops=2 * 10**9,
         )(cols, tiles2 if fresh else forms, vector, y)
 
+    incoming = exchange(msgs[:4])
+    acc, forms = local(z, y, nf, None)
+    acc, incoming, last = lax.optimization_barrier((acc, incoming, msgs[4:]))
+    later = along_slabs(*last) + incoming[2:]
+    *msgs, qn, wd, wn, y = call(
+        functools.partial(second_kernel, nf, blocks, cap),
+        [VMEM] * 8 + [SMEM] * 3,
+        [msg] * 4 + [like(nf, width), like(blocks, both, LANES), like(nf, width), like(blocks, 2 * both, LANES, dtype=BF16)],
+        [pltpu.VMEM((blocks, nf, LANES), F32), pltpu.VMEM((blocks, 2 * nf, LANES), BF16),
+         pltpu.VMEM((blocks, nf, LANES), F32), pltpu.VMEM((blocks, 2 * nf, LANES), BF16)],
+        "second",
+    )(acc, *incoming, z, winv, wcoup, send, recv, counts)
+    msgs, later = lax.optimization_barrier((msgs, later))
     incoming = exchange(msgs)
-    acc, forms = local(z, y, both, None)
-    msg = like(cap, nf, LANES)
-    *msgs, qn, w, wn, y = call(
-        functools.partial(second_kernel, nf, blocks, cap),
-        [VMEM] * 7 + [SMEM] * 3,
-        [msg] * 4 + [like(both, width), like(blocks, nf, LANES), like(nf, width), like(blocks, 2 * nf, LANES, dtype=BF16)],
-        [pltpu.VMEM((blocks, both, LANES), F32), pltpu.VMEM((blocks, 2 * nf, LANES), BF16)],
-        "second",
-    )(acc, *incoming, winv, wcoup, send, recv, counts)
-    incoming = exchange(msgs)
-    (acc,) = local(w, y, nf, forms)
+    (acc,) = local(wd, y, both, forms)
     sn, pay = call(
         functools.partial(third_kernel, nf, blocks, cap),
-        [VMEM] * 6 + [SMEM] * 3 + [VMEM] * 5,
-        [like(nf, width), like(devices, nf, LANES)],
-        [pltpu.VMEM((blocks, nf, LANES), F32), pltpu.VMEM((24, LANES), F32)],
+        [VMEM] * 10 + [SMEM] * 3 + [VMEM] * 5,
+        [like(both, width), like(devices, nf // 2, LANES)],
+        [pltpu.VMEM((blocks, both, LANES), F32), pltpu.VMEM((nf + both, LANES), F32)],
         "third",
-    )(acc, *incoming, wcoup, send, recv, counts, zn, qn, wn, r0, cd)
+    )(acc, *incoming, *later, wcoup, send, recv, counts, zn, qn, wn, r0, cd)
     everyone = lax.all_to_all(pay, AXES, 0, 0)
     out, res = call(
         functools.partial(last_kernel, nf, rho),

time: 57 us -> 52.2 us (0.916)
  Pallas kernels: 27.7 us -> 25.2 us
  starting transfers between devices: 14.4 us -> 12 us
  blocking collectives: 11.3 us -> 13.6 us
  waiting for transfers between devices: 2.67 us -> 0.52 us
    ppermute x8 -> x10, starting transfers between devices: 14.4 us -> 12 us  [the longest x3 7.72 us: along_slabs(): lax.ppermute(one, AXES, steps(0))]
    all_to_all x1, blocking collectives: 11.3 us -> 13.6 us  [on_device(): everyone = lax.all_to_all(pay, AXES, 0, 0)]
    pallas_call x2, Pallas kernels: 10.2 us -> 7.98 us  [the longest x1 4.61 us: on_device(): call(functools.partial(second_kernel, nf, blocks, cap), [VMEM] * 8 + [SME...]
    ppermute x8 -> x10, waiting for transfers between devices: 2.67 us -> 0.52 us  [the longest x3 0.34 us: along_slabs(): lax.ppermute(two, AXES, steps(1))]
  transfers between devices with their start and end apart: 8 -> 10, of which waited for: 2 -> 2; matrix products, arithmetic and copies ran while one was open for 0% -> 0% of each run, Pallas kernels for 17% -> 28%
where the time goes in v3:
time: 52.2 us; the launch traced here: 51.9 us
  Pallas kernels  25.2 us (48%)
  blocking collectives  13.6 us (26%)
  starting transfers between devices  12 us (23%)
  between operations  0.7 us (1%)
    all_to_all x1, blocking collectives, on_device(): everyone = lax.all_to_all(pay, AXES, 0, 0)  13.6 us
    pallas_call x2, Pallas kernels, local(): call(functools.partial(local_kernel, n, blocks, kt, fresh), [SMEM, ANY if...  9.71 us
    ppermute x3, starting transfers between devices, along_slabs(): lax.ppermute(one, AXES, steps(0))  7.72 us
    pallas_call x1, Pallas kernels, on_device(): call(functools.partial(first_kernel, both, blocks, cap), [VMEM] * 4 + [AN...  5.41 us
    pallas_call x1, Pallas kernels, on_device(): call(functools.partial(second_kernel, nf, blocks, cap), [VMEM] * 8 + [SME...  4.61 us
    ppermute x4, starting transfers between devices, along_sectors(): return (lax.ppermute(one, 'sector', up), lax.ppermute(two, 'sector', down))  4.23 us
    pallas_call x1, Pallas kernels, on_device(): call(functools.partial(third_kernel, nf, blocks, cap), [VMEM] * 10 + [SME...  3.37 us
    pallas_call x1, Pallas kernels, on_device(): call(functools.partial(last_kernel, nf, rho), [VMEM] * 7, [jax.ShapeDtype...  2.08 us
  transfers between devices with their start and end apart: 10, of which 2 were waited for; matrix products, arithmetic and copies ran while one was open for 0% of the time, Pallas kernels for 28%

profile of v3, /device:TPU:0, one launch (start us, length us, event | category | flops | bytes accessed | tf_op | source)
XLA Modules:
  0.0 51.9 jit_solution(14180136444826768172)
XLA Ops:
  0.6 5.4 %first.1 = (f32[32,8,128]{2,1,0:T(8,128)S(1)}, f32[32,8,128]{2,1,0:T(8,128)S(1)}, f32[32,16,128]{2,1,0:T(8,128)S(1)}, f32[32,16,128]{2,1,0:T(8,128)S(1)}, f32[32...) custom-call(f32[8,4096]{1,0:T(8,128)} %bitcast.27, ...), custom_call_target="tpu_custom_call" | custom-call | tf_op jit(solution)/shard_map/first/pallas_call | solution.py:567
  6.0 0.5 collective-permute-start.2
  6.5 2.0 %collective-permute-start.3 = (f32[32,16,128]{2,1,0:T(8,128)S(1)}, f32[32,16,128]{2,1,0:T(8,128)S(1)}, u32[]{:S(2)}, u32[]{:S(2)}) collective-permute-start(f32[32,16,128]{2,1,0:T(8,128)S(1)} %get-tuple-element.51), channel_id=1, source_target_pairs={{1,0},{2,1},{3,2},{0,3},{5,4},{6,5},{7,6},{4,7},{9,8},{10,9},{11,1... | collective-permute-start | bytes 786440 | tf_op jit(solution)/shard_map/ppermute | solution.py:538
  8.5 2.3 %collective-permute-start = (f32[32,8,128]{2,1,0:T(8,128)S(1)}, f32[32,8,128]{2,1,0:T(8,128)S(1)}, u32[]{:S(2)}, u32[]{:S(2)}) collective-permute-start(f32[32,8,128]{2,1,0:T(8,128)S(1)} %get-tuple-element.48), channel_id=1, source_target_pairs={{0,4},{1,0},{2,6},{3,2},{4,8},{5,1},{6,10},{7,3},{8,12},{9,5},{10,... | collective-permute-start | bytes 393224 | tf_op jit(solution)/shard_map/ppermute | solution.py:531
  10.8 0.0 collective-permute-start.1
  10.8 5.6 %local.2 = (f32[64,8,128]{2,1,0:T(8,128)S(1)}, bf16[64,128,256]{2,1,0:T(8,128)(2,1)S(1)}) custom-call(s32[4,64]{1,0:T(4,128)} %bitcast.39, f32[8192,128]{1,0:T(8,128)} %bitcast.36, f32[64,16,128]{2,1,0:T(8,128)S(1)} %get-tuple-element.44.z_ref, bf16[64,16,128]{2,1,0:T(8,128)(2,1)S(1)} %get-tuple-element.45.y_ref), custom_call_target="tpu_custom_call" | custom-call | flops 2000000000 | bytes 8388608 | tf_op jit(solution)/shard_map/local/pallas_call | solution.py:587
  16.5 0.2 collective-permute-done.i0
  16.6 0.0 collective-permute-done.1.i1
  16.6 0.0 collective-permute-done.2.i2.e2
  16.6 0.0 collective-permute-done.3.i3.e3
  16.6 2.5 %collective-permute-start.4 = (f32[32,8,128]{2,1,0:T(8,128)S(1)}, f32[32,8,128]{2,1,0:T(8,128)S(1)}, u32[]{:S(2)}, u32[]{:S(2)}) collective-permute-start(f32[32,8,128]{2,1,0:T(8,128)S(1)} %get-tuple-element.67), channel_id=1, source_target_pairs={{0,4},{1,0},{2,6},{3,2},{4,8},{5,1},{6,10},{7,3},{8,12},{9,5},{10,... | collective-permute-start | bytes 393224 | tf_op jit(solution)/shard_map/ppermute | solution.py:531
  19.2 0.0 collective-permute-start.5
  19.2 4.6 %second.1 = (f32[32,8,128]{2,1,0:T(8,128)S(1)}, f32[32,8,128]{2,1,0:T(8,128)S(1)}, f32[32,8,128]{2,1,0:T(8,128)S(1)}, f32[32,8,128]{2,1,0:T(8,128)S(1)}, f32[8,4...) custom-call(f32[64,8,128]{2,1,0:T(8,128)S(1)} %get-tuple-element.54.acc_i, ...), custom_call_target="tpu_custom_call" | custom-call | tf_op jit(solution)/shard_map/second/pallas_call | solution.py:596
  23.8 0.0 collective-permute-done.4.d0
  23.8 0.3 collective-permute-done.5.d1
  24.1 2.9 %collective-permute-start.6 = (f32[32,8,128]{2,1,0:T(8,128)S(1)}, f32[32,8,128]{2,1,0:T(8,128)S(1)}, u32[]{:S(2)}, u32[]{:S(2)}) collective-permute-start(f32[32,8,128]{2,1,0:T(8,128)S(1)} %get-tuple-element.69), channel_id=1, source_target_pairs={{0,4},{1,0},{2,6},{3,2},{4,8},{5,1},{6,10},{7,3},{8,12},{9,5},{10,... | collective-permute-start | bytes 393224 | tf_op jit(solution)/shard_map/ppermute | solution.py:531
  27.0 0.0 collective-permute-start.7
  27.0 0.0 collective-permute-start.8
  27.1 1.7 %collective-permute-start.9 = (f32[32,8,128]{2,1,0:T(8,128)S(1)}, f32[32,8,128]{2,1,0:T(8,128)S(1)}, u32[]{:S(2)}, u32[]{:S(2)}) collective-permute-start(f32[32,8,128]{2,1,0:T(8,128)S(1)} %get-tuple-element.72), channel_id=1, source_target_pairs={{1,0},{2,1},{3,2},{0,3},{5,4},{6,5},{7,6},{4,7},{9,8},{10,9},{11,1... | collective-permute-start | bytes 393224 | tf_op jit(solution)/shard_map/ppermute | solution.py:538
  28.8 4.1 %local.3.acc_in = f32[64,16,128]{2,1,0:T(8,128)S(1)} custom-call(s32[4,64]{1,0:T(4,128)} %bitcast.40, bf16[64,128,256]{2,1,0:T(8,128)(2,1)S(1)} %get-tuple-element.46.tiles_hbm, f32[64,16,128]{2,1,0:T(8,128)S(1)} %get-tuple-element.61.z_ref, bf16[64,32,128]{2,1,0:T(8,128)(2,1)S(1)} %get-tuple-element.62.y_ref), custom_call_target="tpu_custom_call" | custom-call | flops 2000000000 | bytes 8388608 | tf_op jit(solution)/shard_map/local/pallas_call | solution.py:587
  32.9 0.0 collective-permute-done.6.i0
  32.9 0.0 collective-permute-done.7.i1
  32.9 0.0 collective-permute-done.8.i2
  32.9 0.0 collective-permute-done.9.i3
  32.9 3.4 %third.1 = (f32[16,4096]{1,0:T(8,128)S(1)}, f32[32,4,128]{2,1,0:T(4,128)S(1)}) custom-call(f32[64,16,128]{2,1,0:T(8,128)S(1)} %local.3.acc_in, f32[32,8,128]{2,1,0:T(8,128)S(1)} %collective-permute-done.6.i0, f32[32,8,128]{2,1,0:T(8,128)S(1)} %collective-permute-done.7.i1, f32[32,8,128]{2,1,0:T(8,128)S(1)} %collective-permute-done.8.i2, ...), custom_call_target="tpu_custom_call" | custom-call | tf_op jit(solution)/shard_map/third/pallas_call | solution.py:607
  36.3 13.6 %all_to_all.5.all_ref = f32[32,4,128]{2,1,0:T(4,128)S(1)} all-to-all(f32[32,4,128]{2,1,0:T(4,128)S(1)} %get-tuple-element.82), channel_id=1, replica_groups=mesh['slab'=8,'sector'=4] {'slab','sector'}, dimensions={0} | all-to-all | bytes 131072 | tf_op jit(solution)/shard_map/all_to_all | solution.py:614
  49.9 2.1 %last.1 = (f32[8,4096]{1,0:T(8,128)}, f32[8,4096]{1,0:T(8,128)}) custom-call(f32[32,4,128]{2,1,0:T(4,128)S(1)} %all_to_all.5.all_ref, f32[16,4096]{1,0:T(8,128)S(1)} %get-tuple-element.77.zn_ref, f32[8,4096]{1,0:T(8,128)S(1)} %get-tuple-element.79.wn_ref, f32[8,4096]{1,0:T(8,128)S(1)} %get-tuple-element.78.qn_ref, f32[8,4096]{1,0:T(8,128)S(1)} %get-tuple-element.80.r0_ref, ...), custom_call_target="tpu_custom_call" | custom-call | tf_op jit(solution)/shard_map/last/pallas_call | solution.py:615
Async XLA Ops:
  6.0 10.6 %collective-permute-start.2 = (f32[32,16,128]{2,1,0:T(8,128)S(1)}, f32[32,16,128]{2,1,0:T(8,128)S(1)}, u32[]{:S(2)}, u32[]{:S(2)}) collective-permute-start(f32[32,16,128]{2,1,0:T(8,128)S(1)} %get-tuple-element.50), channel_id=1, source_target_pairs={{0,1},{1,2},{2,3},{3,0},{4,5},{5,6},{6,7},{7,4},{8,9},{9,10},{10,1... | collective-permute-start | bytes 786440 | tf_op jit(solution)/shard_map/ppermute | solution.py:538
  6.5 10.1 %collective-permute-start.3 = (f32[32,16,128]{2,1,0:T(8,128)S(1)}, f32[32,16,128]{2,1,0:T(8,128)S(1)}, u32[]{:S(2)}, u32[]{:S(2)}) collective-permute-start(f32[32,16,128]{2,1,0:T(8,128)S(1)} %get-tuple-element.51), channel_id=1, source_target_pairs={{1,0},{2,1},{3,2},{0,3},{5,4},{6,5},{7,6},{4,7},{9,8},{10,9},{11,1... | collective-permute-start | bytes 786440 | tf_op jit(solution)/shard_map/ppermute | solution.py:538
  8.5 8.1 %collective-permute-start = (f32[32,8,128]{2,1,0:T(8,128)S(1)}, f32[32,8,128]{2,1,0:T(8,128)S(1)}, u32[]{:S(2)}, u32[]{:S(2)}) collective-permute-start(f32[32,8,128]{2,1,0:T(8,128)S(1)} %get-tuple-element.48), channel_id=1, source_target_pairs={{0,4},{1,0},{2,6},{3,2},{4,8},{5,1},{6,10},{7,3},{8,12},{9,5},{10,... | collective-permute-start | bytes 393224 | tf_op jit(solution)/shard_map/ppermute | solution.py:531
  10.8 5.8 %collective-permute-start.1 = (f32[32,8,128]{2,1,0:T(8,128)S(1)}, f32[32,8,128]{2,1,0:T(8,128)S(1)}, u32[]{:S(2)}, u32[]{:S(2)}) collective-permute-start(f32[32,8,128]{2,1,0:T(8,128)S(1)} %get-tuple-element.49), channel_id=1, source_target_pairs={{0,1},{1,5},{2,3},{3,7},{4,0},{5,9},{6,2},{7,11},{8,4},{9,13},{10,... | collective-permute-start | bytes 393224 | tf_op jit(solution)/shard_map/ppermute | solution.py:531
  16.6 7.2 %collective-permute-start.4 = (f32[32,8,128]{2,1,0:T(8,128)S(1)}, f32[32,8,128]{2,1,0:T(8,128)S(1)}, u32[]{:S(2)}, u32[]{:S(2)}) collective-permute-start(f32[32,8,128]{2,1,0:T(8,128)S(1)} %get-tuple-element.67), channel_id=1, source_target_pairs={{0,4},{1,0},{2,6},{3,2},{4,8},{5,1},{6,10},{7,3},{8,12},{9,5},{10,... | collective-permute-start | bytes 393224 | tf_op jit(solution)/shard_map/ppermute | solution.py:531
  19.2 5.0 %collective-permute-start.5 = (f32[32,8,128]{2,1,0:T(8,128)S(1)}, f32[32,8,128]{2,1,0:T(8,128)S(1)}, u32[]{:S(2)}, u32[]{:S(2)}) collective-permute-start(f32[32,8,128]{2,1,0:T(8,128)S(1)} %get-tuple-element.68), channel_id=1, source_target_pairs={{0,1},{1,5},{2,3},{3,7},{4,0},{5,9},{6,2},{7,11},{8,4},{9,13},{10,... | collective-permute-start | bytes 393224 | tf_op jit(solution)/shard_map/ppermute | solution.py:531
  24.1 8.7 %collective-permute-start.6 = (f32[32,8,128]{2,1,0:T(8,128)S(1)}, f32[32,8,128]{2,1,0:T(8,128)S(1)}, u32[]{:S(2)}, u32[]{:S(2)}) collective-permute-start(f32[32,8,128]{2,1,0:T(8,128)S(1)} %get-tuple-element.69), channel_id=1, source_target_pairs={{0,4},{1,0},{2,6},{3,2},{4,8},{5,1},{6,10},{7,3},{8,12},{9,5},{10,... | collective-permute-start | bytes 393224 | tf_op jit(solution)/shard_map/ppermute | solution.py:531
  27.0 5.8 %collective-permute-start.7 = (f32[32,8,128]{2,1,0:T(8,128)S(1)}, f32[32,8,128]{2,1,0:T(8,128)S(1)}, u32[]{:S(2)}, u32[]{:S(2)}) collective-permute-start(f32[32,8,128]{2,1,0:T(8,128)S(1)} %get-tuple-element.70), channel_id=1, source_target_pairs={{0,1},{1,5},{2,3},{3,7},{4,0},{5,9},{6,2},{7,11},{8,4},{9,13},{10,... | collective-permute-start | bytes 393224 | tf_op jit(solution)/shard_map/ppermute | solution.py:531
  27.0 5.8 %collective-permute-start.8 = (f32[32,8,128]{2,1,0:T(8,128)S(1)}, f32[32,8,128]{2,1,0:T(8,128)S(1)}, u32[]{:S(2)}, u32[]{:S(2)}) collective-permute-start(f32[32,8,128]{2,1,0:T(8,128)S(1)} %get-tuple-element.71), channel_id=1, source_target_pairs={{0,1},{1,2},{2,3},{3,0},{4,5},{5,6},{6,7},{7,4},{8,9},{9,10},{10,1... | collective-permute-start | bytes 393224 | tf_op jit(solution)/shard_map/ppermute | solution.py:538
  27.1 5.8 %collective-permute-start.9 = (f32[32,8,128]{2,1,0:T(8,128)S(1)}, f32[32,8,128]{2,1,0:T(8,128)S(1)}, u32[]{:S(2)}, u32[]{:S(2)}) collective-permute-start(f32[32,8,128]{2,1,0:T(8,128)S(1)} %get-tuple-element.72), channel_id=1, source_target_pairs={{1,0},{2,1},{3,2},{0,3},{5,4},{6,5},{7,6},{4,7},{9,8},{10,9},{11,1... | collective-permute-start | bytes 393224 | tf_op jit(solution)/shard_map/ppermute | solution.py:538

commit v4 on v3

--- a/solution.py
+++ b/solution.py
@@ -12,8 +12,8 @@
 F32 = jnp.float32
 BF16 = jnp.bfloat16
 AXES = ("slab", "sector")
-ROWS_STEP = 32
-SMOOTH_STEP = 32
+ROWS_STEP = 64
+SMOOTH_STEP = 64
 SEND_STEP = 32
 ABSORB_STEP = 32
 LOCAL_STEP = 16
@@ -95,16 +95,12 @@
     return out[:nf] + out[nf:]
 
 
-def write_row_form(load, y_ref, nf, blocks, matrix, narrow_ref=None):
+def write_row_form(load, y_ref, nf, blocks, matrix):
     def body(i, carry):
         x = jnp.concatenate([stacked(load(i * ROWS_STEP + j)) for j in range(ROWS_STEP)], axis=0)
-        out = dot(x, matrix)
+        out = dot(x, matrix).astype(BF16)
         for j in range(ROWS_STEP):
-            o = out[j * 2 * nf : (j + 1) * 2 * nf]
-            y_ref[i * ROWS_STEP + j] = o.astype(BF16)
-            if narrow_ref is not None:
-                half = nf // 2
-                narrow_ref[i * ROWS_STEP + j] = jnp.concatenate([o[:half], o[nf : nf + half]], axis=0).astype(BF16)
+            y_ref[i * ROWS_STEP + j] = out[j * 2 * nf : (j + 1) * 2 * nf]
         return carry
 
     lax.fori_loop(0, blocks // ROWS_STEP, body, 0)
@@ -138,7 +134,7 @@
             ws = [tile(g * SMOOTH_STEP, c + i) for i in range(4)]
             at = g * SMOOTH_STEP + c
             for i, value in enumerate(turned_products([y_ref[at + i] for i in range(4)], ws, nf)):
-                out_ref[at + i] = value
+                out_ref[at + i, 0:nf] = value
         return carry
 
     lax.fori_loop(0, blocks // SMOOTH_STEP, body, 0)
@@ -177,6 +173,10 @@
         self.copies[i].wait()
 
 
+def lists(hbm, smem, sems):
+    return Copies(sems, list(zip(hbm, smem)))
+
+
 def quarters(hbm, vmem):
     rows = vmem.shape[0] // 4
     return [(hbm.at[pl.ds(d * rows, rows)], vmem.at[pl.ds(d * rows, rows)]) for d in range(4)]
@@ -190,17 +190,23 @@
     return out
 
 
-def first_kernel(nf, blocks, cap, src_ref, per_ref, edges_ref, signs_ref, inv_hbm, coup_hbm, send_ref, recv_ref, counts_ref,
-                 m0, m1, m2, m3, d0, d1, z_ref, zn_ref, r0_ref, cd_ref, narrow_ref, winv_ref, wcoup_ref,
-                 x_ref, y0_ref, y_ref, inv_ref, coup_ref, sems):
-    copies = Copies(sems, [(inv_hbm, inv_ref)] + quarters(coup_hbm, coup_ref))
+def first_kernel(nf, blocks, cap, src_hbm, per_hbm, edges_hbm, signs_hbm, inv_hbm, coup_hbm, send_hbm, recv_hbm,
+                 counts_hbm, m0, m1, m2, m3, d0, d1, z_ref, r0_ref, cd_ref, winv_ref, wcoup_ref,
+                 x_ref, y0_ref, y_ref, inv_ref, coup_ref, src_ref, per_ref, edges_ref, signs_ref, send_ref, recv_ref,
+                 counts_ref, sems):
+    small = [(edges_hbm, edges_ref), (signs_hbm, signs_ref), (per_hbm, per_ref), (src_hbm, src_ref), (send_hbm, send_ref),
+             (recv_hbm, recv_ref), (counts_hbm, counts_ref)]
+    large = [(inv_hbm, inv_ref)] + quarters(coup_hbm, coup_ref)
+    copies = Copies(sems, small + large)
+    for i in range(len(small)):
+        copies.wait(i)
     fields = src_ref.shape[0]
     width = src_ref.shape[1]
     count = edges_ref.shape[0]
     edges = edges_ref[...]
     orient = (2 * signs_ref[...] - 1).astype(F32)
     low = lane_of((fields, LANES)) < 64
-    step = 8 * LANES
+    step = 16 * LANES
     place = lane_of((count, step))
     totals = per_ref[...].T
 
@@ -224,41 +230,44 @@
         x_ref[2 * t + 1] = jnp.concatenate([jnp.where(low, rt, r), jnp.where(low, ct, c)], axis=0)
     matrix = into_rows()
     write_row_form(lambda b: x_ref[b], y0_ref, nf, blocks, matrix)
-    copies.wait(0)
+    copies.wait(len(small))
     smooth_into(made(inv_ref, winv_ref), y0_ref, z_ref, nf, blocks)
-    write_row_form(lambda b: z_ref[b], y_ref, nf, blocks, matrix, narrow_ref)
+    write_row_form(lambda b: z_ref[b], y_ref, nf, blocks, matrix)
 
 
     def ready(way):
         for part in ((0, 1), (), (3,), (2,))[way]:
-            copies.wait(1 + part)
+            copies.wait(len(small) + 1 + part)
 
     write_messages(lambda b: z_ref[b], y_ref, ready, made(coup_ref, wcoup_ref),
                    send_ref, recv_ref, counts_ref, ((m0, d0), (m1, d1), (m2,), (m3,)), nf, cap)
-    to_natural(z_ref, zn_ref, blocks)
-
-
-def local_kernel(nf, blocks, kt, fresh, cols_ref, tiles_hbm, z_ref, y_ref, acc_ref, *rest):
+
+
+def local_kernel(nf, blocks, kt, fresh, plain, cols_hbm, tiles_in, *rest):
+    vectors, rest = rest[:plain], rest[plain:]
+    z_ref = vectors[0]
+    acc_ref, rest = rest[0], rest[1:]
+    w_ref, rest = (rest[0], rest[1:]) if fresh else (tiles_in, rest)
+    naturals, (x_ref, y_ref, u_ref, t_ref, cols_ref, col_sem) = rest[:plain], rest[plain : plain + 6]
+    listed = lists([cols_hbm], [cols_ref], col_sem)
     if fresh:
-        w_ref, x_ref, u_ref, t_ref, tiles_ref, sems = rest
-    else:
-        x_ref, u_ref, t_ref = rest
-        w_ref = tiles_hbm
-    rows = LOCAL_STEP * kt * 32
-
-    def copy(i):
-        at = pl.ds(pl.multiple_of(i * rows, rows), rows)
-        return pltpu.make_async_copy(tiles_hbm.at[at], tiles_ref.at[at], sems.at[i])
-
-    if fresh:
+        tiles_ref, sems = rest[plain + 6 :]
+        rows = LOCAL_STEP * kt * 32
+
+        def copy(i):
+            at = pl.ds(pl.multiple_of(i * rows, rows), rows)
+            return pltpu.make_async_copy(tiles_in.at[at], tiles_ref.at[at], sems.at[i])
+
         for i in range(blocks // LOCAL_STEP):
             copy(i).start()
+    write_row_form(lambda b: z_ref[b, 0:nf], y_ref, nf, blocks, into_rows())
 
     def left(b, carry):
         x_ref[b] = stacked(z_ref[b, 0:nf])
         return carry
 
     lax.fori_loop(0, blocks, left, 0, unroll=8)
+    listed.wait(0)
     wide = lane_of((2 * nf, LANES)) < 64
 
     def body(i, carry):
@@ -304,6 +313,8 @@
         return carry
 
     lax.fori_loop(0, blocks // 32, finish, 0)
+    for vector, natural in zip(vectors, naturals):
+        to_natural(vector, natural, blocks)
 
 
 def odd_sector():
@@ -362,21 +373,21 @@
         lax.fori_loop(0, cap // ABSORB_STEP, body, 0)
 
 
-def second_kernel(nf, blocks, cap, acc_in, i0, i1, i2, i3, z_ref, winv_ref, wcoup_ref, send_ref, recv_ref, counts_ref,
-                  m0, m1, m2, m3, qn_ref, wd_ref, wn_ref, y_ref, acc_ref, y0_ref, w_ref, narrow_ref):
+def second_kernel(nf, blocks, cap, acc_in, i0, i1, i2, i3, z_ref, winv_ref, wcoup_ref, send_hbm, recv_hbm, counts_hbm,
+                  m0, m1, m2, m3, acc_ref, wd_ref, y0_ref, y_ref, send_ref, recv_ref, counts_ref, sems):
+    listed = lists([send_hbm, recv_hbm, counts_hbm], [send_ref, recv_ref, counts_ref], sems)
     acc_ref[...] = acc_in[...]
+    wd_ref[:, nf:] = z_ref[:, nf:]
+    for i in range(3):
+        listed.wait(i)
     coup = kept(wcoup_ref)
     absorb(acc_ref, [[(inc, 0)] for inc in (i0, i1, i2, i3)], coup, send_ref, recv_ref, counts_ref, nf, cap)
     matrix = into_rows()
     write_row_form(lambda b: acc_ref[b], y0_ref, nf, blocks, matrix)
-    smooth_into(kept(winv_ref), y0_ref, w_ref, nf, blocks)
-    for b in range(blocks):
-        wd_ref[b] = jnp.concatenate([w_ref[b], z_ref[b, nf:]], axis=0)
-    write_row_form(lambda b: wd_ref[b], y_ref, wd_ref.shape[1], blocks, matrix, narrow_ref)
-    write_messages(lambda b: w_ref[b], narrow_ref, lambda d: None, coup, send_ref, recv_ref, counts_ref,
+    smooth_into(kept(winv_ref), y0_ref, wd_ref, nf, blocks)
+    write_row_form(lambda b: wd_ref[b, 0:nf], y_ref, nf, blocks, matrix)
+    write_messages(lambda b: wd_ref[b, 0:nf], y_ref, lambda way: None, coup, send_ref, recv_ref, counts_ref,
                    ((m0,), (m1,), (m2,), (m3,)), nf, cap)
-    to_natural(acc_ref, qn_ref, blocks)
-    to_natural(w_ref, wn_ref, blocks)
 
 
 def column_of(values, lane, at):
@@ -481,7 +492,7 @@
     lead = alpha0 + alpha1 * (1.0 + beta)
     on_d = -(both * rho) * t0
     on_c = rho * (both * tw - lead * t0)
-    chunk = 8 * LANES
+    chunk = 32 * LANES
 
     def body(i, carry):
         at = pl.ds(pl.multiple_of(i * chunk, chunk), chunk)
@@ -564,46 +575,52 @@
     counts, periods, src = in_hbm(counts), in_hbm(periods), in_hbm(src)
     edges, signs = in_hbm(cycle_edges[0, 0]), in_hbm(cycle_signs[0, 0])
     msg = like(cap, nf, LANES)
-    *msgs, z, zn, r0, cd, y, winv, wcoup = call(
+    rows = pltpu.VMEM((blocks, 2 * nf, LANES), BF16)
+    tables = [pltpu.SMEM(send.shape, jnp.int32), pltpu.SMEM(recv.shape, jnp.int32), pltpu.SMEM(counts.shape, jnp.int32),
+              pltpu.SemaphoreType.DMA((3,))]
+    rows_both = pltpu.VMEM((blocks, 2 * both, LANES), BF16)
+    *msgs, z, r0, cd, winv, wcoup = call(
         functools.partial(first_kernel, both, blocks, cap),
-        [VMEM] * 4 + [ANY] * 2 + [SMEM] * 3,
-        [msg] * 2 + [like(cap, both, LANES)] * 2 + [msg] * 2 + [like(blocks, both, LANES), like(both, width), like(nf, width), like(cycles, width),
-                     like(blocks, 2 * nf, LANES, dtype=BF16), like(blocks, LANES, LANES, dtype=BF16),
-                     like(4 * cap, LANES, LANES, dtype=BF16)],
-        [pltpu.VMEM((blocks, both, LANES), F32), pltpu.VMEM((blocks, 2 * both, LANES), BF16),
-         pltpu.VMEM((blocks, 2 * both, LANES), BF16), pltpu.VMEM(inv2.shape, F32), pltpu.VMEM(coup2.shape, F32),
-         pltpu.SemaphoreType.DMA((5,))],
+        [ANY] * 9,
+        [msg] * 2 + [like(cap, both, LANES)] * 2 + [msg] * 2 + [
+            like(blocks, both, LANES), like(nf, width), like(cycles, width), like(blocks, LANES, LANES, dtype=BF16),
+            like(4 * cap, LANES, LANES, dtype=BF16)],
+        [pltpu.VMEM((blocks, both, LANES), F32), rows_both, rows_both, pltpu.VMEM(inv2.shape, F32),
+         pltpu.VMEM(coup2.shape, F32), pltpu.VMEM(src.shape, F32), pltpu.VMEM(periods.shape, F32),
+         pltpu.VMEM(edges.shape, jnp.int32), pltpu.VMEM(signs.shape, jnp.int32), pltpu.SMEM(send.shape, jnp.int32),
+         pltpu.SMEM(recv.shape, jnp.int32), pltpu.SMEM(counts.shape, jnp.int32), pltpu.SemaphoreType.DMA((12,))],
         "first",
     )(src, periods, edges, signs, inv2, coup2, send, recv, counts)
 
-    def local(vector, y, n, forms):
-        fresh = forms is None
+    def local(n, fresh, tiles, *vectors):
         out = [like(blocks, n, LANES)]
-        scratch = [pltpu.VMEM((blocks, 2 * n, LANES), BF16), pltpu.VMEM((blocks, 2 * n, LANES), BF16),
-                   pltpu.VMEM((blocks, n, kt // 2 * LANES), F32)]
         if fresh:
             out.append(like(blocks, LANES, kt // 2 * LANES, dtype=BF16))
-            scratch += [pltpu.VMEM(tiles2.shape, F32), pltpu.SemaphoreType.DMA((blocks // LOCAL_STEP,))]
+        out += [like(both, width)] if fresh else [like(nf, width)] * 2
+        form = pltpu.VMEM((blocks, 2 * n, LANES), BF16)
+        scratch = [form, form, form, pltpu.VMEM((blocks, n, kt // 2 * LANES), F32), pltpu.SMEM(cols.shape, jnp.int32),
+                   pltpu.SemaphoreType.DMA((1,))]
+        if fresh:
+            scratch += [pltpu.VMEM(tiles.shape, F32), pltpu.SemaphoreType.DMA((blocks // LOCAL_STEP,))]
         return call(
-            functools.partial(local_kernel, n, blocks, kt, fresh),
-            [SMEM, ANY if fresh else VMEM, VMEM, VMEM], out, scratch, "local", flops=2 * 10**9,
-        )(cols, tiles2 if fresh else forms, vector, y)
+            functools.partial(local_kernel, n, blocks, kt, fresh, len(vectors)),
+            [ANY, ANY if fresh else VMEM] + [VMEM] * len(vectors), out, scratch, "local", flops=2 * 10**9,
+        )(cols, tiles, *vectors)
 
     incoming = exchange(msgs[:4])
-    acc, forms = local(z, y, nf, None)
+    acc, forms, zn = local(nf, True, tiles2, z)
     acc, incoming, last = lax.optimization_barrier((acc, incoming, msgs[4:]))
     later = along_slabs(*last) + incoming[2:]
-    *msgs, qn, wd, wn, y = call(
+    *msgs, q, wd = call(
         functools.partial(second_kernel, nf, blocks, cap),
-        [VMEM] * 8 + [SMEM] * 3,
-        [msg] * 4 + [like(nf, width), like(blocks, both, LANES), like(nf, width), like(blocks, 2 * both, LANES, dtype=BF16)],
-        [pltpu.VMEM((blocks, nf, LANES), F32), pltpu.VMEM((blocks, 2 * nf, LANES), BF16),
-         pltpu.VMEM((blocks, nf, LANES), F32), pltpu.VMEM((blocks, 2 * nf, LANES), BF16)],
+        [VMEM] * 8 + [ANY] * 3,
+        [msg] * 4 + [like(blocks, nf, LANES), like(blocks, both, LANES)],
+        [rows, rows] + tables,
         "second",
     )(acc, *incoming, z, winv, wcoup, send, recv, counts)
     msgs, later = lax.optimization_barrier((msgs, later))
     incoming = exchange(msgs)
-    (acc,) = local(wd, y, both, forms)
+    acc, wn, qn = local(both, False, forms, wd, q)
     sn, pay = call(
         functools.partial(third_kernel, nf, blocks, cap),
         [VMEM] * 10 + [SMEM] * 3 + [VMEM] * 5,

time: 52.2 us -> 50.9 us (0.975)
  Pallas kernels: 25.2 us -> 23.2 us
  waiting for transfers between devices: 0.52 us -> 1.68 us
    pallas_call x4, Pallas kernels: 19.7 us -> 18 us  [the longest x2 9 us: local(): call(functools.partial(local_kernel, n, blocks, kt, fresh, len(vectors)),...]
    ppermute x3, waiting for transfers between devices: 0.17 us -> 0.85 us  [along_slabs(): lax.ppermute(one, AXES, steps(0))]
  transfers between devices with their start and end apart: 10 -> 10, of which waited for: 2 -> 2; matrix products, arithmetic and copies ran while one was open for 0% -> 0% of each run, Pallas kernels for 28% -> 26%
where the time goes in v4:
time: 50.9 us; the launch traced here: 50.7 us
  Pallas kernels  23.2 us (46%)
  blocking collectives  13.2 us (26%)
  starting transfers between devices  11.8 us (23%)
  waiting for transfers between devices  1.68 us (3%)
  between operations  0.72 us (1%)
    all_to_all x1, blocking collectives, on_device(): everyone = lax.all_to_all(pay, AXES, 0, 0)  13.2 us
    pallas_call x2, Pallas kernels, local(): call(functools.partial(local_kernel, n, blocks, kt, fresh, len(vectors)),...  9 us
    ppermute x3, starting transfers between devices, along_slabs(): lax.ppermute(one, AXES, steps(0))  7.54 us
    pallas_call x1, Pallas kernels, on_device(): call(functools.partial(first_kernel, both, blocks, cap), [ANY] * 9, [msg]...  4.86 us
    ppermute x4, starting transfers between devices, along_sectors(): return (lax.ppermute(one, 'sector', up), lax.ppermute(two, 'sector', down))  4.24 us
    pallas_call x1, Pallas kernels, on_device(): call(functools.partial(second_kernel, nf, blocks, cap), [VMEM] * 8 + [ANY...  4.13 us
    pallas_call x1, Pallas kernels, on_device(): call(functools.partial(third_kernel, nf, blocks, cap), [VMEM] * 10 + [SME...  3.37 us
    pallas_call x1, Pallas kernels, on_device(): call(functools.partial(last_kernel, nf, rho), [VMEM] * 7, [jax.ShapeDtype...  1.87 us
  transfers between devices with their start and end apart: 10, of which 2 were waited for; matrix products, arithmetic and copies ran while one was open for 0% of the time, Pallas kernels for 26%

profile of v4, /device:TPU:0, one launch (start us, length us, event | category | flops | bytes accessed | tf_op | source)
XLA Modules:
  0.0 50.7 jit_solution(1150359280182687099)
XLA Ops:
  0.6 4.9 %first.1 = (f32[32,8,128]{2,1,0:T(8,128)S(1)}, f32[32,8,128]{2,1,0:T(8,128)S(1)}, f32[32,16,128]{2,1,0:T(8,128)S(1)}, f32[32,16,128]{2,1,0:T(8,128)S(1)}, f32[32...) custom-call(f32[8,4096]{1,0:T(8,128)} %bitcast.27, ...), custom_call_target="tpu_custom_call" | custom-call | tf_op jit(solution)/shard_map/first/pallas_call | solution.py:582
  5.5 0.5 collective-permute-start.2
  6.0 2.0 %collective-permute-start.3 = (f32[32,16,128]{2,1,0:T(8,128)S(1)}, f32[32,16,128]{2,1,0:T(8,128)S(1)}, u32[]{:S(2)}, u32[]{:S(2)}) collective-permute-start(f32[32,16,128]{2,1,0:T(8,128)S(1)} %get-tuple-element.50), channel_id=1, source_target_pairs={{1,0},{2,1},{3,2},{0,3},{5,4},{6,5},{7,6},{4,7},{9,8},{10,9},{11,1... | collective-permute-start | bytes 786440 | tf_op jit(solution)/shard_map/ppermute | solution.py:549
  8.0 2.3 %collective-permute-start = (f32[32,8,128]{2,1,0:T(8,128)S(1)}, f32[32,8,128]{2,1,0:T(8,128)S(1)}, u32[]{:S(2)}, u32[]{:S(2)}) collective-permute-start(f32[32,8,128]{2,1,0:T(8,128)S(1)} %get-tuple-element.47), channel_id=1, source_target_pairs={{0,4},{1,0},{2,6},{3,2},{4,8},{5,1},{6,10},{7,3},{8,12},{9,5},{10,... | collective-permute-start | bytes 393224 | tf_op jit(solution)/shard_map/ppermute | solution.py:542
  10.3 0.0 collective-permute-start.1
  10.3 5.0 %local.2 = (f32[64,8,128]{2,1,0:T(8,128)S(1)}, bf16[64,128,256]{2,1,0:T(8,128)(2,1)S(1)}, f32[16,4096]{1,0:T(8,128)S(1)}) custom-call(s32[4,64]{1,0:T(4,128)} %bitcast.39, f32[8192,128]{1,0:T(8,128)} %bitcast.36, f32[64,16,128]{2,1,0:T(8,128)S(1)} %get-tuple-element.44.rest_0_.z_ref), custom_call_target="tpu_custom_call" | custom-call | flops 2000000000 | bytes 8388608 | tf_op jit(solution)/shard_map/local/pallas_call | solution.py:605
  15.2 0.8 %collective-permute-done.i0 = f32[32,8,128]{2,1,0:T(8,128)S(1)} collective-permute-done((f32[32,8,128]{2,1,0:T(8,128)S(1)}, f32[32,8,128]{2,1,0:T(8,128)S(1)}, u32[]{:S(2)}, u32[]{:S(2)}) %collective-permute-start) | collective-permute-done | bytes 131104 | tf_op jit(solution)/shard_map/ppermute | solution.py:542
  16.1 0.0 collective-permute-done.1.i1
  16.1 0.0 collective-permute-done.2.i2.e2
  16.1 0.0 collective-permute-done.3.i3.e3
  16.1 2.5 %collective-permute-start.4 = (f32[32,8,128]{2,1,0:T(8,128)S(1)}, f32[32,8,128]{2,1,0:T(8,128)S(1)}, u32[]{:S(2)}, u32[]{:S(2)}) collective-permute-start(f32[32,8,128]{2,1,0:T(8,128)S(1)} %get-tuple-element.67), channel_id=1, source_target_pairs={{0,4},{1,0},{2,6},{3,2},{4,8},{5,1},{6,10},{7,3},{8,12},{9,5},{10,... | collective-permute-start | bytes 393224 | tf_op jit(solution)/shard_map/ppermute | solution.py:542
  18.6 0.0 collective-permute-start.5
  18.6 4.1 %second.1 = (f32[32,8,128]{2,1,0:T(8,128)S(1)}, f32[32,8,128]{2,1,0:T(8,128)S(1)}, f32[32,8,128]{2,1,0:T(8,128)S(1)}, f32[32,8,128]{2,1,0:T(8,128)S(1)}, f32[64,...) custom-call(f32[64,8,128]{2,1,0:T(8,128)S(1)} %get-tuple-element.53.acc_in, f32[32,8,128]{2,1,0:T(8,128)S(1)} %collective-permute-done.i0, ...), custom_call_target="tpu_custom_call" | custom-call | tf_op jit(solution)/shard_map/second/pallas_call | solution.py:614
  22.8 0.0 collective-permute-done.4.d0
  22.8 0.8 %collective-permute-done.5.d1 = f32[32,8,128]{2,1,0:T(8,128)S(1)} collective-permute-done((f32[32,8,128]{2,1,0:T(8,128)S(1)}, f32[32,8,128]{2,1,0:T(8,128)S(1)}, u32[]{:S(2)}, u32[]{:S(2)}) %collective-permute-start.5) | collective-permute-done | bytes 131104 | tf_op jit(solution)/shard_map/ppermute | solution.py:542
  23.6 2.7 %collective-permute-start.6 = (f32[32,8,128]{2,1,0:T(8,128)S(1)}, f32[32,8,128]{2,1,0:T(8,128)S(1)}, u32[]{:S(2)}, u32[]{:S(2)}) collective-permute-start(f32[32,8,128]{2,1,0:T(8,128)S(1)} %get-tuple-element.69), channel_id=1, source_target_pairs={{0,4},{1,0},{2,6},{3,2},{4,8},{5,1},{6,10},{7,3},{8,12},{9,5},{10,... | collective-permute-start | bytes 393224 | tf_op jit(solution)/shard_map/ppermute | solution.py:542
  26.3 0.0 collective-permute-start.7
  26.3 0.0 collective-permute-start.8
  26.3 1.7 %collective-permute-start.9 = (f32[32,8,128]{2,1,0:T(8,128)S(1)}, f32[32,8,128]{2,1,0:T(8,128)S(1)}, u32[]{:S(2)}, u32[]{:S(2)}) collective-permute-start(f32[32,8,128]{2,1,0:T(8,128)S(1)} %get-tuple-element.72), channel_id=1, source_target_pairs={{1,0},{2,1},{3,2},{0,3},{5,4},{6,5},{7,6},{4,7},{9,8},{10,9},{11,1... | collective-permute-start | bytes 393224 | tf_op jit(solution)/shard_map/ppermute | solution.py:549
  28.1 4.0 %local.3 = (f32[64,16,128]{2,1,0:T(8,128)S(1)}, f32[8,4096]{1,0:T(8,128)S(1)}, f32[8,4096]{1,0:T(8,128)S(1)}) custom-call(s32[4,64]{1,0:T(4,128)} %bitcast.40, bf16[64,128,256]{2,1,0:T(8,128)(2,1)S(1)} %get-tuple-element.45.tiles_in, f32[64,16,128]{2,1,0:T(8,128)S(1)} %get-tuple-element.60.rest_0_, f32[64,8,128]{2,1,0:T(8,128)S(1)} %get-tuple-element.61.rest_1_), custom_call_target="tpu_custom_call" | custom-call | flops 2000000000 | bytes 8388608 | tf_op jit(solution)/shard_map/local/pallas_call | solution.py:605
  32.1 0.0 collective-permute-done.6.i0
  32.1 0.0 collective-permute-done.7.i1
  32.2 0.0 collective-permute-done.8.i2
  32.2 0.0 collective-permute-done.9.i3
  32.2 3.4 %third.1 = (f32[16,4096]{1,0:T(8,128)S(1)}, f32[32,4,128]{2,1,0:T(4,128)S(1)}) custom-call(f32[64,16,128]{2,1,0:T(8,128)S(1)} %get-tuple-element.62.acc_in, f32[32,8,128]{2,1,0:T(8,128)S(1)} %collective-permute-done.6.i0, f32[32,8,128]{2,1,0:T(8,128)S(1)} %collective-permute-done.7.i1, f32[32,8,128]{2,1,0:T(8,128)S(1)} %collective-permute-done.8.i2, ...), custom_call_target="tpu_custom_call" | custom-call | tf_op jit(solution)/shard_map/third/pallas_call | solution.py:624
  35.6 13.2 %all_to_all.5.all_ref = f32[32,4,128]{2,1,0:T(4,128)S(1)} all-to-all(f32[32,4,128]{2,1,0:T(4,128)S(1)} %get-tuple-element.82), channel_id=1, replica_groups=mesh['slab'=8,'sector'=4] {'slab','sector'}, dimensions={0} | all-to-all | bytes 131072 | tf_op jit(solution)/shard_map/all_to_all | solution.py:631
  48.8 1.9 %last.1 = (f32[8,4096]{1,0:T(8,128)}, f32[8,4096]{1,0:T(8,128)}) custom-call(f32[32,4,128]{2,1,0:T(4,128)S(1)} %all_to_all.5.all_ref, f32[16,4096]{1,0:T(8,128)S(1)} %get-tuple-element.77.zn_ref, f32[8,4096]{1,0:T(8,128)S(1)} %get-tuple-element.79.wn_ref, f32[8,4096]{1,0:T(8,128)S(1)} %get-tuple-element.78.qn_ref, f32[8,4096]{1,0:T(8,128)S(1)} %get-tuple-element.80.r0_ref, ...), custom_call_target="tpu_custom_call" | custom-call | tf_op jit(solution)/shard_map/last/pallas_call | solution.py:632
Async XLA Ops:
  5.5 10.6 %collective-permute-start.2 = (f32[32,16,128]{2,1,0:T(8,128)S(1)}, f32[32,16,128]{2,1,0:T(8,128)S(1)}, u32[]{:S(2)}, u32[]{:S(2)}) collective-permute-start(f32[32,16,128]{2,1,0:T(8,128)S(1)} %get-tuple-element.49), channel_id=1, source_target_pairs={{0,1},{1,2},{2,3},{3,0},{4,5},{5,6},{6,7},{7,4},{8,9},{9,10},{10,1... | collective-permute-start | bytes 786440 | tf_op jit(solution)/shard_map/ppermute | solution.py:549
  6.0 10.1 %collective-permute-start.3 = (f32[32,16,128]{2,1,0:T(8,128)S(1)}, f32[32,16,128]{2,1,0:T(8,128)S(1)}, u32[]{:S(2)}, u32[]{:S(2)}) collective-permute-start(f32[32,16,128]{2,1,0:T(8,128)S(1)} %get-tuple-element.50), channel_id=1, source_target_pairs={{1,0},{2,1},{3,2},{0,3},{5,4},{6,5},{7,6},{4,7},{9,8},{10,9},{11,1... | collective-permute-start | bytes 786440 | tf_op jit(solution)/shard_map/ppermute | solution.py:549
  8.0 8.1 %collective-permute-start = (f32[32,8,128]{2,1,0:T(8,128)S(1)}, f32[32,8,128]{2,1,0:T(8,128)S(1)}, u32[]{:S(2)}, u32[]{:S(2)}) collective-permute-start(f32[32,8,128]{2,1,0:T(8,128)S(1)} %get-tuple-element.47), channel_id=1, source_target_pairs={{0,4},{1,0},{2,6},{3,2},{4,8},{5,1},{6,10},{7,3},{8,12},{9,5},{10,... | collective-permute-start | bytes 393224 | tf_op jit(solution)/shard_map/ppermute | solution.py:542
  10.3 5.8 %collective-permute-start.1 = (f32[32,8,128]{2,1,0:T(8,128)S(1)}, f32[32,8,128]{2,1,0:T(8,128)S(1)}, u32[]{:S(2)}, u32[]{:S(2)}) collective-permute-start(f32[32,8,128]{2,1,0:T(8,128)S(1)} %get-tuple-element.48), channel_id=1, source_target_pairs={{0,1},{1,5},{2,3},{3,7},{4,0},{5,9},{6,2},{7,11},{8,4},{9,13},{10,... | collective-permute-start | bytes 393224 | tf_op jit(solution)/shard_map/ppermute | solution.py:542
  16.1 6.7 %collective-permute-start.4 = (f32[32,8,128]{2,1,0:T(8,128)S(1)}, f32[32,8,128]{2,1,0:T(8,128)S(1)}, u32[]{:S(2)}, u32[]{:S(2)}) collective-permute-start(f32[32,8,128]{2,1,0:T(8,128)S(1)} %get-tuple-element.67), channel_id=1, source_target_pairs={{0,4},{1,0},{2,6},{3,2},{4,8},{5,1},{6,10},{7,3},{8,12},{9,5},{10,... | collective-permute-start | bytes 393224 | tf_op jit(solution)/shard_map/ppermute | solution.py:542
  18.6 5.0 %collective-permute-start.5 = (f32[32,8,128]{2,1,0:T(8,128)S(1)}, f32[32,8,128]{2,1,0:T(8,128)S(1)}, u32[]{:S(2)}, u32[]{:S(2)}) collective-permute-start(f32[32,8,128]{2,1,0:T(8,128)S(1)} %get-tuple-element.68), channel_id=1, source_target_pairs={{0,1},{1,5},{2,3},{3,7},{4,0},{5,9},{6,2},{7,11},{8,4},{9,13},{10,... | collective-permute-start | bytes 393224 | tf_op jit(solution)/shard_map/ppermute | solution.py:542
  23.6 8.5 %collective-permute-start.6 = (f32[32,8,128]{2,1,0:T(8,128)S(1)}, f32[32,8,128]{2,1,0:T(8,128)S(1)}, u32[]{:S(2)}, u32[]{:S(2)}) collective-permute-start(f32[32,8,128]{2,1,0:T(8,128)S(1)} %get-tuple-element.69), channel_id=1, source_target_pairs={{0,4},{1,0},{2,6},{3,2},{4,8},{5,1},{6,10},{7,3},{8,12},{9,5},{10,... | collective-permute-start | bytes 393224 | tf_op jit(solution)/shard_map/ppermute | solution.py:542
  26.3 5.8 %collective-permute-start.7 = (f32[32,8,128]{2,1,0:T(8,128)S(1)}, f32[32,8,128]{2,1,0:T(8,128)S(1)}, u32[]{:S(2)}, u32[]{:S(2)}) collective-permute-start(f32[32,8,128]{2,1,0:T(8,128)S(1)} %get-tuple-element.70), channel_id=1, source_target_pairs={{0,1},{1,5},{2,3},{3,7},{4,0},{5,9},{6,2},{7,11},{8,4},{9,13},{10,... | collective-permute-start | bytes 393224 | tf_op jit(solution)/shard_map/ppermute | solution.py:542
  26.3 5.8 %collective-permute-start.8 = (f32[32,8,128]{2,1,0:T(8,128)S(1)}, f32[32,8,128]{2,1,0:T(8,128)S(1)}, u32[]{:S(2)}, u32[]{:S(2)}) collective-permute-start(f32[32,8,128]{2,1,0:T(8,128)S(1)} %get-tuple-element.71), channel_id=1, source_target_pairs={{0,1},{1,2},{2,3},{3,0},{4,5},{5,6},{6,7},{7,4},{8,9},{9,10},{10,1... | collective-permute-start | bytes 393224 | tf_op jit(solution)/shard_map/ppermute | solution.py:549
  26.3 5.8 %collective-permute-start.9 = (f32[32,8,128]{2,1,0:T(8,128)S(1)}, f32[32,8,128]{2,1,0:T(8,128)S(1)}, u32[]{:S(2)}, u32[]{:S(2)}) collective-permute-start(f32[32,8,128]{2,1,0:T(8,128)S(1)} %get-tuple-element.72), channel_id=1, source_target_pairs={{1,0},{2,1},{3,2},{0,3},{5,4},{6,5},{7,6},{4,7},{9,8},{10,9},{11,1... | collective-permute-start | bytes 393224 | tf_op jit(solution)/shard_map/ppermute | solution.py:549

commit v5 on v4

--- a/solution.py
+++ b/solution.py
@@ -206,7 +206,7 @@
     edges = edges_ref[...]
     orient = (2 * signs_ref[...] - 1).astype(F32)
     low = lane_of((fields, LANES)) < 64
-    step = 16 * LANES
+    step = 32 * LANES
     place = lane_of((count, step))
     totals = per_ref[...].T
 
@@ -446,7 +446,7 @@
 
 def last_kernel(nf, rho, all_ref, zn_ref, wn_ref, qn_ref, r0_ref, cd_ref, sn_ref, x_ref, res_ref):
     lane = lane_of((nf, LANES))
-    total = lax.fori_loop(0, all_ref.shape[0], lambda d, t: t + all_ref[d], jnp.zeros((nf // 2, LANES), F32), unroll=16)
+    total = lax.fori_loop(0, all_ref.shape[0], lambda d, t: t + all_ref[d], jnp.zeros((nf // 2, LANES), F32), unroll=32)
     total = jnp.concatenate([total, turn(total)], axis=0)
 
     def mat(a, b):
@@ -475,7 +475,7 @@
         off = wide - pltpu.roll(part, LANES - 6, 1)
         return carry + part * jnp.where(constant, 1.0, jnp.where(linear, -2.0 * off, off * off))
 
-    sums = lax.fori_loop(0, all_ref.shape[0], about, jnp.zeros((nf // 2, LANES), F32), unroll=16)
+    sums = lax.fori_loop(0, all_ref.shape[0], about, jnp.zeros((nf // 2, LANES), F32), unroll=32)
     sums = jnp.concatenate([sums, turn(sums)], axis=0)
     gamma1 = jnp.sum(jnp.where((lane >= 18) & (lane < 21), sums, 0.0), axis=1, keepdims=True)
     delta = jnp.sum(jnp.where((lane >= 21) & (lane < 24), sums, 0.0), axis=1, keepdims=True)
@@ -527,7 +527,7 @@
         cost_estimate=pl.CostEstimate(flops=flops, transcendentals=0, bytes_accessed=8 << 20) if flops else None)
 
 
-def along_slabs(one, two):
+def along_slabs(*blocks):
     slabs, sectors = lax.axis_size("slab"), lax.axis_size("sector")
 
     def steps(way):
@@ -539,7 +539,7 @@
                 pairs.append((s * sectors + e, target[0] * sectors + target[1]))
         return pairs
 
-    return lax.ppermute(one, AXES, steps(0)), lax.ppermute(two, AXES, steps(1))
+    return tuple(lax.ppermute(block, AXES, steps(way)) for way, block in enumerate(blocks) if block is not None)
 
 
 def along_sectors(one, two):
@@ -608,9 +608,10 @@
         )(cols, tiles, *vectors)
 
     incoming = exchange(msgs[:4])
+    early = along_slabs(None, msgs[5])
     acc, forms, zn = local(nf, True, tiles2, z)
-    acc, incoming, last = lax.optimization_barrier((acc, incoming, msgs[4:]))
-    later = along_slabs(*last) + incoming[2:]
+    acc, incoming, last = lax.optimization_barrier((acc, incoming, msgs[4]))
+    later = along_slabs(last, None) + early + incoming[2:]
     *msgs, q, wd = call(
         functools.partial(second_kernel, nf, blocks, cap),
         [VMEM] * 8 + [ANY] * 3,

time: 50.9 us -> 49.9 us (0.980)
  starting transfers between devices: 11.8 us -> 10.2 us
  waiting for transfers between devices: 1.68 us -> 3.02 us
    ppermute x6, starting transfers between devices: 7.54 us -> 5.95 us  [along_slabs(): lax.ppermute(block, AXES, steps(way))]
    ppermute x6, waiting for transfers between devices: 1.67 us -> 3.01 us  [along_slabs(): lax.ppermute(block, AXES, steps(way))]
    all_to_all x1, blocking collectives: 13.2 us -> 12.7 us  [on_device(): everyone = lax.all_to_all(pay, AXES, 0, 0)]
  transfers between devices with their start and end apart: 10 -> 10, of which waited for: 2 -> 1; matrix products, arithmetic and copies ran while one was open for 0% -> 0% of each run, Pallas kernels for 26% -> 26%
where the time goes in v5:
time: 49.9 us; the launch traced here: 49.6 us
  Pallas kernels  22.9 us (46%)
  blocking collectives  12.7 us (25%)
  starting transfers between devices  10.2 us (20%)
  waiting for transfers between devices  3.02 us (6%)
  between operations  0.73 us (1%)
    all_to_all x1, blocking collectives, on_device(): everyone = lax.all_to_all(pay, AXES, 0, 0)  12.7 us
    pallas_call x2, Pallas kernels, local(): call(functools.partial(local_kernel, n, blocks, kt, fresh, len(vectors)),...  9 us
    ppermute x6, starting transfers between devices, along_slabs(): lax.ppermute(block, AXES, steps(way))  5.95 us
    pallas_call x1, Pallas kernels, on_device(): call(functools.partial(first_kernel, both, blocks, cap), [ANY] * 9, [msg]...  4.79 us
    ppermute x4, starting transfers between devices, along_sectors(): return (lax.ppermute(one, 'sector', up), lax.ppermute(two, 'sector', down))  4.24 us
    pallas_call x1, Pallas kernels, on_device(): call(functools.partial(second_kernel, nf, blocks, cap), [VMEM] * 8 + [ANY...  4.13 us
    pallas_call x1, Pallas kernels, on_device(): call(functools.partial(third_kernel, nf, blocks, cap), [VMEM] * 10 + [SME...  3.37 us
    ppermute x6, waiting for transfers between devices, along_slabs(): lax.ppermute(block, AXES, steps(way))  3.01 us
  transfers between devices with their start and end apart: 10, of which 1 were waited for; matrix products, arithmetic and copies ran while one was open for 0% of the time, Pallas kernels for 26%

profile of v5, /device:TPU:0, one launch (start us, length us, event | category | flops | bytes accessed | tf_op | source)
XLA Modules:
  0.0 49.6 jit_solution(6074753688269567962)
XLA Ops:
  0.6 4.8 %first.1 = (f32[32,8,128]{2,1,0:T(8,128)S(1)}, f32[32,8,128]{2,1,0:T(8,128)S(1)}, f32[32,16,128]{2,1,0:T(8,128)S(1)}, f32[32,16,128]{2,1,0:T(8,128)S(1)}, f32[32...) custom-call(f32[8,4096]{1,0:T(8,128)} %bitcast.27, ...), custom_call_target="tpu_custom_call" | custom-call | tf_op jit(solution)/shard_map/first/pallas_call | solution.py:582
  5.4 0.5 %collective-permute-start.2 = (f32[32,16,128]{2,1,0:T(8,128)S(1)}, f32[32,16,128]{2,1,0:T(8,128)S(1)}, u32[]{:S(2)}, u32[]{:S(2)}) collective-permute-start(f32[32,16,128]{2,1,0:T(8,128)S(1)} %get-tuple-element.48), channel_id=1, source_target_pairs={{0,1},{1,2},{2,3},{3,0},{4,5},{5,6},{6,7},{7,4},{8,9},{9,10},{10,1... | collective-permute-start | bytes 786440 | tf_op jit(solution)/shard_map/ppermute | solution.py:549
  5.9 2.0 %collective-permute-start.3 = (f32[32,16,128]{2,1,0:T(8,128)S(1)}, f32[32,16,128]{2,1,0:T(8,128)S(1)}, u32[]{:S(2)}, u32[]{:S(2)}) collective-permute-start(f32[32,16,128]{2,1,0:T(8,128)S(1)} %get-tuple-element.49), channel_id=1, source_target_pairs={{1,0},{2,1},{3,2},{0,3},{5,4},{6,5},{7,6},{4,7},{9,8},{10,9},{11,1... | collective-permute-start | bytes 786440 | tf_op jit(solution)/shard_map/ppermute | solution.py:549
  7.9 2.3 %collective-permute-start = (f32[32,8,128]{2,1,0:T(8,128)S(1)}, f32[32,8,128]{2,1,0:T(8,128)S(1)}, u32[]{:S(2)}, u32[]{:S(2)}) collective-permute-start(f32[32,8,128]{2,1,0:T(8,128)S(1)} %get-tuple-element.46), channel_id=1, source_target_pairs={{0,4},{1,0},{2,6},{3,2},{4,8},{5,1},{6,10},{7,3},{8,12},{9,5},{10,... | collective-permute-start | bytes 393224 | tf_op jit(solution)/shard_map/ppermute | solution.py:542
  10.2 0.0 collective-permute-start.1
  10.2 0.0 collective-permute-start.5
  10.2 5.0 %local.2 = (f32[64,8,128]{2,1,0:T(8,128)S(1)}, bf16[64,128,256]{2,1,0:T(8,128)(2,1)S(1)}, f32[16,4096]{1,0:T(8,128)S(1)}) custom-call(s32[4,64]{1,0:T(4,128)} %bitcast.39, f32[8192,128]{1,0:T(8,128)} %bitcast.36, f32[64,16,128]{2,1,0:T(8,128)S(1)} %get-tuple-element.43.rest_0_.z_ref), custom_call_target="tpu_custom_call" | custom-call | flops 2000000000 | bytes 8388608 | tf_op jit(solution)/shard_map/local/pallas_call | solution.py:605
  15.2 3.0 %collective-permute-done.i0 = f32[32,8,128]{2,1,0:T(8,128)S(1)} collective-permute-done((f32[32,8,128]{2,1,0:T(8,128)S(1)}, f32[32,8,128]{2,1,0:T(8,128)S(1)}, u32[]{:S(2)}, u32[]{:S(2)}) %collective-permute-start) | collective-permute-done | bytes 131104 | tf_op jit(solution)/shard_map/ppermute | solution.py:542
  18.2 0.0 collective-permute-done.1.i1
  18.2 0.0 collective-permute-done.2.i2.e2
  18.2 0.0 collective-permute-done.3.i3.e3
  18.2 2.5 %collective-permute-start.4 = (f32[32,8,128]{2,1,0:T(8,128)S(1)}, f32[32,8,128]{2,1,0:T(8,128)S(1)}, u32[]{:S(2)}, u32[]{:S(2)}) collective-permute-start(f32[32,8,128]{2,1,0:T(8,128)S(1)} %get-tuple-element.65), channel_id=1, source_target_pairs={{0,4},{1,0},{2,6},{3,2},{4,8},{5,1},{6,10},{7,3},{8,12},{9,5},{10,... | collective-permute-start | bytes 393224 | tf_op jit(solution)/shard_map/ppermute | solution.py:542
  20.7 4.1 %second.1 = (f32[32,8,128]{2,1,0:T(8,128)S(1)}, f32[32,8,128]{2,1,0:T(8,128)S(1)}, f32[32,8,128]{2,1,0:T(8,128)S(1)}, f32[32,8,128]{2,1,0:T(8,128)S(1)}, f32[64,...) custom-call(f32[64,8,128]{2,1,0:T(8,128)S(1)} %get-tuple-element.51.acc_in, f32[32,8,128]{2,1,0:T(8,128)S(1)} %collective-permute-done.i0, ...), custom_call_target="tpu_custom_call" | custom-call | tf_op jit(solution)/shard_map/second/pallas_call | solution.py:615
  24.9 0.0 collective-permute-done.5.d1
  24.9 0.0 collective-permute-done.4.d0
  24.9 1.1 %collective-permute-start.6 = (f32[32,8,128]{2,1,0:T(8,128)S(1)}, f32[32,8,128]{2,1,0:T(8,128)S(1)}, u32[]{:S(2)}, u32[]{:S(2)}) collective-permute-start(f32[32,8,128]{2,1,0:T(8,128)S(1)} %get-tuple-element.67), channel_id=1, source_target_pairs={{0,4},{1,0},{2,6},{3,2},{4,8},{5,1},{6,10},{7,3},{8,12},{9,5},{10,... | collective-permute-start | bytes 393224 | tf_op jit(solution)/shard_map/ppermute | solution.py:542
  26.0 0.0 collective-permute-start.7
  26.0 0.0 collective-permute-start.8
  26.0 1.7 %collective-permute-start.9 = (f32[32,8,128]{2,1,0:T(8,128)S(1)}, f32[32,8,128]{2,1,0:T(8,128)S(1)}, u32[]{:S(2)}, u32[]{:S(2)}) collective-permute-start(f32[32,8,128]{2,1,0:T(8,128)S(1)} %get-tuple-element.70), channel_id=1, source_target_pairs={{1,0},{2,1},{3,2},{0,3},{5,4},{6,5},{7,6},{4,7},{9,8},{10,9},{11,1... | collective-permute-start | bytes 393224 | tf_op jit(solution)/shard_map/ppermute | solution.py:549
  27.8 4.0 %local.3 = (f32[64,16,128]{2,1,0:T(8,128)S(1)}, f32[8,4096]{1,0:T(8,128)S(1)}, f32[8,4096]{1,0:T(8,128)S(1)}) custom-call(s32[4,64]{1,0:T(4,128)} %bitcast.40, bf16[64,128,256]{2,1,0:T(8,128)(2,1)S(1)} %get-tuple-element.44.tiles_in, f32[64,16,128]{2,1,0:T(8,128)S(1)} %get-tuple-element.58.rest_0_, f32[64,8,128]{2,1,0:T(8,128)S(1)} %get-tuple-element.59.rest_1_), custom_call_target="tpu_custom_call" | custom-call | flops 2000000000 | bytes 8388608 | tf_op jit(solution)/shard_map/local/pallas_call | solution.py:605
  31.8 0.0 collective-permute-done.6.i0
  31.8 0.0 collective-permute-done.7.i1
  31.8 0.0 collective-permute-done.8.i2
  31.8 0.0 collective-permute-done.9.i3
  31.8 3.4 %third.1 = (f32[16,4096]{1,0:T(8,128)S(1)}, f32[32,4,128]{2,1,0:T(4,128)S(1)}) custom-call(f32[64,16,128]{2,1,0:T(8,128)S(1)} %get-tuple-element.60.acc_in, f32[32,8,128]{2,1,0:T(8,128)S(1)} %collective-permute-done.6.i0, f32[32,8,128]{2,1,0:T(8,128)S(1)} %collective-permute-done.7.i1, f32[32,8,128]{2,1,0:T(8,128)S(1)} %collective-permute-done.8.i2, ...), custom_call_target="tpu_custom_call" | custom-call | tf_op jit(solution)/shard_map/third/pallas_call | solution.py:625
  35.2 12.7 %all_to_all.5.all_ref = f32[32,4,128]{2,1,0:T(4,128)S(1)} all-to-all(f32[32,4,128]{2,1,0:T(4,128)S(1)} %get-tuple-element.80), channel_id=1, replica_groups=mesh['slab'=8,'sector'=4] {'slab','sector'}, dimensions={0} | all-to-all | bytes 131072 | tf_op jit(solution)/shard_map/all_to_all | solution.py:632
  48.0 1.6 %last.1 = (f32[8,4096]{1,0:T(8,128)}, f32[8,4096]{1,0:T(8,128)}) custom-call(f32[32,4,128]{2,1,0:T(4,128)S(1)} %all_to_all.5.all_ref, f32[16,4096]{1,0:T(8,128)S(1)} %get-tuple-element.75.zn_ref, f32[8,4096]{1,0:T(8,128)S(1)} %get-tuple-element.77.wn_ref, f32[8,4096]{1,0:T(8,128)S(1)} %get-tuple-element.76.qn_ref, f32[8,4096]{1,0:T(8,128)S(1)} %get-tuple-element.78.r0_ref, ...), custom_call_target="tpu_custom_call" | custom-call | tf_op jit(solution)/shard_map/last/pallas_call | solution.py:633
Async XLA Ops:
  5.4 12.7 %collective-permute-start.2 = (f32[32,16,128]{2,1,0:T(8,128)S(1)}, f32[32,16,128]{2,1,0:T(8,128)S(1)}, u32[]{:S(2)}, u32[]{:S(2)}) collective-permute-start(f32[32,16,128]{2,1,0:T(8,128)S(1)} %get-tuple-element.48), channel_id=1, source_target_pairs={{0,1},{1,2},{2,3},{3,0},{4,5},{5,6},{6,7},{7,4},{8,9},{9,10},{10,1... | collective-permute-start | bytes 786440 | tf_op jit(solution)/shard_map/ppermute | solution.py:549
  5.9 12.2 %collective-permute-start.3 = (f32[32,16,128]{2,1,0:T(8,128)S(1)}, f32[32,16,128]{2,1,0:T(8,128)S(1)}, u32[]{:S(2)}, u32[]{:S(2)}) collective-permute-start(f32[32,16,128]{2,1,0:T(8,128)S(1)} %get-tuple-element.49), channel_id=1, source_target_pairs={{1,0},{2,1},{3,2},{0,3},{5,4},{6,5},{7,6},{4,7},{9,8},{10,9},{11,1... | collective-permute-start | bytes 786440 | tf_op jit(solution)/shard_map/ppermute | solution.py:549
  7.9 10.2 %collective-permute-start = (f32[32,8,128]{2,1,0:T(8,128)S(1)}, f32[32,8,128]{2,1,0:T(8,128)S(1)}, u32[]{:S(2)}, u32[]{:S(2)}) collective-permute-start(f32[32,8,128]{2,1,0:T(8,128)S(1)} %get-tuple-element.46), channel_id=1, source_target_pairs={{0,4},{1,0},{2,6},{3,2},{4,8},{5,1},{6,10},{7,3},{8,12},{9,5},{10,... | collective-permute-start | bytes 393224 | tf_op jit(solution)/shard_map/ppermute | solution.py:542
  10.2 8.0 %collective-permute-start.1 = (f32[32,8,128]{2,1,0:T(8,128)S(1)}, f32[32,8,128]{2,1,0:T(8,128)S(1)}, u32[]{:S(2)}, u32[]{:S(2)}) collective-permute-start(f32[32,8,128]{2,1,0:T(8,128)S(1)} %get-tuple-element.47), channel_id=1, source_target_pairs={{0,1},{1,5},{2,3},{3,7},{4,0},{5,9},{6,2},{7,11},{8,4},{9,13},{10,... | collective-permute-start | bytes 393224 | tf_op jit(solution)/shard_map/ppermute | solution.py:542
  10.2 14.7 %collective-permute-start.5 = (f32[32,8,128]{2,1,0:T(8,128)S(1)}, f32[32,8,128]{2,1,0:T(8,128)S(1)}, u32[]{:S(2)}, u32[]{:S(2)}) collective-permute-start(f32[32,8,128]{2,1,0:T(8,128)S(1)} %get-tuple-element.66), channel_id=1, source_target_pairs={{0,1},{1,5},{2,3},{3,7},{4,0},{5,9},{6,2},{7,11},{8,4},{9,13},{10,... | collective-permute-start | bytes 393224 | tf_op jit(solution)/shard_map/ppermute | solution.py:542
  18.2 6.7 %collective-permute-start.4 = (f32[32,8,128]{2,1,0:T(8,128)S(1)}, f32[32,8,128]{2,1,0:T(8,128)S(1)}, u32[]{:S(2)}, u32[]{:S(2)}) collective-permute-start(f32[32,8,128]{2,1,0:T(8,128)S(1)} %get-tuple-element.65), channel_id=1, source_target_pairs={{0,4},{1,0},{2,6},{3,2},{4,8},{5,1},{6,10},{7,3},{8,12},{9,5},{10,... | collective-permute-start | bytes 393224 | tf_op jit(solution)/shard_map/ppermute | solution.py:542
  24.9 6.9 %collective-permute-start.6 = (f32[32,8,128]{2,1,0:T(8,128)S(1)}, f32[32,8,128]{2,1,0:T(8,128)S(1)}, u32[]{:S(2)}, u32[]{:S(2)}) collective-permute-start(f32[32,8,128]{2,1,0:T(8,128)S(1)} %get-tuple-element.67), channel_id=1, source_target_pairs={{0,4},{1,0},{2,6},{3,2},{4,8},{5,1},{6,10},{7,3},{8,12},{9,5},{10,... | collective-permute-start | bytes 393224 | tf_op jit(solution)/shard_map/ppermute | solution.py:542
  26.0 5.8 %collective-permute-start.7 = (f32[32,8,128]{2,1,0:T(8,128)S(1)}, f32[32,8,128]{2,1,0:T(8,128)S(1)}, u32[]{:S(2)}, u32[]{:S(2)}) collective-permute-start(f32[32,8,128]{2,1,0:T(8,128)S(1)} %get-tuple-element.68), channel_id=1, source_target_pairs={{0,1},{1,5},{2,3},{3,7},{4,0},{5,9},{6,2},{7,11},{8,4},{9,13},{10,... | collective-permute-start | bytes 393224 | tf_op jit(solution)/shard_map/ppermute | solution.py:542
  26.0 5.8 %collective-permute-start.8 = (f32[32,8,128]{2,1,0:T(8,128)S(1)}, f32[32,8,128]{2,1,0:T(8,128)S(1)}, u32[]{:S(2)}, u32[]{:S(2)}) collective-permute-start(f32[32,8,128]{2,1,0:T(8,128)S(1)} %get-tuple-element.69), channel_id=1, source_target_pairs={{0,1},{1,2},{2,3},{3,0},{4,5},{5,6},{6,7},{7,4},{8,9},{9,10},{10,1... | collective-permute-start | bytes 393224 | tf_op jit(solution)/shard_map/ppermute | solution.py:549
  26.0 5.8 %collective-permute-start.9 = (f32[32,8,128]{2,1,0:T(8,128)S(1)}, f32[32,8,128]{2,1,0:T(8,128)S(1)}, u32[]{:S(2)}, u32[]{:S(2)}) collective-permute-start(f32[32,8,128]{2,1,0:T(8,128)S(1)} %get-tuple-element.70), channel_id=1, source_target_pairs={{1,0},{2,1},{3,2},{0,3},{5,4},{6,5},{7,6},{4,7},{9,8},{10,9},{11,1... | collective-permute-start | bytes 393224 | tf_op jit(solution)/shard_map/ppermute | solution.py:549

commit v6 on v5

--- a/solution.py
+++ b/solution.py
@@ -236,7 +236,7 @@
 
 
     def ready(way):
-        for part in ((0, 1), (), (3,), (2,))[way]:
+        for part in ((0, 1), (), (2, 3), ())[way]:
             copies.wait(len(small) + 1 + part)
 
     write_messages(lambda b: z_ref[b], y_ref, ready, made(coup_ref, wcoup_ref),
@@ -300,9 +300,9 @@
     low = lane_of((nf, LANES)) < 64
 
     def finish(i, carry):
-        out = dot(u_ref[pl.ds(i * 32, 32)].reshape(32 * 2 * nf, LANES), matrix)
-        for j in range(32):
-            b = i * 32 + j
+        out = dot(u_ref[pl.ds(i * 64, 64)].reshape(64 * 2 * nf, LANES), matrix)
+        for j in range(64):
+            b = i * 64 + j
             t = None
             for k in range(0, kt, 2):
                 at = slice(k // 2 * LANES, (k // 2 + 1) * LANES)
@@ -312,7 +312,7 @@
             acc_ref[b] = z_ref[b, 0:nf] + halves(out[j * 2 * nf : (j + 1) * 2 * nf], nf) + t + turn(t)
         return carry
 
-    lax.fori_loop(0, blocks // 32, finish, 0)
+    lax.fori_loop(0, blocks // 64, finish, 0)
     for vector, natural in zip(vectors, naturals):
         to_natural(vector, natural, blocks)
 
@@ -322,11 +322,13 @@
 
 
 def sends(way):
-    return 1 - odd_sector() if way == 0 else odd_sector() if way == 1 else 5 - way
+    odd = odd_sector()
+    return (1 - odd, odd, 3 - odd, 2 + odd)[way]
 
 
 def receives(way):
-    return odd_sector() if way == 0 else 1 - odd_sector() if way == 1 else way
+    odd = odd_sector()
+    return (odd, 1 - odd, 3 - odd, 2 + odd)[way]
 
 
 def present(way, d):
@@ -544,9 +546,8 @@
 
 def along_sectors(one, two):
     count = lax.axis_size("sector")
-    up = [(i, (i + 1) % count) for i in range(count)]
-    down = [((i + 1) % count, i) for i in range(count)]
-    return lax.ppermute(one, "sector", up), lax.ppermute(two, "sector", down)
+    swaps = [[(e, (e + 1 if (e + way) % 2 == 0 else e - 1) % count) for e in range(count)] for way in range(2)]
+    return lax.ppermute(one, "sector", swaps[0]), lax.ppermute(two, "sector", swaps[1])
 
 
 def exchange(msgs):

time: 49.9 us -> 49.3 us (0.988)
  starting transfers between devices: 10.2 us -> 8.92 us
  waiting for transfers between devices: 3.02 us -> 3.83 us
  Pallas kernels: 22.9 us -> 22.4 us
  blocking collectives: 12.7 us -> 13.2 us
    ppermute x6, starting transfers between devices: 5.95 us -> 5.14 us  [along_slabs(): lax.ppermute(block, AXES, steps(way))]
    ppermute x6, waiting for transfers between devices: 3.01 us -> 3.64 us  [along_slabs(): lax.ppermute(block, AXES, steps(way))]
  transfers between devices with their start and end apart: 10 -> 10, of which waited for: 1 -> 3; matrix products, arithmetic and copies ran while one was open for 0% -> 0% of each run, Pallas kernels for 26% -> 26%
where the time goes in v6:
time: 49.3 us; the launch traced here: 49.1 us
  Pallas kernels  22.4 us (45%)
  blocking collectives  13.2 us (27%)
  starting transfers between devices  8.92 us (18%)
  waiting for transfers between devices  3.83 us (8%)
  between operations  0.71 us (1%)
    all_to_all x1, blocking collectives, on_device(): everyone = lax.all_to_all(pay, AXES, 0, 0)  13.2 us
    pallas_call x2, Pallas kernels, local(): call(functools.partial(local_kernel, n, blocks, kt, fresh, len(vectors)),...  8.7 us
    ppermute x6, starting transfers between devices, along_slabs(): lax.ppermute(block, AXES, steps(way))  5.14 us
    pallas_call x1, Pallas kernels, on_device(): call(functools.partial(first_kernel, both, blocks, cap), [ANY] * 9, [msg]...  4.57 us
    pallas_call x1, Pallas kernels, on_device(): call(functools.partial(second_kernel, nf, blocks, cap), [VMEM] * 8 + [ANY...  4.14 us
    ppermute x6, waiting for transfers between devices, along_slabs(): lax.ppermute(block, AXES, steps(way))  3.64 us
    pallas_call x1, Pallas kernels, on_device(): call(functools.partial(third_kernel, nf, blocks, cap), [VMEM] * 10 + [SME...  3.35 us
    ppermute x2, starting transfers between devices, along_sectors(): lax.ppermute(two, 'sector', swaps[1])  3.27 us
  transfers between devices with their start and end apart: 10, of which 3 were waited for; matrix products, arithmetic and copies ran while one was open for 0% of the time, Pallas kernels for 26%

profile of v6, /device:TPU:0, one launch (start us, length us, event | category | flops | bytes accessed | tf_op | source)
XLA Modules:
  0.0 49.1 jit_solution(6288839220957652399)
XLA Ops:
  0.6 4.6 %first.1 = (f32[32,8,128]{2,1,0:T(8,128)S(1)}, f32[32,8,128]{2,1,0:T(8,128)S(1)}, f32[32,16,128]{2,1,0:T(8,128)S(1)}, f32[32,16,128]{2,1,0:T(8,128)S(1)}, f32[32...) custom-call(f32[8,4096]{1,0:T(8,128)} %bitcast.27, ...), custom_call_target="tpu_custom_call" | custom-call | tf_op jit(solution)/shard_map/first/pallas_call | solution.py:583
  5.2 0.5 %collective-permute-start.2 = (f32[32,16,128]{2,1,0:T(8,128)S(1)}, f32[32,16,128]{2,1,0:T(8,128)S(1)}, u32[]{:S(2)}, u32[]{:S(2)}) collective-permute-start(f32[32,16,128]{2,1,0:T(8,128)S(1)} %get-tuple-element.48), channel_id=1, source_target_pairs={{0,1},{1,0},{2,3},{3,2},{4,5},{5,4},{6,7},{7,6},{8,9},{9,8},{10,11... | collective-permute-start | bytes 786440 | tf_op jit(solution)/shard_map/ppermute | solution.py:550
  5.7 2.6 %collective-permute-start.3 = (f32[32,16,128]{2,1,0:T(8,128)S(1)}, f32[32,16,128]{2,1,0:T(8,128)S(1)}, u32[]{:S(2)}, u32[]{:S(2)}) collective-permute-start(f32[32,16,128]{2,1,0:T(8,128)S(1)} %get-tuple-element.49), channel_id=1, source_target_pairs={{0,3},{1,2},{2,1},{3,0},{4,7},{5,6},{6,5},{7,4},{8,11},{9,10},{10,... | collective-permute-start | bytes 786440 | tf_op jit(solution)/shard_map/ppermute | solution.py:550
  8.3 1.5 %collective-permute-start = (f32[32,8,128]{2,1,0:T(8,128)S(1)}, f32[32,8,128]{2,1,0:T(8,128)S(1)}, u32[]{:S(2)}, u32[]{:S(2)}) collective-permute-start(f32[32,8,128]{2,1,0:T(8,128)S(1)} %get-tuple-element.46), channel_id=1, source_target_pairs={{0,4},{1,0},{2,6},{3,2},{4,8},{5,1},{6,10},{7,3},{8,12},{9,5},{10,... | collective-permute-start | bytes 393224 | tf_op jit(solution)/shard_map/ppermute | solution.py:544
  9.9 0.0 collective-permute-start.1
  9.9 0.0 collective-permute-start.5
  9.9 4.8 %local.2 = (f32[64,8,128]{2,1,0:T(8,128)S(1)}, bf16[64,128,256]{2,1,0:T(8,128)(2,1)S(1)}, f32[16,4096]{1,0:T(8,128)S(1)}) custom-call(s32[4,64]{1,0:T(4,128)} %bitcast.39, f32[8192,128]{1,0:T(8,128)} %bitcast.36, f32[64,16,128]{2,1,0:T(8,128)S(1)} %get-tuple-element.43.rest_0_.z_ref), custom_call_target="tpu_custom_call" | custom-call | flops 2000000000 | bytes 8388608 | tf_op jit(solution)/shard_map/local/pallas_call | solution.py:606
  14.7 3.2 %collective-permute-done.i0 = f32[32,8,128]{2,1,0:T(8,128)S(1)} collective-permute-done((f32[32,8,128]{2,1,0:T(8,128)S(1)}, f32[32,8,128]{2,1,0:T(8,128)S(1)}, u32[]{:S(2)}, u32[]{:S(2)}) %collective-permute-start) | collective-permute-done | bytes 131104 | tf_op jit(solution)/shard_map/ppermute | solution.py:544
  17.9 0.0 collective-permute-done.1.i1
  17.9 0.0 collective-permute-done.2.i2.e2
  17.9 0.0 collective-permute-done.3.i3.e3
  17.9 2.5 %collective-permute-start.4 = (f32[32,8,128]{2,1,0:T(8,128)S(1)}, f32[32,8,128]{2,1,0:T(8,128)S(1)}, u32[]{:S(2)}, u32[]{:S(2)}) collective-permute-start(f32[32,8,128]{2,1,0:T(8,128)S(1)} %get-tuple-element.65), channel_id=1, source_target_pairs={{0,4},{1,0},{2,6},{3,2},{4,8},{5,1},{6,10},{7,3},{8,12},{9,5},{10,... | collective-permute-start | bytes 393224 | tf_op jit(solution)/shard_map/ppermute | solution.py:544
  20.5 4.1 %second.1 = (f32[32,8,128]{2,1,0:T(8,128)S(1)}, f32[32,8,128]{2,1,0:T(8,128)S(1)}, f32[32,8,128]{2,1,0:T(8,128)S(1)}, f32[32,8,128]{2,1,0:T(8,128)S(1)}, f32[64,...) custom-call(f32[64,8,128]{2,1,0:T(8,128)S(1)} %get-tuple-element.51.acc_in, f32[32,8,128]{2,1,0:T(8,128)S(1)} %collective-permute-done.i0, ...), custom_call_target="tpu_custom_call" | custom-call | tf_op jit(solution)/shard_map/second/pallas_call | solution.py:616
  24.6 0.0 collective-permute-done.5.d1
  24.6 0.0 collective-permute-done.4.d0
  24.6 1.1 %collective-permute-start.6 = (f32[32,8,128]{2,1,0:T(8,128)S(1)}, f32[32,8,128]{2,1,0:T(8,128)S(1)}, u32[]{:S(2)}, u32[]{:S(2)}) collective-permute-start(f32[32,8,128]{2,1,0:T(8,128)S(1)} %get-tuple-element.67), channel_id=1, source_target_pairs={{0,4},{1,0},{2,6},{3,2},{4,8},{5,1},{6,10},{7,3},{8,12},{9,5},{10,... | collective-permute-start | bytes 393224 | tf_op jit(solution)/shard_map/ppermute | solution.py:544
  25.7 0.0 collective-permute-start.7
  25.7 0.0 collective-permute-start.8
  25.7 0.6 %collective-permute-start.9 = (f32[32,8,128]{2,1,0:T(8,128)S(1)}, f32[32,8,128]{2,1,0:T(8,128)S(1)}, u32[]{:S(2)}, u32[]{:S(2)}) collective-permute-start(f32[32,8,128]{2,1,0:T(8,128)S(1)} %get-tuple-element.70), channel_id=1, source_target_pairs={{0,3},{1,2},{2,1},{3,0},{4,7},{5,6},{6,5},{7,4},{8,11},{9,10},{10,... | collective-permute-start | bytes 393224 | tf_op jit(solution)/shard_map/ppermute | solution.py:550
  26.4 3.9 %local.3 = (f32[64,16,128]{2,1,0:T(8,128)S(1)}, f32[8,4096]{1,0:T(8,128)S(1)}, f32[8,4096]{1,0:T(8,128)S(1)}) custom-call(s32[4,64]{1,0:T(4,128)} %bitcast.40, bf16[64,128,256]{2,1,0:T(8,128)(2,1)S(1)} %get-tuple-element.44.tiles_in, f32[64,16,128]{2,1,0:T(8,128)S(1)} %get-tuple-element.58.rest_0_, f32[64,8,128]{2,1,0:T(8,128)S(1)} %get-tuple-element.59.rest_1_), custom_call_target="tpu_custom_call" | custom-call | flops 2000000000 | bytes 8388608 | tf_op jit(solution)/shard_map/local/pallas_call | solution.py:606
  30.2 0.0 collective-permute-done.6.i0
  30.2 0.4 collective-permute-done.7.i1
  30.7 0.0 collective-permute-done.8.i2
  30.7 0.2 collective-permute-done.9.i3
  30.9 3.4 %third.1 = (f32[16,4096]{1,0:T(8,128)S(1)}, f32[32,4,128]{2,1,0:T(4,128)S(1)}) custom-call(f32[64,16,128]{2,1,0:T(8,128)S(1)} %get-tuple-element.60.acc_in, f32[32,8,128]{2,1,0:T(8,128)S(1)} %collective-permute-done.6.i0, f32[32,8,128]{2,1,0:T(8,128)S(1)} %collective-permute-done.7.i1, f32[32,8,128]{2,1,0:T(8,128)S(1)} %collective-permute-done.8.i2, ...), custom_call_target="tpu_custom_call" | custom-call | tf_op jit(solution)/shard_map/third/pallas_call | solution.py:626
  34.2 13.2 %all_to_all.5.all_ref = f32[32,4,128]{2,1,0:T(4,128)S(1)} all-to-all(f32[32,4,128]{2,1,0:T(4,128)S(1)} %get-tuple-element.80), channel_id=1, replica_groups=mesh['slab'=8,'sector'=4] {'slab','sector'}, dimensions={0} | all-to-all | bytes 131072 | tf_op jit(solution)/shard_map/all_to_all | solution.py:633
  47.4 1.6 %last.1 = (f32[8,4096]{1,0:T(8,128)}, f32[8,4096]{1,0:T(8,128)}) custom-call(f32[32,4,128]{2,1,0:T(4,128)S(1)} %all_to_all.5.all_ref, f32[16,4096]{1,0:T(8,128)S(1)} %get-tuple-element.75.zn_ref, f32[8,4096]{1,0:T(8,128)S(1)} %get-tuple-element.77.wn_ref, f32[8,4096]{1,0:T(8,128)S(1)} %get-tuple-element.76.qn_ref, f32[8,4096]{1,0:T(8,128)S(1)} %get-tuple-element.78.r0_ref, ...), custom_call_target="tpu_custom_call" | custom-call | tf_op jit(solution)/shard_map/last/pallas_call | solution.py:634
Async XLA Ops:
  5.2 12.7 %collective-permute-start.2 = (f32[32,16,128]{2,1,0:T(8,128)S(1)}, f32[32,16,128]{2,1,0:T(8,128)S(1)}, u32[]{:S(2)}, u32[]{:S(2)}) collective-permute-start(f32[32,16,128]{2,1,0:T(8,128)S(1)} %get-tuple-element.48), channel_id=1, source_target_pairs={{0,1},{1,0},{2,3},{3,2},{4,5},{5,4},{6,7},{7,6},{8,9},{9,8},{10,11... | collective-permute-start | bytes 786440 | tf_op jit(solution)/shard_map/ppermute | solution.py:550
  5.7 12.2 %collective-permute-start.3 = (f32[32,16,128]{2,1,0:T(8,128)S(1)}, f32[32,16,128]{2,1,0:T(8,128)S(1)}, u32[]{:S(2)}, u32[]{:S(2)}) collective-permute-start(f32[32,16,128]{2,1,0:T(8,128)S(1)} %get-tuple-element.49), channel_id=1, source_target_pairs={{0,3},{1,2},{2,1},{3,0},{4,7},{5,6},{6,5},{7,4},{8,11},{9,10},{10,... | collective-permute-start | bytes 786440 | tf_op jit(solution)/shard_map/ppermute | solution.py:550
  8.3 9.6 %collective-permute-start = (f32[32,8,128]{2,1,0:T(8,128)S(1)}, f32[32,8,128]{2,1,0:T(8,128)S(1)}, u32[]{:S(2)}, u32[]{:S(2)}) collective-permute-start(f32[32,8,128]{2,1,0:T(8,128)S(1)} %get-tuple-element.46), channel_id=1, source_target_pairs={{0,4},{1,0},{2,6},{3,2},{4,8},{5,1},{6,10},{7,3},{8,12},{9,5},{10,... | collective-permute-start | bytes 393224 | tf_op jit(solution)/shard_map/ppermute | solution.py:544
  9.9 8.0 %collective-permute-start.1 = (f32[32,8,128]{2,1,0:T(8,128)S(1)}, f32[32,8,128]{2,1,0:T(8,128)S(1)}, u32[]{:S(2)}, u32[]{:S(2)}) collective-permute-start(f32[32,8,128]{2,1,0:T(8,128)S(1)} %get-tuple-element.47), channel_id=1, source_target_pairs={{0,1},{1,5},{2,3},{3,7},{4,0},{5,9},{6,2},{7,11},{8,4},{9,13},{10,... | collective-permute-start | bytes 393224 | tf_op jit(solution)/shard_map/ppermute | solution.py:544
  9.9 14.7 %collective-permute-start.5 = (f32[32,8,128]{2,1,0:T(8,128)S(1)}, f32[32,8,128]{2,1,0:T(8,128)S(1)}, u32[]{:S(2)}, u32[]{:S(2)}) collective-permute-start(f32[32,8,128]{2,1,0:T(8,128)S(1)} %get-tuple-element.66), channel_id=1, source_target_pairs={{0,1},{1,5},{2,3},{3,7},{4,0},{5,9},{6,2},{7,11},{8,4},{9,13},{10,... | collective-permute-start | bytes 393224 | tf_op jit(solution)/shard_map/ppermute | solution.py:544
  17.9 6.7 %collective-permute-start.4 = (f32[32,8,128]{2,1,0:T(8,128)S(1)}, f32[32,8,128]{2,1,0:T(8,128)S(1)}, u32[]{:S(2)}, u32[]{:S(2)}) collective-permute-start(f32[32,8,128]{2,1,0:T(8,128)S(1)} %get-tuple-element.65), channel_id=1, source_target_pairs={{0,4},{1,0},{2,6},{3,2},{4,8},{5,1},{6,10},{7,3},{8,12},{9,5},{10,... | collective-permute-start | bytes 393224 | tf_op jit(solution)/shard_map/ppermute | solution.py:544
  24.6 5.6 %collective-permute-start.6 = (f32[32,8,128]{2,1,0:T(8,128)S(1)}, f32[32,8,128]{2,1,0:T(8,128)S(1)}, u32[]{:S(2)}, u32[]{:S(2)}) collective-permute-start(f32[32,8,128]{2,1,0:T(8,128)S(1)} %get-tuple-element.67), channel_id=1, source_target_pairs={{0,4},{1,0},{2,6},{3,2},{4,8},{5,1},{6,10},{7,3},{8,12},{9,5},{10,... | collective-permute-start | bytes 393224 | tf_op jit(solution)/shard_map/ppermute | solution.py:544
  25.7 5.0 %collective-permute-start.7 = (f32[32,8,128]{2,1,0:T(8,128)S(1)}, f32[32,8,128]{2,1,0:T(8,128)S(1)}, u32[]{:S(2)}, u32[]{:S(2)}) collective-permute-start(f32[32,8,128]{2,1,0:T(8,128)S(1)} %get-tuple-element.68), channel_id=1, source_target_pairs={{0,1},{1,5},{2,3},{3,7},{4,0},{5,9},{6,2},{7,11},{8,4},{9,13},{10,... | collective-permute-start | bytes 393224 | tf_op jit(solution)/shard_map/ppermute | solution.py:544
  25.7 5.0 %collective-permute-start.8 = (f32[32,8,128]{2,1,0:T(8,128)S(1)}, f32[32,8,128]{2,1,0:T(8,128)S(1)}, u32[]{:S(2)}, u32[]{:S(2)}) collective-permute-start(f32[32,8,128]{2,1,0:T(8,128)S(1)} %get-tuple-element.69), channel_id=1, source_target_pairs={{0,1},{1,0},{2,3},{3,2},{4,5},{5,4},{6,7},{7,6},{8,9},{9,8},{10,11... | collective-permute-start | bytes 393224 | tf_op jit(solution)/shard_map/ppermute | solution.py:550
  25.7 5.2 %collective-permute-start.9 = (f32[32,8,128]{2,1,0:T(8,128)S(1)}, f32[32,8,128]{2,1,0:T(8,128)S(1)}, u32[]{:S(2)}, u32[]{:S(2)}) collective-permute-start(f32[32,8,128]{2,1,0:T(8,128)S(1)} %get-tuple-element.70), channel_id=1, source_target_pairs={{0,3},{1,2},{2,1},{3,0},{4,7},{5,6},{6,5},{7,4},{8,11},{9,10},{10,... | collective-permute-start | bytes 393224 | tf_op jit(solution)/shard_map/ppermute | solution.py:550
